TPU v7x, 32 devices: a whole 2x2x4 slice. The times are simulated.
32 devices in a mesh: tok: 16 (over z, x, core), ffn: 2 (over y).
Axes of the slice: x: 2, y: 2, z: 4, core: 2. Of those that a mesh axis runs over, the one named last changes fastest.
Arguments:
- tokens: bfloat16 [16384, 768], P(('tok', 'ffn')), may hold values from -6 to 6
- rel_ids: int32 [32, 512, 512], P(('tok', 'ffn')), may hold values from 1 to 511, as said below
- mask_pos: int32 [32, 80], P(('tok', 'ffn')), may hold values from -1 to 511, as said below
- grad_vals: bfloat16 [32, 80, 768], P(('tok', 'ffn')), may hold values from -6 to 6
- w_query: bfloat16 [768, 768], replicated, may hold values from -0.21875 to 0.21875
- w_key: bfloat16 [768, 768], replicated, may hold values from -0.21875 to 0.21875
- w_value: bfloat16 [768, 768], replicated, may hold values from -0.21875 to 0.21875
- w_out: bfloat16 [768, 768], replicated, may hold values from -3 to 3
- b_query: float32 [768], replicated, may hold values from -3 to 3
- b_key: float32 [768], replicated, may hold values from -3 to 3
- b_value: float32 [768], replicated, may hold values from -3 to 3
- b_out: float32 [768], replicated, may hold values from -3 to 3
- rel_table: bfloat16 [512, 768], replicated, may hold values from -6 to 6
- ln1_gain: float32 [768], replicated, may hold values from 0.5 to 1.5
- ln1_bias: float32 [768], replicated, may hold values from -2 to 2
- w_in: bfloat16 [768, 3072], P(None, 'ffn'), may hold values from -0.21875 to 0.21875
- b_in: float32 [3072], P('ffn'), may hold values from -3 to 3
- w_down: bfloat16 [3072, 768], P('ffn'), may hold values from -0.109375 to 0.109375
- b_down: float32 [768], replicated, may hold values from -2 to 2
- ln2_gain: float32 [768], replicated, may hold values from 0.5 to 1.5
- ln2_bias: float32 [768], replicated, may hold values from -2 to 2
Outputs:
- output: bfloat16 [16384, 768], P(('tok', 'ffn'))
- grad_tokens: float32 [16384, 768], P(('tok', 'ffn'))
- grad_w_query: float32 [768, 768], P(('tok', 'ffn'))
- grad_w_key: float32 [768, 768], P(('tok', 'ffn'))
- grad_w_value: float32 [768, 768], P(('tok', 'ffn'))
- grad_w_out: float32 [768, 768], P(('tok', 'ffn'))
- grad_b_query: float32 [768], P(('tok', 'ffn'))
- grad_b_key: float32 [768], P(('tok', 'ffn'))
- grad_b_value: float32 [768], P(('tok', 'ffn'))
- grad_b_out: float32 [768], P(('tok', 'ffn'))
- grad_rel_table: float32 [512, 768], P(('tok', 'ffn'))
- grad_ln1_gain: float32 [768], P(('tok', 'ffn'))
- grad_ln1_bias: float32 [768], P(('tok', 'ffn'))
- grad_w_in: float32 [768, 3072], P('tok', 'ffn')
- grad_b_in: float32 [2, 1536], P('ffn', 'tok')
- grad_w_down: float32 [3072, 768], P('ffn', 'tok')
- grad_b_down: float32 [768], P(('tok', 'ffn'))
- grad_ln2_gain: float32 [768], P(('tok', 'ffn'))
- grad_ln2_bias: float32 [768], P(('tok', 'ffn'))
Inputs may be any that keep to these rules, and one draw needn't show every extreme that they name: `mask_pos`: row s names distinct positions of sequence s in its first slots and -1 in the others; each row names 64 to 80 positions, and some row names 80. rel_ids[s, i, j] = 256 + the DeBERTa log bucket (identity up to 128, logarithmic beyond, maximum position 512) of p_i - p_j, where p_i counts word starts before token i of sequence s, tokens of one word sharing it; so rel_ids[s, j, i] = 512 - rel_ids[s, i, j].
All inputs are finite; a program needn't handle non-finite values.
Results may differ from a plain program's by a relative error of at most 0.034.
Values may be sent and summed in bfloat16 or wider, within the bound.
No kernel may reach another device: no remote copies, remote signals or barrier semaphores. Data moves between devices by JAX's collectives and lax.ppermute only.
A program may use at most 256 MiB of HBM per device.

v0:
```python
from functools import partial
import math

import jax
import jax.numpy as jnp
from jax import lax
from jax.sharding import PartitionSpec as P

H = 12
DH = 64


norm_eps = 1e-07


def plain_dot(first_op, second_op):
    return jnp.dot(first_op, second_op, preferred_element_type=jnp.float32)


def rows_inner(first_op, second_op):
    return lax.dot_general(
        first_op, second_op, (((0,), (0,)), ((), ())), preferred_element_type=jnp.float32
    )


def cols_inner(first_op, second_op):
    return lax.dot_general(
        first_op, second_op, (((1,), (1,)), ((), ())), preferred_element_type=jnp.float32
    )


def split_parts(values):
    upper_part = values.astype(jnp.bfloat16)
    lower_part = (values - upper_part.astype(jnp.float32)).astype(jnp.bfloat16)
    return (upper_part, lower_part)


def rows_split(narrow, wide):
    upper_part, lower_part = split_parts(wide)
    return rows_inner(narrow, upper_part) + rows_inner(narrow, lower_part)


def cols_split(wide, narrow):
    upper_part, lower_part = split_parts(wide)
    return cols_inner(upper_part, narrow) + cols_inner(lower_part, narrow)


def norm_forward(values, norm_gain, norm_bias):
    centered = values - jnp.mean(values, axis=1, keepdims=True)
    inv_std = lax.rsqrt(jnp.mean(centered * centered, axis=1, keepdims=True) + norm_eps)
    normed = centered * inv_std
    return (normed * norm_gain + norm_bias, normed, inv_std)


def norm_backward(upstream, normed, inv_std, norm_gain):
    scaled = upstream * norm_gain
    adjusted = (
        scaled
        - jnp.mean(scaled, axis=1, keepdims=True)
        - normed * jnp.mean(scaled * normed, axis=1, keepdims=True)
    )
    return (inv_std * adjusted, jnp.sum(upstream * normed, axis=0), jnp.sum(upstream, axis=0))


def gelu_slope(pre_act):
    cdf_part = 0.5 * (1.0 + lax.erf(pre_act * (1.0 / math.sqrt(2.0))))
    pdf_part = jnp.exp(-0.5 * pre_act * pre_act) * (1.0 / math.sqrt(2.0 * math.pi))
    return cdf_part + pre_act * pdf_part


def block_layout(values, block_rows):
    head_count, query_count = (values.shape[0], values.shape[1])
    block_count = query_count // block_rows
    shaped = values.reshape((head_count, block_count, block_rows) + values.shape[2:])
    return jnp.moveaxis(shaped, 1, 0)


def unblock_layout(values):
    merged = jnp.moveaxis(values, 0, 1)
    return merged.reshape((merged.shape[0], merged.shape[1] * merged.shape[2]) + merged.shape[3:])


def pick_cols(table, seq_ids):
    rel_width = table.shape[2]
    block_rows = min(64, table.shape[1])
    table_blocks = block_layout(table, block_rows)
    id_blocks = seq_ids.reshape(seq_ids.shape[0] // block_rows, block_rows, seq_ids.shape[1])

    def pick_block(inputs):
        table_block, id_block = inputs
        selector = (
            id_block[:, :, None] == lax.broadcasted_iota(jnp.int32, (1, 1, rel_width), 2)
        ).astype(jnp.bfloat16)
        upper_part, lower_part = split_parts(table_block)
        return jnp.einsum(
            "hir,ijr->hij", upper_part, selector, preferred_element_type=jnp.float32
        ) + jnp.einsum("hir,ijr->hij", lower_part, selector, preferred_element_type=jnp.float32)

    return unblock_layout(lax.map(pick_block, (table_blocks, id_blocks)))


def spread_cols(values, seq_ids, rel_width):
    block_rows = min(64, values.shape[1])
    value_blocks = block_layout(values, block_rows)
    id_blocks = seq_ids.reshape(seq_ids.shape[0] // block_rows, block_rows, seq_ids.shape[1])

    def spread_block(inputs):
        value_block, id_block = inputs
        selector = (
            id_block[:, :, None] == lax.broadcasted_iota(jnp.int32, (1, 1, rel_width), 2)
        ).astype(jnp.bfloat16)
        upper_part, lower_part = split_parts(value_block)
        return jnp.einsum(
            "hij,ijr->hir", upper_part, selector, preferred_element_type=jnp.float32
        ) + jnp.einsum("hij,ijr->hir", lower_part, selector, preferred_element_type=jnp.float32)

    return unblock_layout(lax.map(spread_block, (value_blocks, id_blocks)))


def seq_scores(queries, key_rows, seq_ids, pos_query, pos_key):
    score_scale = 1.0 / math.sqrt(3.0 * queries.shape[2])
    direct = jnp.einsum("ihd,jhd->hij", queries, key_rows, preferred_element_type=jnp.float32)
    to_pos = jnp.einsum("ihd,rhd->hir", queries, pos_key, preferred_element_type=jnp.float32)
    from_pos = jnp.einsum("jhd,rhd->hjr", key_rows, pos_query, preferred_element_type=jnp.float32)
    picked = pick_cols(to_pos, seq_ids)
    mirrored = jnp.swapaxes(pick_cols(from_pos, seq_ids), 1, 2)
    return (direct + picked + mirrored) * score_scale


def attend(pos_query, pos_key, inputs):
    queries, key_rows, value_rows, seq_ids = inputs
    scores = seq_scores(queries, key_rows, seq_ids, pos_query, pos_key)
    maxima = jnp.max(scores, axis=2, keepdims=True)
    weights = jnp.exp(scores - maxima)
    totals = jnp.sum(weights, axis=2, keepdims=True)
    attn_probs = (weights / totals).astype(jnp.bfloat16)
    mixed_ctx = jnp.einsum(
        "hij,jhd->ihd", attn_probs, value_rows, preferred_element_type=jnp.float32
    )
    return (mixed_ctx.astype(jnp.bfloat16), (maxima + jnp.log(totals))[:, :, 0])


def attend_back(pos_query, pos_key, carried, inputs):
    acc_key, acc_query = carried
    queries, key_rows, value_rows, seq_ids, logsum, dmixed = inputs
    score_scale = 1.0 / math.sqrt(3.0 * queries.shape[2])
    scores = seq_scores(queries, key_rows, seq_ids, pos_query, pos_key)
    attn_probs = jnp.exp(scores - logsum[:, :, None])
    dprobs = jnp.einsum("ihd,jhd->hij", dmixed, value_rows, preferred_element_type=jnp.float32)
    score_grad = (
        attn_probs * (dprobs - jnp.sum(attn_probs * dprobs, axis=2, keepdims=True)) * score_scale
    )
    score_low = score_grad.astype(jnp.bfloat16)
    value_grad = jnp.einsum(
        "hij,ihd->jhd", attn_probs.astype(jnp.bfloat16), dmixed, preferred_element_type=jnp.float32
    ).astype(jnp.bfloat16)
    rel_width = pos_key.shape[0]
    to_pos = spread_cols(score_grad, seq_ids, rel_width).astype(jnp.bfloat16)
    from_pos = spread_cols(jnp.swapaxes(score_grad, 1, 2), seq_ids, rel_width).astype(jnp.bfloat16)
    query_grad = (
        jnp.einsum("hij,jhd->ihd", score_low, key_rows, preferred_element_type=jnp.float32)
        + jnp.einsum("hir,rhd->ihd", to_pos, pos_key, preferred_element_type=jnp.float32)
    ).astype(jnp.bfloat16)
    key_grad = (
        jnp.einsum("hij,ihd->jhd", score_low, queries, preferred_element_type=jnp.float32)
        + jnp.einsum("hjr,rhd->jhd", from_pos, pos_query, preferred_element_type=jnp.float32)
    ).astype(jnp.bfloat16)
    acc_key = acc_key + jnp.einsum(
        "hir,ihd->rhd", to_pos, queries, preferred_element_type=jnp.float32
    )
    acc_query = acc_query + jnp.einsum(
        "hjr,jhd->rhd", from_pos, key_rows, preferred_element_type=jnp.float32
    )
    return ((acc_key, acc_query), (query_grad, key_grad, value_grad))


def local(
    tokens,
    rel_ids,
    mask_pos,
    grad_vals,
    w_query,
    w_key,
    w_value,
    w_out,
    b_query,
    b_key,
    b_value,
    b_out,
    rel_table,
    ln1_gain,
    ln1_bias,
    w_in,
    b_in,
    w_down,
    b_down,
    ln2_gain,
    ln2_bias,
):
    seq_count = rel_ids.shape[0]
    seq_len = rel_ids.shape[1]
    rows_here = tokens.shape[0]
    width = tokens.shape[1]
    table_rows = rel_table.shape[0]
    hidden_cols = w_in.shape[1]
    n_tok = lax.axis_size("tok")
    queries = (plain_dot(tokens, w_query) + b_query).astype(jnp.bfloat16)
    key_rows = (plain_dot(tokens, w_key) + b_key).astype(jnp.bfloat16)
    value_rows = (plain_dot(tokens, w_value) + b_value).astype(jnp.bfloat16)
    pos_query = (
        (plain_dot(rel_table, w_query) + b_query).astype(jnp.bfloat16).reshape(table_rows, H, DH)
    )
    pos_key = (plain_dot(rel_table, w_key) + b_key).astype(jnp.bfloat16).reshape(table_rows, H, DH)
    query_h = queries.reshape(seq_count, seq_len, H, DH)
    key_h = key_rows.reshape(seq_count, seq_len, H, DH)
    value_h = value_rows.reshape(seq_count, seq_len, H, DH)
    mixed_ctx, logsum = lax.map(
        partial(attend, pos_query, pos_key), (query_h, key_h, value_h, rel_ids)
    )
    context = mixed_ctx.reshape(rows_here, width)
    attn_out = plain_dot(context, w_out) + b_out
    middle, normed1, inv1 = norm_forward(tokens.astype(jnp.float32) + attn_out, ln1_gain, ln1_bias)
    middle_low = middle.astype(jnp.bfloat16)
    shard_rows = lax.all_gather(middle_low, "ffn", axis=0, tiled=True)
    pre_act = plain_dot(shard_rows, w_in) + b_in
    gathered = shard_rows
    hidden = jax.nn.gelu(pre_act, approximate=False).astype(jnp.bfloat16)
    branch = (
        lax.psum_scatter(
            plain_dot(hidden, w_down).astype(jnp.bfloat16), "ffn", scatter_dimension=0, tiled=True
        ).astype(jnp.float32)
        + b_down
    )
    final, normed2, inv2 = norm_forward(middle + branch, ln2_gain, ln2_bias)
    output = final.astype(jnp.bfloat16)
    seq_base = lax.broadcasted_iota(jnp.int32, mask_pos.shape, 0) * seq_len
    places = (mask_pos + seq_base).reshape(-1)
    valid = (mask_pos >= 0).reshape(-1)
    row_iota = lax.broadcasted_iota(jnp.int32, (places.shape[0], rows_here), 1)
    picker = ((places[:, None] == row_iota) & valid[:, None]).astype(jnp.bfloat16)
    cotangent = rows_inner(picker, grad_vals.reshape(-1, width))
    dz2, g_ln2_gain, g_ln2_bias = norm_backward(cotangent, normed2, inv2, ln2_gain)
    dbranch = dz2.astype(jnp.bfloat16)
    g_b_down = jnp.sum(dbranch.astype(jnp.float32), axis=0)
    shard_rows = lax.all_gather(dbranch, "ffn", axis=0, tiled=True)
    dpre = (cols_inner(shard_rows, w_down) * gelu_slope(pre_act)).astype(jnp.bfloat16)
    gw_down_t = rows_inner(shard_rows, hidden)
    gw_in = rows_inner(gathered, dpre)
    gb_in = jnp.sum(dpre.astype(jnp.float32), axis=0)
    gw_down_t, gw_in, gb_in, grad_store = (gw_down_t, gw_in, gb_in, dpre)
    dh1_ffn = lax.psum_scatter(
        cols_inner(grad_store, w_in).astype(jnp.bfloat16), "ffn", scatter_dimension=0, tiled=True
    ).astype(jnp.float32)
    dh1 = dz2 + dh1_ffn
    dz1, g_ln1_gain, g_ln1_bias = norm_backward(dh1, normed1, inv1, ln1_gain)
    dattn = dz1.astype(jnp.bfloat16)
    g_b_out = jnp.sum(dattn.astype(jnp.float32), axis=0)
    g_w_out = rows_inner(context, dattn)
    dcontext = cols_inner(dattn, w_out).astype(jnp.bfloat16).reshape(seq_count, seq_len, H, DH)
    zero_pos = jnp.zeros((table_rows, H, DH), jnp.float32)
    (acc_key, acc_query), (query_grad, key_grad, value_grad) = lax.scan(
        partial(attend_back, pos_query, pos_key),
        (zero_pos, zero_pos),
        (query_h, key_h, value_h, rel_ids, logsum, dcontext),
    )
    query_grad = query_grad.reshape(rows_here, width)
    key_grad = key_grad.reshape(rows_here, width)
    value_grad = value_grad.reshape(rows_here, width)
    acc_key = acc_key.reshape(table_rows, width)
    acc_query = acc_query.reshape(table_rows, width)
    grad_tokens = (
        dz1
        + cols_inner(query_grad, w_query)
        + cols_inner(key_grad, w_key)
        + cols_inner(value_grad, w_value)
    )
    g_w_query = rows_inner(tokens, query_grad) + rows_split(rel_table, acc_query)
    g_b_query = jnp.sum(query_grad.astype(jnp.float32), axis=0) + jnp.sum(acc_query, axis=0)
    g_w_key = rows_inner(tokens, key_grad) + rows_split(rel_table, acc_key)
    g_b_key = jnp.sum(key_grad.astype(jnp.float32), axis=0) + jnp.sum(acc_key, axis=0)
    g_w_value = rows_inner(tokens, value_grad)
    g_b_value = jnp.sum(value_grad.astype(jnp.float32), axis=0)
    g_rel = cols_split(acc_query, w_query) + cols_split(acc_key, w_key)
    vectors = jnp.stack(
        [
            g_b_query,
            g_b_key,
            g_b_value,
            g_b_out,
            g_ln1_gain,
            g_ln1_bias,
            g_b_down,
            g_ln2_gain,
            g_ln2_bias,
        ],
        axis=1,
    )
    gb_in_rows = gb_in.reshape(n_tok, hidden_cols // n_tok)
    s_wq, s_wk, s_wv, s_wo, s_rel, s_vec = (
        lax.psum_scatter(g_w_query, ("tok", "ffn"), scatter_dimension=0, tiled=True),
        lax.psum_scatter(g_w_key, ("tok", "ffn"), scatter_dimension=0, tiled=True),
        lax.psum_scatter(g_w_value, ("tok", "ffn"), scatter_dimension=0, tiled=True),
        lax.psum_scatter(g_w_out, ("tok", "ffn"), scatter_dimension=0, tiled=True),
        lax.psum_scatter(g_rel, ("tok", "ffn"), scatter_dimension=0, tiled=True),
        lax.psum_scatter(vectors, ("tok", "ffn"), scatter_dimension=0, tiled=True),
    )
    s_win, s_wdown_t, s_bin = (
        lax.psum_scatter(gw_in, "tok", scatter_dimension=0, tiled=True),
        lax.psum_scatter(gw_down_t, "tok", scatter_dimension=0, tiled=True),
        lax.psum_scatter(gb_in_rows, "tok", scatter_dimension=0, tiled=True),
    )
    return (
        output,
        grad_tokens,
        s_wq,
        s_wk,
        s_wv,
        s_wo,
        s_vec[:, 0],
        s_vec[:, 1],
        s_vec[:, 2],
        s_vec[:, 3],
        s_rel,
        s_vec[:, 4],
        s_vec[:, 5],
        s_win,
        s_bin,
        jnp.transpose(s_wdown_t),
        s_vec[:, 6],
        s_vec[:, 7],
        s_vec[:, 8],
    )


def solution(mesh):
    placed = (
        P(("tok", "ffn"), None),
        P(("tok", "ffn"), None, None),
        P(("tok", "ffn"), None),
        P(("tok", "ffn"), None, None),
        P(),
        P(),
        P(),
        P(),
        P(),
        P(),
        P(),
        P(),
        P(),
        P(),
        P(),
        P(None, "ffn"),
        P("ffn"),
        P("ffn", None),
        P(),
        P(),
        P(),
    )
    return jax.shard_map(
        local,
        mesh=mesh,
        in_specs=placed,
        out_specs=(
            P(("tok", "ffn"), None),
            P(("tok", "ffn"), None),
            P(("tok", "ffn"), None),
            P(("tok", "ffn"), None),
            P(("tok", "ffn"), None),
            P(("tok", "ffn"), None),
            P(("tok", "ffn")),
            P(("tok", "ffn")),
            P(("tok", "ffn")),
            P(("tok", "ffn")),
            P(("tok", "ffn"), None),
            P(("tok", "ffn")),
            P(("tok", "ffn")),
            P("tok", "ffn"),
            P("ffn", "tok"),
            P("ffn", "tok"),
            P(("tok", "ffn")),
            P(("tok", "ffn")),
            P(("tok", "ffn")),
        ),
        check_vma=False,
    )
```

profile of v0, /device:TPU:0, one launch (start us, length us, event | category | flops | bytes accessed | tf_op | source)
XLA Modules:
  0.0 2024.8 jit_solution(6676035225300939446)
XLA Ops:
  27.2 18.2 copy.162
  53.3 247.4 %while.79 = (s32[]{:T(128)}, f32[8,12,64,512]{3,1,2,0:T(8,128)}, s32[8,64,512]{2,1,0:T(8,128)}, f32[8,12,64,512]{3,1,2,0:T(8,128)}, s32[]{:T(128)}) while((s32[]{:T(128)}, f32[8,12,64,512]{3,1,2,0:T(8,128)}, s32[8,64,512]{2,1,0:T(8,128)}, f32[8,12,64,512]{3,1,2,0:T(8,128)}, s32[]{:T(128)}) %tuple.143), condition=%wide.region_1.2_spmd, body=%wide.region_0.1_spmd.sunk | while | flops 840826880 | bytes 8914497 | solution.py:99
  54.2 15.4 fusion.193
  69.6 14.6 bitcast_dynamic-update-slice_fusion.8
  85.1 15.4 fusion.193
  100.5 14.6 bitcast_dynamic-update-slice_fusion.8
  116.1 15.4 fusion.193
  131.5 14.6 bitcast_dynamic-update-slice_fusion.8
  147.0 15.4 fusion.193
  162.4 14.6 bitcast_dynamic-update-slice_fusion.8
  177.9 15.4 fusion.193
  193.3 14.6 bitcast_dynamic-update-slice_fusion.8
  208.9 15.4 fusion.193
  224.3 14.6 bitcast_dynamic-update-slice_fusion.8
  239.8 15.4 fusion.193
  255.2 14.6 bitcast_dynamic-update-slice_fusion.8
  270.7 15.4 fusion.193
  286.1 14.6 bitcast_dynamic-update-slice_fusion.8
  300.7 17.7 copy.104
  329.9 17.9 copy.161
  355.7 247.6 %while.80 = (s32[]{:T(128)}, f32[8,12,64,512]{3,1,2,0:T(8,128)}, s32[8,64,512]{2,1,0:T(8,128)}, f32[8,12,64,512]{3,1,2,0:T(8,128)}, s32[]{:T(128)}) while((s32[]{:T(128)}, f32[8,12,64,512]{3,1,2,0:T(8,128)}, s32[8,64,512]{2,1,0:T(8,128)}, f32[8,12,64,512]{3,1,2,0:T(8,128)}, s32[]{:T(128)}) %tuple.144), condition=%wide.region_3.4_spmd, body=%wide.region_2.3_spmd.sunk | while | flops 840826880 | bytes 8914497 | solution.py:99
  356.8 15.4 fusion.195
  372.2 14.6 bitcast_dynamic-update-slice_fusion.9
  387.7 15.4 fusion.195
  403.1 14.6 bitcast_dynamic-update-slice_fusion.9
  418.6 15.4 fusion.195
  434.0 14.6 bitcast_dynamic-update-slice_fusion.9
  449.5 15.4 fusion.195
  464.9 14.6 bitcast_dynamic-update-slice_fusion.9
  480.4 15.4 fusion.195
  495.8 14.6 bitcast_dynamic-update-slice_fusion.9
  511.4 15.4 fusion.195
  526.8 14.6 bitcast_dynamic-update-slice_fusion.9
  542.3 15.4 fusion.195
  557.7 14.6 bitcast_dynamic-update-slice_fusion.9
  573.2 15.4 fusion.195
  588.6 14.6 bitcast_dynamic-update-slice_fusion.9
  603.2 17.5 copy.107
  626.3 14.9 fusion.97
  655.4 30.0 %all-gather.3.cloned.1.call-done = bf16[1024,768]{1,0:T(8,128)(2,1)} async-done(((bf16[512,768]{1,0:T(8,128)(2,1)}), bf16[1024,768]{1,0:T(8,128)(2,1)}) %all-gather.3.cloned.1.call-update) | async-done | bytes 1572880 | tf_op jit(solution)/shard_map/all_gather | solution.py:224
  685.4 17.7 fusion.43
  709.0 25.7 %reduce-scatter.17.cloned.1.call-done = bf16[512,768]{1,0:T(8,128)(2,1)} async-done(((bf16[1024,768]{1,0:T(8,128)(2,1)}), bf16[512,768]{1,0:T(8,128)(2,1)}) %reduce-scatter.17.cloned.1.call-update) | async-done | bytes 786448 | tf_op jit(solution)/shard_map/reduce_scatter | solution.py:229
  741.7 27.3 %all-gather.5.cloned.1.call-done = bf16[1024,768]{1,0:T(8,128)(2,1)} async-done(((bf16[512,768]{1,0:T(8,128)(2,1)}), bf16[1024,768]{1,0:T(8,128)(2,1)}) %all-gather.5.cloned.1.call-update) | async-done | bytes 1572880 | tf_op jit(solution)/shard_map/all_gather | solution.py:245
  816.5 16.8 multiply_multiply_fusion
  833.3 18.4 copy.128
  851.7 17.9 copy.160
  869.6 221.8 %while.82 = (s32[]{:T(128)}, bf16[8,12,64,512]{3,1,2,0:T(8,128)(2,1)}, s32[8,64,512]{2,1,0:T(8,128)}, f32[8,12,64,512]{3,1,2,0:T(8,128)}, s32[]{:T(128)}) while((s32[]{:T(128)}, bf16[8,12,64,512]{3,1,2,0:T(8,128)(2,1)}, s32[8,64,512]{2,1,0:T(8,128)}, f32[8,12,64,512]{3,1,2,0:T(8,128)}, s32[]{:T(128)}) %tuple.145), condition=%wide.region_20.21_spmd, body=%wide.region_19.20_spmd.sunk | while | flops 840826880 | bytes 8914497 | solution.py:117
  870.8 13.8 fusion.199
  926.2 13.8 fusion.199
  953.9 13.8 fusion.199
  1009.3 13.8 fusion.199
  1037.0 13.8 fusion.199
  1064.6 13.8 fusion.199
  1107.9 222.0 %while.81 = (s32[]{:T(128)}, bf16[8,12,64,512]{3,1,2,0:T(8,128)(2,1)}, s32[8,64,512]{2,1,0:T(8,128)}, f32[8,12,64,512]{3,1,2,0:T(8,128)}, s32[]{:T(128)}) while((s32[]{:T(128)}, bf16[8,12,64,512]{3,1,2,0:T(8,128)(2,1)}, s32[8,64,512]{2,1,0:T(8,128)}, f32[8,12,64,512]{3,1,2,0:T(8,128)}, s32[]{:T(128)}) %tuple.146), condition=%wide.region_18.19_spmd, body=%wide.region_17.18_spmd.sunk | while | flops 840826880 | bytes 8914497 | solution.py:117
  1109.2 13.8 fusion.197
  1136.9 13.8 fusion.197
  1428.7 33.7 %all-reduce.1 = f32[16,96]{1,0:T(8,128)S(1)} all-reduce(f32[16,96]{1,0:T(8,128)S(1)} %reshape.269), channel_id=11, replica_groups=mesh['tok'=16,'ffn'=2] {'tok'}, use_global_device_ids=true, to_apply=%region_40.41.clone | all-reduce | flops 1536 | bytes 12288
  1464.0 37.3 %all-reduce = f32[768,9]{0,1:T(8,128)S(1)} all-reduce(f32[768,9]{0,1:T(8,128)S(1)} %stack.33), channel_id=8, replica_groups=mesh['tok'=16,'ffn'=2] {'tok','ffn'}, use_global_device_ids=true, to_apply=%region_36.37.clone | all-reduce | flops 6912 | bytes 55296
  1507.2 38.9 %reduce-scatter.21.cloned.1.call-done = f32[24,768]{1,0:T(8,128)} async-done(((f32[768,768]{1,0:T(8,128)}), f32[24,768]{1,0:T(8,128)}) %reduce-scatter.21.cloned.1.call-update) | async-done | bytes 73744 | tf_op jit(solution)/shard_map/reduce_scatter | solution.py:303
  1546.1 104.6 %reduce-scatter.31.cloned.1.call-done = f32[24,768]{1,0:T(8,128)} async-done(((f32[768,768]{1,0:T(8,128)}), f32[24,768]{1,0:T(8,128)}) %reduce-scatter.31.cloned.1.call-update) | async-done | bytes 73744
  1650.8 104.0 %reduce-scatter.29.cloned.1.call-done = f32[24,768]{1,0:T(8,128)} async-done(((f32[768,768]{1,0:T(8,128)}), f32[24,768]{1,0:T(8,128)}) %reduce-scatter.29.cloned.1.call-update) | async-done | bytes 73744
  1754.7 104.7 %reduce-scatter.33.cloned.1.call-done = f32[24,768]{1,0:T(8,128)} async-done(((f32[768,768]{1,0:T(8,128)}), f32[24,768]{1,0:T(8,128)}) %reduce-scatter.33.cloned.1.call-update) | async-done | bytes 73744
  1859.4 78.9 %reduce-scatter.27.cloned.1.call-done = f32[48,1536]{1,0:T(8,128)} async-done(((f32[768,1536]{1,0:T(8,128)}), f32[48,1536]{1,0:T(8,128)}) %reduce-scatter.27.cloned.1.call-update) | async-done | bytes 294928 | tf_op jit(solution)/shard_map/reduce_scatter | solution.py:309
  1938.3 79.5 %reduce-scatter.25.cloned.1.call-done = f32[48,1536]{1,0:T(8,128)} async-done(((f32[768,1536]{1,0:T(8,128)}), f32[48,1536]{1,0:T(8,128)}) %reduce-scatter.25.cloned.1.call-update) | async-done | bytes 294928 | tf_op jit(solution)/shard_map/reduce_scatter | solution.py:308
  (316 shorter events, 596.2 us)
Async XLA Ops:
  7.2 678.2 %copy-start = (bf16[768,1536]{1,0:T(8,128)(2,1)S(1)}, bf16[768,1536]{1,0:T(8,128)(2,1)}, u32[]{:S(2)}) copy-start(bf16[768,1536]{1,0:T(8,128)(2,1)} %param.44) | copy-start | bytes 7077892
  7.2 3.4 copy-start.69
  7.2 3.4 copy-start.16
  7.2 678.2 %all-gather.3.cloned.1.call-start = ((), (), s32[]{:S(2)}) async-start(), calls=%async_computation.9 | async-start | bytes 2359296 | tf_op jit(solution)/shard_map/all_gather | solution.py:224
  7.3 3.3 copy-start.40
  10.6 1.7 copy-start.64
  17.1 10.1 copy-start.5
  319.8 10.1 copy-start.8
  603.2 17.5 copy-start.71
  620.8 5.6 copy-start.6
  626.3 21.6 %copy-start.44 = (bf16[512,768]{0,1:T(8,128)(2,1)S(1)}, bf16[512,768]{0,1:T(8,128)(2,1)}, u32[]{:S(2)}) copy-start(bf16[512,768]{0,1:T(8,128)(2,1)} %copy.98) | copy-start | bytes 2359300
  641.3 8.2 copy-start.2
  649.4 2.5 copy-start.17
  649.4 2.5 copy-start.62
  649.5 2.5 copy-start.72
  651.9 2.1 copy-start.48
  652.0 2.1 copy-start.50
  653.0 32.4 %copy-start.68 = (f32[1536]{0:T(1024)S(1)}, f32[1536]{0:T(1024)}, u32[]{:S(2)}) copy-start(f32[1536]{0:T(1024)} %param.45) | copy-start | bytes 18436
  655.3 79.4 %reduce-scatter.17.cloned.1.call-start = ((), (), s32[]{:S(2)}) async-start(), calls=%async_computation.10 | async-start | bytes 2359296 | tf_op jit(solution)/shard_map/reduce_scatter | solution.py:229
  685.4 19.4 copy-start.61
  704.8 4.2 copy-start.73
  704.8 29.9 %copy-start.56 = (f32[768]{0:T(1024)S(1)}, f32[768]{0:T(1024)}, u32[]{:S(2)}) copy-start(f32[768]{0:T(1024)} %param.47) | copy-start | bytes 9220
  708.5 60.6 %all-gather.5.cloned.1.call-start = ((), (), s32[]{:S(2)}) async-start(), calls=%async_computation.11 | async-start | bytes 2359296 | tf_op jit(solution)/shard_map/all_gather | solution.py:245
  708.9 28.3 %copy-start.59 = (f32[768]{0:T(1024)S(1)}, f32[768]{0:T(1024)}, u32[]{:S(2)}) copy-start(f32[768]{0:T(1024)} %param.48) | copy-start | bytes 9220
  708.9 28.3 %copy-start.67 = (bf16[1,80,768]{2,1,0:T(8,128)(2,1)S(1)}, bf16[1,80,768]{2,1,0:T(8,128)(2,1)}, u32[]{:S(2)}) copy-start(bf16[1,80,768]{2,1,0:T(8,128)(2,1)} %param.32) | copy-start | bytes 368644
  736.9 1.8 copy-start.60
  741.7 66.7 %reduce-scatter.19.cloned.1.call-start = ((), (), s32[]{:S(2)}) async-start(), calls=%async_computation.12 | async-start | bytes 2359296 | tf_op jit(solution)/shard_map/reduce_scatter | solution.py:251
  776.6 1.8 copy-start.27
  782.2 725.0 %reduce-scatter.23.cloned.1.call-start = ((), (), s32[]{:S(2)}) async-start(), calls=%async_computation.14 | async-start | bytes 1622016 | tf_op jit(solution)/shard_map/reduce_scatter | solution.py:304
  786.5 21.9 %copy-start.4 = (f32[512,768]{1,0:T(8,128)S(1)}, f32[512,768]{1,0:T(8,128)}, u32[]{:S(2)}) copy-start(f32[512,768]{1,0:T(8,128)} %copy-done.3) | copy-start | bytes 4718596
  794.8 21.7 %copy-start.46 = (f32[12,512]{1,0:T(8,128)}, f32[12,512]{1,0:T(8,128)S(1)}, u32[]{:S(2)}) copy-start(f32[12,512]{1,0:T(8,128)S(1)} %log_add_fusion) | copy-start | bytes 73732
  808.4 3.1 copy-start.30
  811.5 3.8 copy-start.63
  816.4 16.8 copy-start.22
  869.6 221.8 %copy-start.9 = (bf16[512,768]{0,1:T(8,128)(2,1)S(1)}, bf16[512,768]{0,1:T(8,128)(2,1)}, u32[]{:S(2)}) copy-start(bf16[512,768]{0,1:T(8,128)(2,1)} %copy-done.8) | copy-start | bytes 2359300
  1102.2 1.7 copy-start.65
  1102.3 5.6 copy-start.24
  1102.4 5.6 copy-start.28
  1107.9 222.0 %copy-start.7 = (bf16[512,768]{0,1:T(8,128)(2,1)S(1)}, bf16[512,768]{0,1:T(8,128)(2,1)}, u32[]{:S(2)}) copy-start(bf16[512,768]{0,1:T(8,128)(2,1)} %copy-done.5) | copy-start | bytes 2359300
  1340.3 4.5 copy-start.31
  1340.3 2.2 copy-start.38
  1340.3 2.4 copy-start.39
  1344.8 201.4 %reduce-scatter.21.cloned.1.call-start = ((), (), s32[]{:S(2)}) async-start(), calls=%async_computation.13 | async-start | bytes 2433024 | tf_op jit(solution)/shard_map/reduce_scatter | solution.py:303
  1348.7 302.1 %reduce-scatter.31.cloned.1.call-start = ((), (), s32[]{:S(2)}) async-start(), calls=%async_computation.18 | async-start | bytes 2433024
  1351.7 6.8 copy-start.15
  1358.5 10.5 copy-start.18
  1375.4 379.3 %reduce-scatter.29.cloned.1.call-start = ((), (), s32[]{:S(2)}) async-start(), calls=%async_computation.17 | async-start | bytes 2433024
  1377.3 6.0 copy-start.14
  1383.3 10.4 copy-start.19
  1393.7 3.7 copy-start.34
  1400.6 458.8 %reduce-scatter.33.cloned.1.call-start = ((), (), s32[]{:S(2)}) async-start(), calls=%async_computation.19 | async-start | bytes 2433024
  1412.1 526.2 %reduce-scatter.27.cloned.1.call-start = ((), (), s32[]{:S(2)}) async-start(), calls=%async_computation.16 | async-start | bytes 5013504 | tf_op jit(solution)/shard_map/reduce_scatter | solution.py:309
  1419.7 598.1 %reduce-scatter.25.cloned.1.call-start = ((), (), s32[]{:S(2)}) async-start(), calls=%async_computation.15 | async-start | bytes 5013504 | tf_op jit(solution)/shard_map/reduce_scatter | solution.py:308
  1427.4 36.3 %copy-start.49 = (f32[12,64]{1,0:T(8,128)S(1)}, f32[12,64]{1,0:T(8,128)}, u32[]{:S(2)}) copy-start(f32[12,64]{1,0:T(8,128)} %get-tuple-element.333) | copy-start | bytes 9220
  1427.4 36.5 %copy-start.54 = (f32[768]{0:T(1024)S(1)}, f32[768]{0:T(1024)}, u32[]{:S(2)}) copy-start(f32[768]{0:T(1024)} %get-tuple-element.304) | copy-start | bytes 9220
  1427.4 36.5 %copy-start.52 = (f32[768]{0:T(1024)S(1)}, f32[768]{0:T(1024)}, u32[]{:S(2)}) copy-start(f32[768]{0:T(1024)} %get-tuple-element.261) | copy-start | bytes 9220
  1427.4 36.5 %copy-start.51 = (f32[768]{0:T(1024)S(1)}, f32[768]{0:T(1024)}, u32[]{:S(2)}) copy-start(f32[768]{0:T(1024)} %get-tuple-element.266) | copy-start | bytes 9220
  1427.4 74.5 %copy-start.35 = (bf16[12,64,512]{2,1,0:T(8,128)(2,1)S(1)}, bf16[12,64,512]{2,1,0:T(8,128)(2,1)}, u32[]{:S(2)}) copy-start(bf16[12,64,512]{2,1,0:T(8,128)(2,1)} %copy-done.34) | copy-start | bytes 2359300
  1427.4 74.5 %copy-start.66 = (bf16[768,768]{1,0:T(8,128)(2,1)S(1)}, bf16[768,768]{1,0:T(8,128)(2,1)}, u32[]{:S(2)}) copy-start(bf16[768,768]{1,0:T(8,128)(2,1)} %param.33) | copy-start | bytes 3538948
  1427.5 75.3 %copy-start.33 = (bf16[12,64,512]{2,1,0:T(8,128)(2,1)S(1)}, bf16[12,64,512]{2,1,0:T(8,128)(2,1)}, u32[]{:S(2)}) copy-start(bf16[12,64,512]{2,1,0:T(8,128)(2,1)} %copy-done.32) | copy-start | bytes 2359300
  1502.8 2.3 copy-start.11
  1502.8 2.3 copy-start.21
  1502.8 2.4 copy-start.42
  1502.8 515.0 %copy-start.1 = (bf16[768,1536]{1,0:T(8,128)(2,1)S(1)}, bf16[768,1536]{1,0:T(8,128)(2,1)}, u32[]{:S(2)}) copy-start(bf16[768,1536]{1,0:T(8,128)(2,1)} %param.44) | copy-start | bytes 7077892
  (22 other events, 27.3 us)
Sparse Core Ops, SparseCore 0:
  655.4 29.8 all-gather.2
  708.6 26.0 reduce-scatter.16
  741.8 27.2 all-gather.4
  782.3 26.0 reduce-scatter.18
  1344.9 97.1 reduce-scatter.22
  1447.8 98.2 reduce-scatter.20
  1552.8 97.8 reduce-scatter.30
  1656.6 98.0 reduce-scatter.28
  1761.5 97.8 reduce-scatter.32
  1863.7 74.6 reduce-scatter.26
  1943.3 74.5 reduce-scatter.24
where the time goes:
time: 2040 us; the launch traced here: 2020 us
  matrix products  1100 us (54%)
  waiting for transfers between devices  608 us (30%)
  local copies, waits for them, and re-layouts  200 us (10%)
  blocking collectives  71 us (3%)
  other arithmetic  23.9 us (1%)
    unnamed x14, waiting for transfers between devices  313 us
    dot_general x16, matrix products, pick_block(): jnp.einsum('hir,ijr->hij', lower_part, selector, preferred_element_type=j...  246 us
    dot_general x16, matrix products, pick_block(): jnp.einsum('hir,ijr->hij', upper_part, selector, preferred_element_type=j...  234 us
    dot_general x16, matrix products, spread_block(): jnp.einsum('hij,ijr->hir', lower_part, selector, preferred_element_type=j...  221 us
    dot_general x16, matrix products, spread_block(): jnp.einsum('hij,ijr->hir', upper_part, selector, preferred_element_type=j...  207 us
    reduce_scatter x1, waiting for transfers between devices, local(): lax.psum_scatter(gw_in, 'tok', scatter_dimension=0, tiled=True)  79.5 us
    reduce_scatter x1, waiting for transfers between devices, local(): lax.psum_scatter(gw_down_t, 'tok', scatter_dimension=0, tiled=True)  78.9 us
    unnamed x2, blocking collectives  71 us
  transfers between devices with their start and end apart: 11, of which 10 were waited for; matrix products, arithmetic and copies ran while one was open for 5% of the time, Pallas kernels for 0%

commit v1 on v0

v1 whole, which is shorter than its diff:
```python
import math

import numpy as np

import jax
import jax.numpy as jnp
from jax import lax
from jax.experimental import pallas as pl
from jax.experimental.pallas import tpu as pltpu
from jax.sharding import PartitionSpec as P

HEAD = 64
LANES = 128
ROWS = 32
norm_eps = 1e-07
bf16 = jnp.bfloat16
f32 = jnp.float32


def dot_nn(first_op, second_op):
    return lax.dot_general(
        first_op, second_op, (((1,), (0,)), ((), ())), preferred_element_type=f32
    )


def dot_nt(first_op, second_op):
    return lax.dot_general(
        first_op, second_op, (((1,), (1,)), ((), ())), preferred_element_type=f32
    )


def dot_tn(first_op, second_op):
    return lax.dot_general(
        first_op, second_op, (((0,), (0,)), ((), ())), preferred_element_type=f32
    )


def distance_rows(seq_len, table_rows):
    side = table_rows // 2
    middle = side // 2
    rows = []
    for m in range(2 * seq_len):
        offset = max(seq_len - 1 - m, 1 - seq_len)
        size = abs(offset)
        if size > middle:
            ratio = math.log(size / middle) / math.log((2 * side - 1) / middle)
            size = int(math.ceil(ratio * (middle - 1))) + middle
        rows.append(side + (size if offset > 0 else -size))
    return np.array(rows, dtype=np.int32)


def lane_iota(rows=1):
    return lax.broadcasted_iota(jnp.int32, (rows, LANES), 1)


def member_chunk(words, c):
    return (words == lane_iota(words.shape[0]) + c * LANES).astype(f32).astype(bf16)


def shift_in_order(source, words_ref, base, emit):
    seq = words_ref.shape[0]
    chunks = seq // LANES
    lane = lane_iota()
    for g in range(chunks):
        first = base[g]
        for sub in range(LANES // ROWS):
            start = g * LANES + sub * ROWS
            rows = slice(start, start + ROWS)
            place = lane + (seq - 1) - words_ref[rows, :] - first * LANES
            index = place & (LANES - 1)
            turned = []
            for c in range(chunks + 2):
                at = pl.multiple_of(jnp.minimum(first + c, 2 * chunks - 1) * LANES, LANES)
                turned.append(
                    jnp.take_along_axis(source[rows, pl.ds(at, LANES)], index, axis=1)
                )
            near = place < LANES
            mid = place < 2 * LANES
            for c in range(chunks):
                value = jnp.where(
                    near, turned[c], jnp.where(mid, turned[c + 1], turned[c + 2])
                )
                emit(rows, c, value)


def unshift_in_order(source, words_ref, base, dest):
    seq = words_ref.shape[0]
    chunks = seq // LANES
    lane = lane_iota()
    zero = jnp.zeros((ROWS, LANES), f32)
    for g in range(chunks):
        first = base[g]
        for sub in range(LANES // ROWS):
            start = g * LANES + sub * ROWS
            rows = slice(start, start + ROWS)
            place = lane - (seq - 1) + words_ref[rows, :] + first * LANES
            index = place & (LANES - 1)
            turned = [
                jnp.take_along_axis(
                    source[rows, c * LANES : (c + 1) * LANES], index, axis=1
                )
                for c in range(chunks)
            ]

            def pick(c):
                return turned[c] if 0 <= c < chunks else zero

            near = place >= 0
            mid = place >= -LANES
            for c in range(chunks + 2):
                value = jnp.where(near, pick(c), jnp.where(mid, pick(c - 1), pick(c - 2)))
                at = pl.multiple_of((first + c) * LANES, LANES)
                dest[rows, pl.ds(at, LANES)] = value.astype(bf16)


def group_bases(words, base):
    seq = words.shape[0]
    for g in range(seq // LANES):
        top = jnp.max(words[g * LANES : (g + 1) * LANES])
        base[g] = (seq - 1 - top) // LANES


def split_store(dest, rows, upper_at, lower_at, value):
    upper = value.astype(bf16)
    dest[rows, upper_at : upper_at + LANES] = upper
    dest[rows, lower_at : lower_at + LANES] = (value - upper.astype(f32)).astype(bf16)


def softmax_rows(scores):
    factor = math.log2(math.e) / math.sqrt(3.0 * HEAD)
    weights = jnp.exp2((scores - jnp.max(scores, axis=1, keepdims=True)) * factor)
    return (weights * (1.0 / jnp.sum(weights, axis=1, keepdims=True))).astype(bf16)


def picked_kernel(
    rel_ref, pick_ref, qc_ref, k_ref, v_ref, pk_ref, pq_ref,
    ctx_ref, prob_ref, keyrow_ref, word_ref, wordc_ref,
    left, right, crel, base,
):
    seq = k_ref.shape[0]
    picks = qc_ref.shape[0]
    chunks = seq // LANES
    at = [LANES + n * seq for n in range(4)]

    @pl.when(pl.program_id(0) == 0)
    def _():
        row = lax.broadcasted_iota(jnp.int32, (seq, seq), 0)
        col = lax.broadcasted_iota(jnp.int32, (seq, seq), 1)
        side = pk_ref.shape[0] // 4
        step = jnp.sum(jnp.where(col == row - 1, rel_ref[...] - side, 0), axis=1, keepdims=True)
        steps = jnp.broadcast_to(step.astype(f32), (seq, LANES)).astype(bf16)
        words = dot_nn((col <= row).astype(f32).astype(bf16), steps).astype(jnp.int32)
        word_ref[...] = words
        group_bases(words, base)
        for c in range(chunks):
            member = member_chunk(words, c)
            right[:, at[0] + c * LANES : at[0] + (c + 1) * LANES] = member
            right[:, at[1] + c * LANES : at[1] + (c + 1) * LANES] = member
        memberc = dot_nn(pick_ref[...], right[:, at[0] : at[1]])
        left[:, at[2] : at[3]] = memberc.astype(bf16)
        left[:, at[3] : at[3] + seq] = memberc.astype(bf16)
        index = lax.broadcasted_iota(jnp.int32, (picks, seq), 1).astype(f32)
        total = jnp.sum(memberc * index, axis=1, keepdims=True)
        wordc_ref[...] = jnp.broadcast_to(total, (picks, LANES)).astype(jnp.int32)

    lane = lane_iota()
    zero = jnp.zeros((), bf16)
    for a in range(2):
        mine = (lane < HEAD) if a == 0 else (lane >= HEAD)
        q_a = jnp.where(mine, qc_ref[...], zero)
        k_a = jnp.where(mine, k_ref[...], zero)
        left[:, :LANES] = q_a
        right[:, :LANES] = k_a
        crel[...] = dot_nt(k_a, pq_ref[...])
        far = dot_nt(q_a, pk_ref[...])

        def emit(rows, c, value):
            split_store(right, rows, at[2] + c * LANES, at[3] + c * LANES, value)

        shift_in_order(crel, word_ref, base, emit)
        keyrow_ref[a] = right[:, at[2] :]
        place = lane + (seq - 1) - wordc_ref[...]
        index = place & (LANES - 1)
        turned = [
            jnp.take_along_axis(far[:, c * LANES : (c + 1) * LANES], index, axis=1)
            for c in range(2 * chunks)
        ]
        for c in range(chunks):
            value = turned[c]
            for n in range(1, chunks + 1):
                if c + n < 2 * chunks:
                    value = jnp.where(place >= n * LANES, turned[c + n], value)
            split_store(left, slice(None), at[0] + c * LANES, at[1] + c * LANES, value)
        probs = softmax_rows(dot_nt(left[...], right[...]))
        prob_ref[a] = probs
        mixed = dot_nn(probs, v_ref[...]).astype(bf16)
        if a == 0:
            ctx_ref[...] = mixed
        else:
            ctx_ref[...] = jnp.where(mine, mixed, ctx_ref[...])


def attend_picked(rel_ids, pick, q_pick, k, v, pos_query, pos_key):
    seq, width = k.shape
    picks = q_pick.shape[0]
    pairs = width // LANES
    wide = LANES + 4 * seq
    whole = lambda rows, cols: pl.BlockSpec((rows, cols), lambda h: (0, 0))
    col = lambda rows: pl.BlockSpec((rows, LANES), lambda h: (0, h))
    return pl.pallas_call(
        picked_kernel,
        grid=(pairs,),
        in_specs=[
            whole(seq, seq), whole(picks, seq),
            col(picks), col(seq), col(seq), col(2 * seq), col(2 * seq),
        ],
        out_specs=[
            col(picks),
            pl.BlockSpec((2, picks, seq), lambda h: (h, 0, 0)),
            pl.BlockSpec((2, seq, 2 * seq), lambda h: (h, 0, 0)),
            whole(seq, LANES), whole(picks, LANES),
        ],
        out_shape=[
            jax.ShapeDtypeStruct((picks, width), bf16),
            jax.ShapeDtypeStruct((2 * pairs, picks, seq), bf16),
            jax.ShapeDtypeStruct((2 * pairs, seq, 2 * seq), bf16),
            jax.ShapeDtypeStruct((seq, LANES), jnp.int32),
            jax.ShapeDtypeStruct((picks, LANES), jnp.int32),
        ],
        scratch_shapes=[
            pltpu.VMEM((picks, wide), bf16),
            pltpu.VMEM((seq, wide), bf16),
            pltpu.VMEM((seq, 2 * seq), f32),
            pltpu.SMEM((seq // LANES,), jnp.int32),
        ],
        compiler_params=pltpu.CompilerParams(vmem_limit_bytes=48 * 2**20),
        name="attend_picked",
    )(rel_ids, pick, q_pick, k, v, pos_key, pos_query)


def full_kernel(
    word_ref, q_ref, k_ref, v_ref, pk_ref, keyrow_ref, ctx_ref, left, right, crel, base
):
    seq = q_ref.shape[0]
    chunks = seq // LANES
    at = [LANES + n * seq for n in range(4)]

    @pl.when(pl.program_id(0) == 0)
    def _():
        words = word_ref[...]
        group_bases(words, base)
        for c in range(chunks):
            member = member_chunk(words, c)
            for ref, n in ((right, 0), (right, 1), (left, 2), (left, 3)):
                ref[:, at[n] + c * LANES : at[n] + (c + 1) * LANES] = member

    lane = lane_iota()
    zero = jnp.zeros((), bf16)
    for a in range(2):
        mine = (lane < HEAD) if a == 0 else (lane >= HEAD)
        q_a = jnp.where(mine, q_ref[...], zero)
        left[:, :LANES] = q_a
        right[:, :LANES] = k_ref[...]
        right[:, at[2] :] = keyrow_ref[a]
        crel[...] = dot_nt(q_a, pk_ref[...])

        def emit(rows, c, value):
            split_store(left, rows, at[0] + c * LANES, at[1] + c * LANES, value)

        shift_in_order(crel, word_ref, base, emit)
        for g in range(chunks):
            rows = slice(g * LANES, (g + 1) * LANES)
            probs = softmax_rows(dot_nt(left[rows, :], right[...]))
            mixed = dot_nn(probs, v_ref[...]).astype(bf16)
            if a == 0:
                ctx_ref[rows, :] = mixed
            else:
                ctx_ref[rows, :] = jnp.where(mine, mixed, ctx_ref[rows, :])


def attend_full(words, q, k, v, pos_key, keyrows):
    seq, width = k.shape
    pairs = width // LANES
    wide = LANES + 4 * seq
    col = lambda rows: pl.BlockSpec((rows, LANES), lambda h: (0, h))
    return pl.pallas_call(
        full_kernel,
        grid=(pairs,),
        in_specs=[
            pl.BlockSpec((seq, LANES), lambda h: (0, 0)),
            col(seq), col(seq), col(seq), col(2 * seq),
            pl.BlockSpec((2, seq, 2 * seq), lambda h: (h, 0, 0)),
        ],
        out_specs=col(seq),
        out_shape=jax.ShapeDtypeStruct((seq, width), bf16),
        scratch_shapes=[
            pltpu.VMEM((seq, wide), bf16),
            pltpu.VMEM((seq, wide), bf16),
            pltpu.VMEM((seq, 2 * seq), f32),
            pltpu.SMEM((seq // LANES,), jnp.int32),
        ],
        compiler_params=pltpu.CompilerParams(vmem_limit_bytes=48 * 2**20),
        name="attend_full",
    )(words, q, k, v, pos_key, keyrows)


def back_kernel(
    word_ref, wordc_ref, qc_ref, k_ref, v_ref, dctx_ref, prob_ref, pk_ref, pq_ref,
    dq_ref, dk_ref, dv_ref, dpk_ref, dpq_ref,
    side, sidec, moved, movedc, grel, base,
):
    seq = k_ref.shape[0]
    picks = qc_ref.shape[0]
    chunks = seq // LANES

    @pl.when(pl.program_id(0) == 0)
    def _():
        words = word_ref[...]
        for c in range(chunks):
            side[:, c * LANES : (c + 1) * LANES] = member_chunk(words, c)
            sidec[:, c * LANES : (c + 1) * LANES] = member_chunk(wordc_ref[...], c)
        group_bases(words, base)
        moved[...] = jnp.zeros_like(moved)

    lane = lane_iota()
    scale = 1.0 / math.sqrt(3.0 * HEAD)
    zero = jnp.zeros((), bf16)
    for a in range(2):
        mine = (lane < HEAD) if a == 0 else (lane >= HEAD)
        keep = lambda value: jnp.where(mine, value, zero)
        dctx_a = keep(dctx_ref[...])
        q_a = keep(qc_ref[...])
        k_a = keep(k_ref[...])
        side[:, seq:] = k_a
        sidec[:, seq:] = q_a
        dprobs = dot_nt(dctx_a, v_ref[...])
        probs = prob_ref[a].astype(f32)
        prod = probs * dprobs
        gs = ((prod - probs * jnp.sum(prod, axis=1, keepdims=True)) * scale).astype(bf16)
        dv = dot_tn(prob_ref[a], dctx_a)

        out = dot_nn(gs, side[...])
        place = lane - (seq - 1) + wordc_ref[...]
        index = place & (LANES - 1)
        turned = [
            jnp.take_along_axis(out[:, c * LANES : (c + 1) * LANES], index, axis=1)
            for c in range(chunks)
        ]
        blank = jnp.zeros((picks, LANES), f32)
        for c in range(2 * chunks):
            value = turned[c] if c < chunks else blank
            for n in range(1, chunks + 1):
                other = turned[c - n] if 0 <= c - n < chunks else blank
                value = jnp.where(place < -LANES * (n - 1), other, value)
            movedc[:, c * LANES : (c + 1) * LANES] = value.astype(bf16)
        dq = out[:, seq:] + dot_nn(movedc[...], keep(pk_ref[...]))
        dpk = dot_tn(movedc[...], q_a)

        out = dot_tn(gs, sidec[...])
        grel[...] = out[:, :seq]
        unshift_in_order(grel, word_ref, base, moved)
        dk = out[:, seq:] + dot_nn(moved[:, : 2 * seq], keep(pq_ref[...]))
        dpq = dot_tn(moved[:, : 2 * seq], k_a)
        for ref, value in (
            (dq_ref, dq), (dk_ref, dk), (dv_ref, dv), (dpk_ref, dpk), (dpq_ref, dpq),
        ):
            low = value.astype(bf16)
            ref[...] = low if a == 0 else jnp.where(mine, low, ref[...])


def attend_back(words, words_pick, q_pick, k, v, dctx, probs, pos_query, pos_key):
    seq, width = k.shape
    picks = q_pick.shape[0]
    pairs = width // LANES
    whole = lambda rows, cols: pl.BlockSpec((rows, cols), lambda h: (0, 0))
    col = lambda rows: pl.BlockSpec((rows, LANES), lambda h: (0, h))
    shape = lambda rows: jax.ShapeDtypeStruct((rows, width), bf16)
    return pl.pallas_call(
        back_kernel,
        grid=(pairs,),
        in_specs=[
            whole(seq, LANES), whole(picks, LANES),
            col(picks), col(seq), col(seq), col(picks),
            pl.BlockSpec((2, picks, seq), lambda h: (h, 0, 0)),
            col(2 * seq), col(2 * seq),
        ],
        out_specs=[col(picks), col(seq), col(seq), col(2 * seq), col(2 * seq)],
        out_shape=[shape(picks), shape(seq), shape(seq), shape(2 * seq), shape(2 * seq)],
        scratch_shapes=[
            pltpu.VMEM((seq, seq + LANES), bf16),
            pltpu.VMEM((picks, seq + LANES), bf16),
            pltpu.VMEM((seq, 2 * seq + LANES), bf16),
            pltpu.VMEM((picks, 2 * seq), bf16),
            pltpu.VMEM((seq, seq), f32),
            pltpu.SMEM((seq // LANES,), jnp.int32),
        ],
        compiler_params=pltpu.CompilerParams(vmem_limit_bytes=48 * 2**20),
        name="attend_back",
    )(words, words_pick, q_pick, k, v, dctx, probs, pos_key, pos_query)


def norm_stats(values):
    centered = values - jnp.mean(values, axis=1, keepdims=True)
    inv_std = lax.rsqrt(jnp.mean(centered * centered, axis=1, keepdims=True) + norm_eps)
    return centered * inv_std, inv_std


def norm_backward(upstream, normed, inv_std, norm_gain):
    scaled = upstream * norm_gain
    adjusted = (
        scaled
        - jnp.mean(scaled, axis=1, keepdims=True)
        - normed * jnp.mean(scaled * normed, axis=1, keepdims=True)
    )
    return (inv_std * adjusted, jnp.sum(upstream * normed, axis=0), jnp.sum(upstream, axis=0))


def normal_cdf(pre_act):
    return 0.5 * (1.0 + lax.erf(pre_act * (1.0 / math.sqrt(2.0))))


def swap(values, axis, bit):
    size = lax.axis_size(axis)
    return lax.ppermute(values, axis, [(n, n ^ bit) for n in range(size)])


def halve_over(values, axis):
    size = lax.axis_size(axis)
    me = lax.axis_index(axis)
    bit = 1
    while bit < size:
        mine = (me // bit) % 2
        view = values.reshape((values.shape[0] // 2, 2) + values.shape[1:])
        send = lax.dynamic_index_in_dim(view, 1 - mine, 1, keepdims=False)
        keep = lax.dynamic_index_in_dim(view, mine, 1, keepdims=False)
        values = (keep.astype(f32) + swap(send, axis, bit).astype(f32)).astype(bf16)
        bit *= 2
    return values[0]


def local(
    tokens, rel_ids, mask_pos, grad_vals, w_query, w_key, w_value, w_out, b_query, b_key,
    b_value, b_out, rel_table, ln1_gain, ln1_bias, w_in, b_in, w_down, b_down, ln2_gain, ln2_bias,
):
    seq_count, seq_len = rel_ids.shape[0], rel_ids.shape[1]
    rows_here, width = tokens.shape
    table_rows = rel_table.shape[0]
    hidden_cols = w_in.shape[1]
    slots = mask_pos.shape[1]
    n_tok = lax.axis_size("tok")
    n_ffn = lax.axis_size("ffn")
    low = lambda value: value.astype(bf16)

    q = low(dot_nn(tokens, w_query) + b_query)
    k = low(dot_nn(tokens, w_key) + b_key)
    v = low(dot_nn(tokens, w_value) + b_value)
    to_rows = (
        distance_rows(seq_len, table_rows)[:, None] == np.arange(table_rows)[None, :]
    ).astype(np.float32)
    expand = jnp.asarray(to_rows, bf16)
    pos_query = low(dot_nn(expand, low(dot_nn(rel_table, w_query) + b_query)))
    pos_key = low(dot_nn(expand, low(dot_nn(rel_table, w_key) + b_key)))

    place = mask_pos + lax.broadcasted_iota(jnp.int32, mask_pos.shape, 0) * seq_len
    place = jnp.where(mask_pos >= 0, place, -1).reshape(-1)
    pick = low(place[:, None] == lax.broadcasted_iota(jnp.int32, (place.shape[0], rows_here), 1))
    x_pick = dot_nn(pick, tokens)
    q_pick = low(dot_nn(pick, q))

    def seq_rows(values, s, count):
        return values if seq_count == 1 else values[s * count : (s + 1) * count]

    firsts = []
    for s in range(seq_count):
        rows = lambda value: seq_rows(value, s, seq_len)
        own_pick = seq_rows(pick, s, slots)
        if seq_count > 1:
            own_pick = own_pick[:, s * seq_len : (s + 1) * seq_len]
        firsts.append(
            attend_picked(
                rel_ids[s], own_pick, seq_rows(q_pick, s, slots), rows(k), rows(v), pos_query, pos_key
            )
        )
    join = lambda parts: parts[0] if seq_count == 1 else jnp.concatenate(parts, axis=0)
    ctx_pick = join([first[0] for first in firsts])

    h1_normed, h1_inv = norm_stats(x_pick + (dot_nn(ctx_pick, w_out) + b_out))
    h1_pick = h1_normed * ln1_gain + ln1_bias
    h1_mine = low(h1_pick)
    pair = lambda value: jnp.concatenate([value, swap(value, "ffn", 1)], axis=0)
    count = h1_mine.shape[0]
    both = lambda value: low(value)[:count].astype(f32) + swap(low(value)[count:], "ffn", 1).astype(f32)
    h1_both = pair(h1_mine)
    pre = dot_nn(h1_both, w_in) + b_in
    cdf = normal_cdf(pre)
    hidden = low(pre * cdf)
    branch = both(dot_nn(hidden, w_down)) + b_down
    z2_normed, z2_inv = norm_stats(h1_pick + branch)
    cot = jnp.where(mask_pos.reshape(-1, 1) >= 0, grad_vals.reshape(-1, width).astype(f32), 0.0)
    dz2, g_ln2_gain, g_ln2_bias = norm_backward(cot, z2_normed, z2_inv, ln2_gain)
    dffn = low(dz2)
    g_b_down = jnp.sum(dffn.astype(f32), axis=0)
    dffn_both = pair(dffn)
    slope = cdf + pre * (jnp.exp(-0.5 * pre * pre) * (1.0 / math.sqrt(2.0 * math.pi)))
    dpre = low(dot_nt(dffn_both, w_down) * slope)
    dh1 = dz2 + both(dot_nt(dpre, w_in))
    gw_down_t = low(dot_tn(dffn_both, hidden))
    gw_in = low(dot_tn(h1_both, dpre))
    gb_in = low(jnp.sum(dpre.astype(f32), axis=0))
    dz1, g_ln1_gain, g_ln1_bias = norm_backward(dh1, h1_normed, h1_inv, ln1_gain)
    dattn = low(dz1)
    g_b_out = jnp.sum(dattn.astype(f32), axis=0)
    g_w_out = dot_tn(ctx_pick, dattn)
    dctx = low(dot_nt(dattn, w_out))

    part = width // n_tok
    ffn_blocks = jnp.concatenate(
        [
            gw_in.reshape(n_tok, part, hidden_cols),
            gw_down_t.reshape(n_tok, part, hidden_cols),
            jnp.pad(
                gb_in.reshape(n_tok, 1, hidden_cols // n_tok),
                ((0, 0), (0, 7), (0, hidden_cols - hidden_cols // n_tok)),
            ),
        ],
        axis=1,
    )
    s_ffn = halve_over(ffn_blocks, "tok")

    backs = []
    for s in range(seq_count):
        rows = lambda value: seq_rows(value, s, seq_len)
        picks = lambda value: seq_rows(value, s, slots)
        _, probs, _, words, words_pick = firsts[s]
        backs.append(
            attend_back(
                words, words_pick, picks(q_pick), rows(k), rows(v), picks(dctx), probs, pos_query, pos_key
            )
        )
    dq = join([back[0] for back in backs])
    dk = join([back[1] for back in backs])
    dv = join([back[2] for back in backs])
    dpos_key = dot_tn(expand, sum(back[3].astype(f32) for back in backs).astype(bf16))
    dpos_query = dot_tn(expand, sum(back[4].astype(f32) for back in backs).astype(bf16))
    sparse = dz1 + dot_nt(dq, w_query)
    sparse_up = low(sparse)
    sparse_lo = low(sparse - sparse_up.astype(f32))
    grad_tokens = (
        dot_tn(pick, sparse_up) + dot_tn(pick, sparse_lo) + dot_nt(dk, w_key) + dot_nt(dv, w_value)
    )
    g_w_query = dot_tn(low(x_pick), dq) + dot_tn(rel_table, low(dpos_query))
    g_w_key = dot_tn(tokens, dk) + dot_tn(rel_table, low(dpos_key))
    g_w_value = dot_tn(tokens, dv)
    g_rel = dot_nt(low(dpos_query), w_query) + dot_nt(low(dpos_key), w_key)
    total = lambda value: jnp.sum(value.astype(f32), axis=0)
    vectors = [
        total(dq) + total(dpos_query),
        total(dk) + total(dpos_key),
        total(dv),
        g_b_out, g_ln1_gain, g_ln1_bias, g_b_down, g_ln2_gain, g_ln2_bias,
    ]
    n_all = n_tok * n_ffn
    own = width // n_all
    vec_blocks = jnp.stack([value.reshape(n_all, own) for value in vectors], axis=1)
    vec_blocks = vec_blocks.reshape(n_all, 1, len(vectors) * own)
    vec_blocks = jnp.pad(vec_blocks, ((0, 0), (0, 7), (0, width - len(vectors) * own)))
    all_blocks = jnp.concatenate(
        [low(value).reshape(n_all, own, width) for value in (g_w_query, g_w_key, g_w_value, g_w_out)]
        + [low(g_rel).reshape(n_all, table_rows // n_all, width), low(vec_blocks)],
        axis=1,
    )
    tok_first = all_blocks.reshape((n_tok, n_ffn) + all_blocks.shape[1:])
    s_tok = halve_over(tok_first, "tok")
    s_all = halve_over(s_tok, "ffn")

    ctx = join(
        [
            attend_full(
                firsts[s][3],
                seq_rows(q, s, seq_len),
                seq_rows(k, s, seq_len),
                seq_rows(v, s, seq_len),
                pos_key,
                firsts[s][2],
            )
            for s in range(seq_count)
        ]
    )
    normed, _ = norm_stats(tokens.astype(f32) + (dot_nn(ctx, w_out) + b_out))
    middle = normed * ln1_gain + ln1_bias
    mine = low(middle)
    theirs = swap(mine, "ffn", 1)

    def ffn_part(value):
        pre_act = dot_nn(value, w_in) + b_in
        return low(dot_nn(low(pre_act * normal_cdf(pre_act)), w_down))

    back = swap(ffn_part(theirs), "ffn", 1)
    branch_all = ffn_part(mine).astype(f32) + back.astype(f32) + b_down
    final, _ = norm_stats(middle + branch_all)
    output = low(final * ln2_gain + ln2_bias)

    wide = lambda value: value.astype(f32)
    s_vec = wide(s_all[4 * own + table_rows // n_all, : len(vectors) * own]).reshape(len(vectors), own)
    s_w = [wide(s_all[n * own : (n + 1) * own]) for n in range(4)]
    s_rel = wide(s_all[4 * own : 4 * own + table_rows // n_all])
    return (
        output,
        grad_tokens,
        s_w[0],
        s_w[1],
        s_w[2],
        s_w[3],
        s_vec[0],
        s_vec[1],
        s_vec[2],
        s_vec[3],
        s_rel,
        s_vec[4],
        s_vec[5],
        wide(s_ffn[:part]),
        wide(s_ffn[2 * part : 2 * part + 1, : hidden_cols // n_tok]),
        jnp.transpose(wide(s_ffn[part : 2 * part])),
        s_vec[6],
        s_vec[7],
        s_vec[8],
    )


def solution(mesh):
    every = ("tok", "ffn")
    placed = (
        P(every, None), P(every, None, None), P(every, None), P(every, None, None),
        P(), P(), P(), P(), P(), P(), P(), P(), P(), P(), P(),
        P(None, "ffn"), P("ffn"), P("ffn", None), P(), P(), P(),
    )
    given = (
        P(every, None), P(every, None),
        P(every, None), P(every, None), P(every, None), P(every, None),
        P(every), P(every), P(every), P(every),
        P(every, None), P(every), P(every),
        P("tok", "ffn"), P("ffn", "tok"), P("ffn", "tok"),
        P(every), P(every), P(every),
    )
    return jax.shard_map(local, mesh=mesh, in_specs=placed, out_specs=given, check_vma=False)
```

time: 2040 us -> 340 us (0.17)
  matrix products: 1100 us -> 61.6 us
  waiting for transfers between devices: 608 us -> 64.4 us
  local copies, waits for them, and re-layouts: 200 us -> 37.6 us
  Pallas kernels: 0 us -> 123 us
  blocking collectives: 71 us -> 0 us
    dot_general x104 -> x33, matrix products: 1090 us -> 61.6 us  [the longest x13 33.4 us: dot_nn(): lax.dot_general(first_op, second_op, (((1,), (0,)), ((), ())), preferred_...]
    unnamed x14 -> x0, waiting for transfers between devices: 313 us -> none
    reduce_scatter x6 -> x0, waiting for transfers between devices: 237 us -> none  [the longest x1 79.5 us: local(): lax.psum_scatter(gw_in, 'tok', scatter_dimension=0, tiled=True)]
    pallas_call x0 -> x3, Pallas kernels: none -> 123 us  [the longest x1 62.8 us: attend_full(): pl.pallas_call(full_kernel, grid=(pairs,), in_specs=[pl.BlockSpec((seq, L...]
    reshape x5 -> x1, local copies, waits for them, and re-layouts: 71.8 us -> 0.08 us  [local(): gb_in.reshape(n_tok, 1, hidden_cols // n_tok)]
    unnamed x2 -> x0, blocking collectives: 71 us -> none
    ppermute x0 -> x15, waiting for transfers between devices: none -> 64.4 us  [swap(): return lax.ppermute(values, axis, [(n, n ^ bit) for n in range(size)])]
    all_gather x2 -> x0, waiting for transfers between devices: 57.3 us -> none  [the longest x1 30 us: local(): shard_rows = lax.all_gather(middle_low, 'ffn', axis=0, tiled=True)]
  transfers between devices with their start and end apart: 11 -> 15, of which waited for: 10 -> 7; matrix products, arithmetic and copies ran while one was open for 5% -> 27% of each run, Pallas kernels for 0% -> 27%
where the time goes in v1:
time: 340 us; the launch traced here: 335 us
  Pallas kernels  123 us (36%)
  waiting for transfers between devices  64.4 us (19%)
  matrix products  61.6 us (18%)
  local copies, waits for them, and re-layouts  37.6 us (11%)
  other arithmetic  24.4 us (7%)
  starting transfers between devices  21.2 us (6%)
    ppermute x15, waiting for transfers between devices, swap(): return lax.ppermute(values, axis, [(n, n ^ bit) for n in range(size)])  64.4 us
    pallas_call x1, Pallas kernels, attend_full(): pl.pallas_call(full_kernel, grid=(pairs,), in_specs=[pl.BlockSpec((seq, L...  62.8 us
    pallas_call x1, Pallas kernels, attend_picked(): pl.pallas_call(picked_kernel, grid=(pairs,), in_specs=[whole(seq, seq), w...  33.6 us
    dot_general x13, matrix products, dot_nn(): lax.dot_general(first_op, second_op, (((1,), (0,)), ((), ())), preferred_...  33.4 us
    pallas_call x1, Pallas kernels, attend_back(): pl.pallas_call(back_kernel, grid=(pairs,), in_specs=[whole(seq, LANES), w...  27 us
    ppermute x15, starting transfers between devices, swap(): return lax.ppermute(values, axis, [(n, n ^ bit) for n in range(size)])  21.2 us
    dot_general x12, matrix products, dot_tn(): lax.dot_general(first_op, second_op, (((0,), (0,)), ((), ())), preferred_...  18.2 us
    unnamed x212, local copies, waits for them, and re-layouts  17.1 us
  transfers between devices with their start and end apart: 15, of which 7 were waited for; matrix products, arithmetic and copies ran while one was open for 27% of the time, Pallas kernels for 27%

profile of v1, /device:TPU:0, one launch (start us, length us, event | category | flops | bytes accessed | tf_op | source)
XLA Modules:
  0.0 334.8 jit_solution(15638377045702069124)
XLA Ops:
  0.7 3.3 add_convert_fusion.7.q_ref
  4.8 4.7 %fusion.6.pk_ref = bf16[1024,768]{1,0:T(8,128)(2,1)} fusion(bf16[1024,512]{1,0:T(8,128)(2,1)} %constant.203.clone, bf16[512,768]{1,0:T(8,128)(2,1)} %param.34, bf16[768,768]{1,0:T(8,128)(2,1)} %param.27, f32[768]{0:T(1024)S(1)} %copy-done.90), kind=kOutput, calls=%fused_computation.42 | convolution fusion | flops 1410859008 | bytes 4590592 | tf_op jit(solution)/shard_map/dot_general | solution.py:21
  9.5 4.7 %fusion.7.pq_ref = bf16[1024,768]{1,0:T(8,128)(2,1)} fusion(bf16[1024,512]{1,0:T(8,128)(2,1)} %constant.203.clone, bf16[512,768]{1,0:T(8,128)(2,1)} %param.34, bf16[768,768]{1,0:T(8,128)(2,1)} %param.26, f32[768]{0:T(1024)S(1)} %copy-done.91), kind=kOutput, calls=%fused_computation.43 | convolution fusion | flops 1410859008 | bytes 4590592 | tf_op jit(solution)/shard_map/dot_general | solution.py:21
  14.3 1.6 fusion.38
  15.9 1.5 convolution_convert_fusion.11.qc_ref
  19.2 33.6 %attend_picked.1 = (bf16[80,768]{1,0:T(8,128)(2,1)S(1)}, bf16[12,80,512]{2,1,0:T(8,128)(2,1)S(1)}, bf16[12,512,1024]{2,1,0:T(8,128)(2,1)}, s32[512,128]{1,0:T(8,128)S(1)}, s32[80,128]{1,0:T(8,128)S(1)}) custom-call(s32[512,512]{1,0:T(8,128)S(1)} %bitcast.197, bf16[80,512]{1,0:T(8,128)(2,1)S(1)} %fusion.39.pick_ref, ...), custom_call_target="tpu_custom_call" | custom-call | tf_op jit(solution)/shard_map/attend_picked/pallas_call | solution.py:210
  54.6 3.0 collective-permute-start.2
  57.6 62.8 %attend_full.1 = bf16[512,768]{1,0:T(8,128)(2,1)S(1)} custom-call(s32[512,128]{1,0:T(8,128)S(1)} %get-tuple-element.29.word_ref, bf16[512,768]{1,0:T(8,128)(2,1)S(1)} %copy-done.6, bf16[512,768]{1,0:T(8,128)(2,1)S(1)} %add_convert_fusion.6.k_ref, bf16[512,768]{1,0:T(8,128)(2,1)S(1)} %add_convert_fusion.5.v_ref, bf16[1024,768]{1,0:T(8,128)(2,1)S(1)} %copy-done.1, ...), custom_call_target="tpu_custom_call" | custom-call | tf_op jit(solution)/shard_map/attend_full/pallas_call | solution.py:286
  122.0 1.6 multiply_convert_fusion.2
  124.7 4.5 %collective-permute-done.3 = bf16[80,768]{1,0:T(8,128)(2,1)S(1)} collective-permute-done((bf16[80,768]{1,0:T(8,128)(2,1)S(1)}, bf16[80,768]{1,0:T(8,128)(2,1)S(1)}, u32[]{:S(2)}, u32[]{:S(2)}) %collective-permute-start.3) | collective-permute-done | bytes 122912 | tf_op jit(solution)/shard_map/ppermute | solution.py:424
  130.5 1.4 fusion.67
  132.4 1.2 fusion.10
  133.7 1.6 collective-permute-start
  135.2 1.4 stack_reshape.34
  136.6 1.4 stack_reshape.35
  138.0 1.4 stack_reshape.36
  139.3 3.6 %fusion.75 = (bf16[1536]{0:T(1024)(128)(2,1)}, bf16[160,1536]{1,0:T(8,128)(2,1)S(1)}) fusion(f32[160,1536]{1,0:T(8,128)} %get-tuple-element.76, bf16[1536,768]{1,0:T(8,128)(2,1)} %param.39, bf16[80,768]{1,0:T(8,128)(2,1)} %collective-permute-done.4, bf16[80,768]{1,0:T(8,128)(2,1)} %get-tuple-element.48), kind=kOutput, calls=%fused_computation.202 | convolution fusion | flops 380680704 | bytes 4082688 | tf_op jit(solution)/shard_map/dot_general | solution.py:27
  145.9 1.6 copy_dynamic-update-slice_fusion.1
  148.4 1.9 concatenate.43
  150.3 2.0 convolution_convert_fusion
  152.3 1.6 copy_dynamic-update-slice_fusion
  153.9 1.0 copy_dynamic-update-slice_fusion.2
  155.0 3.5 %dynamic-slice_bitcast_fusion.1 = bf16[8,104,1536]{2,1,0:T(8,128)(2,1)} fusion(bf16[8,2,104,1536]{3,2,0,1:T(8,128)(2,1)} %copy_dynamic-update-slice_fusion.2, s32[]{:T(128)S(6)} %select_n.106), kind=kLoop, calls=%fused_computation.17 | loop fusion | bytes 5111812 | tf_op jit(solution)/shard_map/jit(dynamic_index_in_dim)/squeeze | solution.py:434
  158.7 1.4 multiply_reduce_fusion.2
  160.8 1.5 convolution_convert_fusion.4
  162.3 27.0 %attend_back.1 = (bf16[80,768]{1,0:T(8,128)(2,1)S(1)}, bf16[512,768]{1,0:T(8,128)(2,1)S(1)}, bf16[512,768]{1,0:T(8,128)(2,1)S(1)}, bf16[1024,768]{1,0:T(8,128)(2,1)}, bf16[1024,768]{1,0:T(8,128)(2,1)}) custom-call(s32[512,128]{1,0:T(8,128)S(1)} %copy-done.10, s32[80,128]{1,0:T(8,128)S(1)} %get-tuple-element.32.wordc_ref, ...), custom_call_target="tpu_custom_call" | custom-call | tf_op jit(solution)/shard_map/attend_back/pallas_call | solution.py:378
  189.4 2.3 fusion.79
  191.8 1.9 convolution_convert_fusion.5
  193.7 1.3 reduce.3
  195.0 2.8 fusion.73
  199.6 1.2 constant_dynamic-update-slice_fusion.14
  201.5 2.0 fusion.74
  204.0 2.7 add_convert_fusion
  206.8 1.1 constant_dynamic-update-slice_fusion.13
  208.4 2.5 constant_dynamic-update-slice_fusion.12
  210.9 1.1 constant_dynamic-update-slice_fusion.11
  216.9 3.7 %dynamic-slice_bitcast_fusion = bf16[8,2,120,768]{3,2,1,0:T(8,128)(2,1)} fusion(bf16[8,2,2,120,768]{4,3,2,1,0:T(8,128)(2,1)} %constant_dynamic-update-slice_fusion.9, s32[]{:T(128)S(6)} %select_n.106), kind=kLoop, calls=%fused_computation.12 | loop fusion | bytes 5898244 | tf_op jit(solution)/shard_map/jit(dynamic_index_in_dim)/squeeze | solution.py:434
  223.5 2.4 fusion.1
  226.0 1.2 dynamic-slice_bitcast_fusion.3
  227.2 1.5 collective-permute-start.12
  228.9 2.0 add_add_fusion
  230.9 5.8 %convolution_convert_fusion.6 = bf16[512,768]{1,0:T(8,128)(2,1)} fusion(bf16[1536,768]{1,0:T(8,128)(2,1)} %param.39, bf16[512,768]{1,0:T(8,128)(2,1)} %collective-permute-done, bf16[768,1536]{1,0:T(8,128)(2,1)S(1)} %copy-done, f32[1536]{0:T(1024)S(1)} %copy-done.67), kind=kOutput, calls=%fused_computation.48 | convolution fusion | flops 2421030912 | bytes 6297600 | tf_op jit(solution)/shard_map/dot_general | solution.py:21
  236.7 1.5 collective-permute-start.1
  238.2 3.5 %fusion = bf16[8,2,120,768]{3,2,1,0:T(8,128)(2,1)S(1)} fusion(bf16[8,2,120,768]{3,2,1,0:T(8,128)(2,1)} %collective-permute-done.6, bf16[8,2,2,120,768]{4,3,2,1,0:T(8,128)(2,1)} %constant_dynamic-update-slice_fusion.9, s32[]{:T(128)S(6)} %select_n.105), kind=kLoop, calls=%fused_computation.1 | loop fusion | flops 5898240 | bytes 8847364 | tf_op jit(solution)/shard_map/convert_element_type | solution.py:436
  241.7 1.2 dynamic-slice_bitcast_fusion.2
  242.9 1.6 collective-permute-start.7
  244.5 13.9 %collective-permute-done.12 = bf16[4,104,1536]{2,1,0:T(8,128)(2,1)} collective-permute-done((bf16[4,104,1536]{2,1,0:T(8,128)(2,1)}, bf16[4,104,1536]{2,1,0:T(8,128)(2,1)}, u32[]{:S(2)}, u32[]{:S(2)}) %collective-permute-start.12) | collective-permute-done | bytes 1277984 | tf_op jit(solution)/shard_map/ppermute | solution.py:424
  258.4 1.6 fusion.3
  260.0 1.1 copy-done.24
  261.2 1.7 collective-permute-start.13
  262.9 6.9 %fusion.71 = (f32[512]{0:T(512)S(1)}, f32[512,768]{1,0:T(8,128)}) fusion(f32[768]{0:T(1024)S(1)} %copy-done.84, bf16[512,768]{1,0:T(8,128)(2,1)} %collective-permute-done.1, bf16[1536,768]{1,0:T(8,128)(2,1)} %param.39, bf16[768,1536]{1,0:T(8,128)(2,1)S(1)} %copy-done, f32[1536]{0:T(1024)S(1)} %copy-done.67, f32[768]{0:T(1024)S(1)} %copy-done.56, ...), kind=kOutput, calls=%fused_computation.198 | convolution fusion | flops 2426928640 | bytes 8672256 | tf_op jit(solution)/shard_map/dot_general | solution.py:21
  269.7 1.9 multiply_reduce_fusion
  271.6 4.5 %collective-permute-done.13 = bf16[2,104,1536]{2,1,0:T(8,128)(2,1)} collective-permute-done((bf16[2,104,1536]{2,1,0:T(8,128)(2,1)S(1)}, bf16[2,104,1536]{2,1,0:T(8,128)(2,1)}, u32[]{:S(2)}, u32[]{:S(2)}) %collective-permute-start.13) | collective-permute-done | bytes 639008 | tf_op jit(solution)/shard_map/ppermute | solution.py:424
  276.1 1.4 fusion.9
  277.6 2.7 collective-permute-start.14
  280.3 8.9 %collective-permute-done.7 = bf16[4,2,120,768]{3,2,1,0:T(8,128)(2,1)} collective-permute-done((bf16[4,2,120,768]{3,2,1,0:T(8,128)(2,1)}, bf16[4,2,120,768]{3,2,1,0:T(8,128)(2,1)}, u32[]{:S(2)}, u32[]{:S(2)}) %collective-permute-start.7) | collective-permute-done | bytes 1474592 | tf_op jit(solution)/shard_map/ppermute | solution.py:424
  289.2 1.8 fusion.2
  291.1 1.7 collective-permute-start.8
  292.8 1.2 add_convert_fusion.2
  294.1 14.8 %collective-permute-done.8 = bf16[2,2,120,768]{3,2,1,0:T(8,128)(2,1)S(1)} collective-permute-done((bf16[2,2,120,768]{3,2,1,0:T(8,128)(2,1)S(1)}, bf16[2,2,120,768]{3,2,1,0:T(8,128)(2,1)S(1)}, u32[]{:S(2)}, u32[]{:S(2)}) %collective-permute-start.8) | collective-permute-done | bytes 737312 | tf_op jit(solution)/shard_map/ppermute | solution.py:424
  309.1 2.7 collective-permute-start.9
  312.6 14.2 %collective-permute-done.9 = bf16[1,2,120,768]{3,2,1,0:T(8,128)(2,1)S(1)} collective-permute-done((bf16[1,2,120,768]{3,2,1,0:T(8,128)(2,1)S(1)}, bf16[1,2,120,768]{3,2,1,0:T(8,128)(2,1)S(1)}, u32[]{:S(2)}, u32[]{:S(2)}) %collective-permute-start.9) | collective-permute-done | bytes 368672 | tf_op jit(solution)/shard_map/ppermute | solution.py:424
  327.0 1.6 collective-permute-start.10
  329.0 3.5 %collective-permute-done.10 = bf16[1,120,768]{2,1,0:T(8,128)(2,1)S(1)} collective-permute-done((bf16[1,120,768]{2,1,0:T(8,128)(2,1)S(1)}, bf16[1,120,768]{2,1,0:T(8,128)(2,1)S(1)}, u32[]{:S(2)}, u32[]{:S(2)}) %collective-permute-start.10) | collective-permute-done | bytes 184352 | tf_op jit(solution)/shard_map/ppermute | solution.py:424
  (289 shorter events, 28.8 us)
Async XLA Ops:
  0.7 121.0 %copy-start = (bf16[768,1536]{1,0:T(8,128)(2,1)S(1)}, bf16[768,1536]{1,0:T(8,128)(2,1)}, u32[]{:S(2)}) copy-start(bf16[768,1536]{1,0:T(8,128)(2,1)} %param.37) | copy-start | bytes 7077892
  4.8 4.7 %copy-start.91 = (f32[768]{0:T(1024)S(1)}, f32[768]{0:T(1024)}, u32[]{:S(2)}) copy-start(f32[768]{0:T(1024)} %param.30) | copy-start | bytes 9220
  9.5 4.7 %copy-start.93 = (s32[1,80]{1,0:T(1,128)S(1)}, s32[1,80]{1,0:T(1,128)}, u32[]{:S(2)}) copy-start(s32[1,80]{1,0:T(1,128)} %param.24) | copy-start | bytes 964
  14.2 4.0 %copy-start.64 = (s32[80]{0:T(128)}, s32[80]{0:T(128)S(1)}, u32[]{:S(2)}) copy-start(s32[80]{0:T(128)S(1)} %fusion.53) | copy-start | bytes 964
  15.9 37.9 %copy-start.36 = (f32[80,768]{1,0:T(8,128)}, f32[80,768]{1,0:T(8,128)S(1)}, u32[]{:S(2)}) copy-start(f32[80,768]{1,0:T(8,128)S(1)} %fusion.38) | copy-start | bytes 737284
  18.3 39.4 %copy-start.2 = (bf16[512,768]{1,0:T(8,128)(2,1)}, bf16[512,768]{1,0:T(8,128)(2,1)S(1)}, u32[]{:S(2)}) copy-start(bf16[512,768]{1,0:T(8,128)(2,1)S(1)} %add_convert_fusion.5.v_ref) | copy-start | bytes 2359300
  19.1 34.6 %copy-start.25 = (bf16[768,768]{1,0:T(8,128)(2,1)S(1)}, bf16[768,768]{1,0:T(8,128)(2,1)}, u32[]{:S(2)}) copy-start(bf16[768,768]{1,0:T(8,128)(2,1)} %param.29) | copy-start | bytes 3538948
  19.2 34.6 %copy-start.82 = (f32[768]{0:T(1024)S(1)}, f32[768]{0:T(1024)}, u32[]{:S(2)}) copy-start(f32[768]{0:T(1024)} %param.33) | copy-start | bytes 9220
  53.8 66.7 %copy-start.9 = (s32[512,128]{1,0:T(8,128)}, s32[512,128]{1,0:T(8,128)S(1)}, u32[]{:S(2)}) copy-start(s32[512,128]{1,0:T(8,128)S(1)} %get-tuple-element.29.word_ref) | copy-start | bytes 786436
  53.8 3.9 %copy-start.6 = (bf16[512,768]{1,0:T(8,128)(2,1)S(1)}, bf16[512,768]{1,0:T(8,128)(2,1)}, u32[]{:S(2)}) copy-start(bf16[512,768]{1,0:T(8,128)(2,1)} %add_convert_fusion.7.q_ref) | copy-start | bytes 2359300
  54.2 75.0 %copy-start.18 = (f32[80,768]{1,0:T(8,128)}, f32[80,768]{1,0:T(8,128)S(1)}, u32[]{:S(2)}) copy-start(f32[80,768]{1,0:T(8,128)S(1)} %get-tuple-element.74) | copy-start | bytes 737284
  54.3 75.0 %copy-start.62 = (f32[80]{0:T(128)}, f32[80]{0:T(128)S(1)}, u32[]{:S(2)}) copy-start(f32[80]{0:T(128)S(1)} %broadcast_multiply_fusion.7) | copy-start | bytes 964
  54.5 74.7 %copy-start.72 = (f32[80]{0:T(128)}, f32[80]{0:T(128)S(1)}, u32[]{:S(2)}) copy-start(f32[80]{0:T(128)S(1)} %add_rsqrt_fusion.3) | copy-start | bytes 964
  54.6 67.1 %collective-permute-start.2 = (bf16[80,768]{1,0:T(8,128)(2,1)S(1)}, bf16[80,768]{1,0:T(8,128)(2,1)S(1)}, u32[]{:S(2)}, u32[]{:S(2)}) collective-permute-start(bf16[80,768]{1,0:T(8,128)(2,1)S(1)} %fusion.35), channel_id=1, source_target_pairs={{0,1},{1,0},{2,3},{3,2},{4,5},{5,4},{6,7},{7,6},{8,9},{9,8},{10,11... | collective-permute-start | bytes 368648 | tf_op jit(solution)/shard_map/ppermute | solution.py:424
  121.3 11.1 %copy-start.20 = (f32[512,768]{1,0:T(8,128)}, f32[512,768]{1,0:T(8,128)S(1)}, u32[]{:S(2)}) copy-start(f32[512,768]{1,0:T(8,128)S(1)} %get-tuple-element.70) | copy-start | bytes 4718596
  121.3 11.1 %copy-start.60 = (f32[512]{0:T(512)}, f32[512]{0:T(512)S(1)}, u32[]{:S(2)}) copy-start(f32[512]{0:T(512)S(1)} %broadcast_multiply_fusion.1) | copy-start | bytes 6148
  121.7 10.8 %copy-start.70 = (f32[512]{0:T(512)}, f32[512]{0:T(512)S(1)}, u32[]{:S(2)}) copy-start(f32[512]{0:T(512)S(1)} %add_rsqrt_fusion.1) | copy-start | bytes 6148
  123.6 5.7 %copy-start.83 = (f32[768]{0:T(1024)S(1)}, f32[768]{0:T(1024)}, u32[]{:S(2)}) copy-start(f32[768]{0:T(1024)} %param.40) | copy-start | bytes 9220
  123.6 6.1 %copy-start.44 = (bf16[1,80,768]{2,1,0:T(8,128)(2,1)S(1)}, bf16[1,80,768]{2,1,0:T(8,128)(2,1)}, u32[]{:S(2)}) copy-start(bf16[1,80,768]{2,1,0:T(8,128)(2,1)} %param.25) | copy-start | bytes 368644
  123.6 6.1 %copy-start.53 = (f32[768]{0:T(1024)S(1)}, f32[768]{0:T(1024)}, u32[]{:S(2)}) copy-start(f32[768]{0:T(1024)} %param.41) | copy-start | bytes 9220
  124.4 4.9 %collective-permute-start.3 = (bf16[80,768]{1,0:T(8,128)(2,1)S(1)}, bf16[80,768]{1,0:T(8,128)(2,1)S(1)}, u32[]{:S(2)}, u32[]{:S(2)}) collective-permute-start(bf16[80,768]{1,0:T(8,128)(2,1)S(1)} %slice.141), channel_id=1, source_target_pairs={{0,1},{1,0},{2,3},{3,2},{4,5},{5,4},{6,7},{7,6},{8,9},{9,8},{10,11... | collective-permute-start | bytes 368648 | tf_op jit(solution)/shard_map/ppermute | solution.py:424
  124.7 8.9 %copy-start.74 = (pred[80]{0:T(512)(128)(4,1)}, pred[80]{0:T(512)(128)(4,1)S(1)}, u32[]{:S(2)}) copy-start(pred[80]{0:T(512)(128)(4,1)S(1)} %compare_bitcast_fusion) | copy-start | bytes 244
  129.5 4.2 %copy-start.68 = (f32[80]{0:T(128)}, f32[80]{0:T(128)S(1)}, u32[]{:S(2)}) copy-start(f32[80]{0:T(128)S(1)} %broadcast_multiply_fusion.6) | copy-start | bytes 964
  129.7 3.9 %copy-start.76 = (f32[80]{0:T(128)}, f32[80]{0:T(128)S(1)}, u32[]{:S(2)}) copy-start(f32[80]{0:T(128)S(1)} %add_rsqrt_fusion.2) | copy-start | bytes 964
  130.5 4.7 %copy-start.78 = (f32[80]{0:T(128)}, f32[80]{0:T(128)S(1)}, u32[]{:S(2)}) copy-start(f32[80]{0:T(128)S(1)} %get-tuple-element.83) | copy-start | bytes 964
  130.5 4.7 %copy-start.80 = (f32[80]{0:T(128)}, f32[80]{0:T(128)S(1)}, u32[]{:S(2)}) copy-start(f32[80]{0:T(128)S(1)} %get-tuple-element.84) | copy-start | bytes 964
  131.9 7.4 %collective-permute-start.4 = (bf16[80,768]{1,0:T(8,128)(2,1)}, bf16[80,768]{1,0:T(8,128)(2,1)}, u32[]{:S(2)}, u32[]{:S(2)}) collective-permute-start(bf16[80,768]{1,0:T(8,128)(2,1)} %get-tuple-element.48), channel_id=1, source_target_pairs={{0,1},{1,0},{2,3},{3,2},{4,5},{5,4},{6,7},{7,6},{8,9},{9,8},{10,11... | collective-permute-start | bytes 368648 | tf_op jit(solution)/shard_map/ppermute | solution.py:424
  133.7 97.2 %collective-permute-start = (bf16[512,768]{1,0:T(8,128)(2,1)}, bf16[512,768]{1,0:T(8,128)(2,1)}, u32[]{:S(2)}, u32[]{:S(2)}) collective-permute-start(bf16[512,768]{1,0:T(8,128)(2,1)} %fusion.10), channel_id=1, source_target_pairs={{0,1},{1,0},{2,3},{3,2},{4,5},{5,4},{6,7},{7,6},{8,9},{9,8},{10,11... | collective-permute-start | bytes 2359304 | tf_op jit(solution)/shard_map/ppermute | solution.py:424
  144.6 13.9 %collective-permute-start.5 = (bf16[80,768]{1,0:T(8,128)(2,1)}, bf16[80,768]{1,0:T(8,128)(2,1)}, u32[]{:S(2)}, u32[]{:S(2)}) collective-permute-start(bf16[80,768]{1,0:T(8,128)(2,1)} %slice.143), channel_id=1, source_target_pairs={{0,1},{1,0},{2,3},{3,2},{4,5},{5,4},{6,7},{7,6},{8,9},{9,8},{10,11... | collective-permute-start | bytes 368648 | tf_op jit(solution)/shard_map/ppermute | solution.py:424
  154.9 3.7 %copy-start.45 = (bf16[1,80,768]{2,1,0:T(8,128)(2,1)S(1)}, bf16[1,80,768]{2,1,0:T(8,128)(2,1)}, u32[]{:S(2)}) copy-start(bf16[1,80,768]{2,1,0:T(8,128)(2,1)} %param.25) | copy-start | bytes 368644
  154.9 3.7 %copy-start.47 = (bf16[160,768]{1,0:T(8,128)(2,1)S(1)}, bf16[160,768]{1,0:T(8,128)(2,1)}, u32[]{:S(2)}) copy-start(bf16[160,768]{1,0:T(8,128)(2,1)} %copy-done.46) | copy-start | bytes 737284
  154.9 3.7 %copy-start.52 = (f32[768]{0:T(1024)S(1)}, f32[768]{0:T(1024)}, u32[]{:S(2)}) copy-start(f32[768]{0:T(1024)} %param.35) | copy-start | bytes 9220
  154.9 3.7 %copy-start.54 = (f32[768]{0:T(1024)S(1)}, f32[768]{0:T(1024)}, u32[]{:S(2)}) copy-start(f32[768]{0:T(1024)} %param.41) | copy-start | bytes 9220
  154.9 3.7 %copy-start.63 = (f32[80]{0:T(128)S(1)}, f32[80]{0:T(128)}, u32[]{:S(2)}) copy-start(f32[80]{0:T(128)} %copy-done.62) | copy-start | bytes 964
  154.9 3.7 %copy-start.69 = (f32[80]{0:T(128)S(1)}, f32[80]{0:T(128)}, u32[]{:S(2)}) copy-start(f32[80]{0:T(128)} %copy-done.68) | copy-start | bytes 964
  154.9 3.7 %copy-start.73 = (f32[80]{0:T(128)S(1)}, f32[80]{0:T(128)}, u32[]{:S(2)}) copy-start(f32[80]{0:T(128)} %copy-done.72) | copy-start | bytes 964
  154.9 3.7 %copy-start.75 = (pred[80]{0:T(512)(128)(4,1)S(1)}, pred[80]{0:T(512)(128)(4,1)}, u32[]{:S(2)}) copy-start(pred[80]{0:T(512)(128)(4,1)} %copy-done.74) | copy-start | bytes 244
  155.0 3.7 %copy-start.77 = (f32[80]{0:T(128)S(1)}, f32[80]{0:T(128)}, u32[]{:S(2)}) copy-start(f32[80]{0:T(128)} %copy-done.76) | copy-start | bytes 964
  155.0 3.7 %copy-start.79 = (f32[80]{0:T(128)S(1)}, f32[80]{0:T(128)}, u32[]{:S(2)}) copy-start(f32[80]{0:T(128)} %copy-done.78) | copy-start | bytes 964
  155.0 3.7 %copy-start.81 = (f32[80]{0:T(128)S(1)}, f32[80]{0:T(128)}, u32[]{:S(2)}) copy-start(f32[80]{0:T(128)} %copy-done.80) | copy-start | bytes 964
  158.5 65.0 %collective-permute-start.11 = (bf16[8,104,1536]{2,1,0:T(8,128)(2,1)}, bf16[8,104,1536]{2,1,0:T(8,128)(2,1)}, u32[]{:S(2)}, u32[]{:S(2)}) collective-permute-start(bf16[8,104,1536]{2,1,0:T(8,128)(2,1)} %dynamic-slice_bitcast_fusion.1), channel_id=1, source_target_pairs={{0,2},{2,0},{4,6},{6,4},{8,10},{10,8},{12,14},{14,12},{16,18},{18,... | collective-permute-start | bytes 7667720 | tf_op jit(solution)/shard_map/ppermute | solution.py:424
  162.3 27.1 %copy-start.34 = (bf16[512,768]{1,0:T(8,128)(2,1)S(1)}, bf16[512,768]{1,0:T(8,128)(2,1)}, u32[]{:S(2)}) copy-start(bf16[512,768]{1,0:T(8,128)(2,1)} %param.22) | copy-start | bytes 2359300
  214.3 9.2 %slice-start = ((s8[5111808]{0:T(1024)(128)(4,1)}), s8[4194304]{0:T(1024)(128)(4,1)S(1)}, s32[]{:S(2)}) async-start(s8[5111808]{0:T(1024)(128)(4,1)} %bitcast.200), calls=%async_computation | async-start | bytes 8388608
  216.9 4.1 %copy-start.30 = (f32[80,768]{1,0:T(8,128)S(1)}, f32[80,768]{1,0:T(8,128)}, u32[]{:S(2)}) copy-start(f32[80,768]{1,0:T(8,128)} %copy-done.29) | copy-start | bytes 737284
  216.9 6.6 %slice-start.1 = ((s8[5111808]{0:T(1024)(128)(4,1)}), s8[917504]{0:T(1024)(128)(4,1)S(1)}, s32[]{:S(2)}) async-start(s8[5111808]{0:T(1024)(128)(4,1)} %bitcast.200), calls=%async_computation.1 | async-start | bytes 1835008
  220.6 17.6 %collective-permute-start.6 = (bf16[8,2,120,768]{3,2,1,0:T(8,128)(2,1)}, bf16[8,2,120,768]{3,2,1,0:T(8,128)(2,1)}, u32[]{:S(2)}, u32[]{:S(2)}) collective-permute-start(bf16[8,2,120,768]{3,2,1,0:T(8,128)(2,1)} %dynamic-slice_bitcast_fusion), channel_id=1, source_target_pairs={{0,2},{2,0},{4,6},{6,4},{8,10},{10,8},{12,14},{14,12},{16,18},{18,... | collective-permute-start | bytes 8847368 | tf_op jit(solution)/shard_map/ppermute | solution.py:424
  226.0 4.9 %copy-start.16 = (bf16[8,104,1536]{2,1,0:T(8,128)(2,1)}, bf16[8,104,1536]{2,1,0:T(8,128)(2,1)S(1)}, u32[]{:S(2)}) copy-start(bf16[8,104,1536]{2,1,0:T(8,128)(2,1)S(1)} %fusion.1) | copy-start | bytes 7667716
  227.2 3.7 %copy-start.67 = (f32[1536]{0:T(1024)S(1)}, f32[1536]{0:T(1024)}, u32[]{:S(2)}) copy-start(f32[1536]{0:T(1024)} %param.38) | copy-start | bytes 18436
  227.2 31.2 %collective-permute-start.12 = (bf16[4,104,1536]{2,1,0:T(8,128)(2,1)}, bf16[4,104,1536]{2,1,0:T(8,128)(2,1)}, u32[]{:S(2)}, u32[]{:S(2)}) collective-permute-start(bf16[4,104,1536]{2,1,0:T(8,128)(2,1)} %dynamic-slice_bitcast_fusion.3), channel_id=1, source_target_pairs={{0,4},{2,6},{4,0},{6,2},{8,12},{10,14},{12,8},{14,10},{16,20},{18,... | collective-permute-start | bytes 3833864 | tf_op jit(solution)/shard_map/ppermute | solution.py:424
  236.7 26.1 %collective-permute-start.1 = (bf16[512,768]{1,0:T(8,128)(2,1)}, bf16[512,768]{1,0:T(8,128)(2,1)}, u32[]{:S(2)}, u32[]{:S(2)}) collective-permute-start(bf16[512,768]{1,0:T(8,128)(2,1)} %convolution_convert_fusion.6), channel_id=1, source_target_pairs={{0,1},{1,0},{2,3},{3,2},{4,5},{5,4},{6,7},{7,6},{8,9},{9,8},{10,11... | collective-permute-start | bytes 2359304 | tf_op jit(solution)/shard_map/ppermute | solution.py:424
  241.7 18.3 %copy-start.14 = (bf16[8,2,120,768]{3,2,1,0:T(8,128)(2,1)}, bf16[8,2,120,768]{3,2,1,0:T(8,128)(2,1)S(1)}, u32[]{:S(2)}) copy-start(bf16[8,2,120,768]{3,2,1,0:T(8,128)(2,1)S(1)} %fusion) | copy-start | bytes 8847364
  241.7 16.7 %copy-start.17 = (bf16[8,104,1536]{2,1,0:T(8,128)(2,1)S(1)}, bf16[8,104,1536]{2,1,0:T(8,128)(2,1)}, u32[]{:S(2)}) copy-start(bf16[8,104,1536]{2,1,0:T(8,128)(2,1)} %copy-done.16) | copy-start | bytes 7667716
  242.9 19.9 %copy-start.56 = (f32[768]{0:T(1024)S(1)}, f32[768]{0:T(1024)}, u32[]{:S(2)}) copy-start(f32[768]{0:T(1024)} %param.36) | copy-start | bytes 9220
  242.9 19.9 %copy-start.61 = (f32[512]{0:T(512)S(1)}, f32[512]{0:T(512)}, u32[]{:S(2)}) copy-start(f32[512]{0:T(512)} %copy-done.60) | copy-start | bytes 6148
  242.9 19.9 %copy-start.71 = (f32[512]{0:T(512)S(1)}, f32[512]{0:T(512)}, u32[]{:S(2)}) copy-start(f32[512]{0:T(512)} %copy-done.70) | copy-start | bytes 6148
  242.9 19.9 %copy-start.84 = (f32[768]{0:T(1024)S(1)}, f32[768]{0:T(1024)}, u32[]{:S(2)}) copy-start(f32[768]{0:T(1024)} %param.40) | copy-start | bytes 9220
  242.9 46.3 %collective-permute-start.7 = (bf16[4,2,120,768]{3,2,1,0:T(8,128)(2,1)}, bf16[4,2,120,768]{3,2,1,0:T(8,128)(2,1)}, u32[]{:S(2)}, u32[]{:S(2)}) collective-permute-start(bf16[4,2,120,768]{3,2,1,0:T(8,128)(2,1)} %dynamic-slice_bitcast_fusion.2), channel_id=1, source_target_pairs={{0,4},{2,6},{4,0},{6,2},{8,12},{10,14},{12,8},{14,10},{16,20},{18,... | collective-permute-start | bytes 4423688 | tf_op jit(solution)/shard_map/ppermute | solution.py:424
  261.2 14.9 %collective-permute-start.13 = (bf16[2,104,1536]{2,1,0:T(8,128)(2,1)S(1)}, bf16[2,104,1536]{2,1,0:T(8,128)(2,1)}, u32[]{:S(2)}, u32[]{:S(2)}) collective-permute-start(bf16[2,104,1536]{2,1,0:T(8,128)(2,1)S(1)} %dynamic-slice_bitcast_fusion.5), channel_id=1, source_target_pairs={{0,8},{2,10},{4,12},{6,14},{8,0},{10,2},{12,4},{14,6},{16,24},{18,... | collective-permute-start | bytes 1916936 | tf_op jit(solution)/shard_map/ppermute | solution.py:424
  269.7 19.4 %copy-start.15 = (bf16[8,2,120,768]{3,2,1,0:T(8,128)(2,1)S(1)}, bf16[8,2,120,768]{3,2,1,0:T(8,128)(2,1)}, u32[]{:S(2)}) copy-start(bf16[8,2,120,768]{3,2,1,0:T(8,128)(2,1)} %copy-done.14) | copy-start | bytes 8847364
  277.6 15.2 %copy-start.85 = (f32[768]{0:T(1024)S(1)}, f32[768]{0:T(1024)}, u32[]{:S(2)}) copy-start(f32[768]{0:T(1024)} %param.42) | copy-start | bytes 9220
  277.6 16.4 %collective-permute-start.14 = (bf16[1,104,1536]{2,1,0:T(8,128)(2,1)S(1)}, bf16[1,104,1536]{2,1,0:T(8,128)(2,1)S(1)}, u32[]{:S(2)}, u32[]{:S(2)}) collective-permute-start(bf16[1,104,1536]{2,1,0:T(8,128)(2,1)S(1)} %constant_dynamic-slice_fusion), channel_id=1, source_target_pairs={{0,16},{2,18},{4,20},{6,22},{8,24},{10,26},{12,28},{14,30},{16,0},... | collective-permute-start | bytes 958472 | tf_op jit(solution)/shard_map/ppermute | solution.py:424
  291.1 17.8 %collective-permute-start.8 = (bf16[2,2,120,768]{3,2,1,0:T(8,128)(2,1)S(1)}, bf16[2,2,120,768]{3,2,1,0:T(8,128)(2,1)S(1)}, u32[]{:S(2)}, u32[]{:S(2)}) collective-permute-start(bf16[2,2,120,768]{3,2,1,0:T(8,128)(2,1)S(1)} %dynamic-slice_bitcast_fusion.4), channel_id=1, source_target_pairs={{0,8},{2,10},{4,12},{6,14},{8,0},{10,2},{12,4},{14,6},{16,24},{18,... | collective-permute-start | bytes 2211848 | tf_op jit(solution)/shard_map/ppermute | solution.py:424
  309.1 17.7 %collective-permute-start.9 = (bf16[1,2,120,768]{3,2,1,0:T(8,128)(2,1)S(1)}, bf16[1,2,120,768]{3,2,1,0:T(8,128)(2,1)S(1)}, u32[]{:S(2)}, u32[]{:S(2)}) collective-permute-start(bf16[1,2,120,768]{3,2,1,0:T(8,128)(2,1)S(1)} %constant_dynamic-slice_fusion.1), channel_id=1, source_target_pairs={{0,16},{2,18},{4,20},{6,22},{8,24},{10,26},{12,28},{14,30},{16,0},... | collective-permute-start | bytes 1105928 | tf_op jit(solution)/shard_map/ppermute | solution.py:424
  327.0 5.6 %collective-permute-start.10 = (bf16[1,120,768]{2,1,0:T(8,128)(2,1)S(1)}, bf16[1,120,768]{2,1,0:T(8,128)(2,1)S(1)}, u32[]{:S(2)}, u32[]{:S(2)}) collective-permute-start(bf16[1,120,768]{2,1,0:T(8,128)(2,1)S(1)} %dynamic-slice_bitcast_fusion.6), channel_id=1, source_target_pairs={{0,1},{1,0},{2,3},{3,2},{4,5},{5,4},{6,7},{7,6},{8,9},{9,8},{10,11... | collective-permute-start | bytes 552968 | tf_op jit(solution)/shard_map/ppermute | solution.py:424
  (49 other events, 95.0 us)

commit v2 on v1

--- a/solution.py
+++ b/solution.py
@@ -1,3 +1,4 @@
+import functools
 import math
 
 import numpy as np
@@ -11,6 +12,7 @@
 
 HEAD = 64
 LANES = 128
+HALF = 64
 ROWS = 32
 norm_eps = 1e-07
 bf16 = jnp.bfloat16
@@ -57,30 +59,49 @@
     return (words == lane_iota(words.shape[0]) + c * LANES).astype(f32).astype(bf16)
 
 
-def shift_in_order(source, words_ref, base, emit):
-    seq = words_ref.shape[0]
+def id_bases(rel_ref, base):
+    seq = rel_ref.shape[0]
     chunks = seq // LANES
-    lane = lane_iota()
-    for g in range(chunks):
-        first = base[g]
-        for sub in range(LANES // ROWS):
-            start = g * LANES + sub * ROWS
-            rows = slice(start, start + ROWS)
-            place = lane + (seq - 1) - words_ref[rows, :] - first * LANES
-            index = place & (LANES - 1)
-            turned = []
-            for c in range(chunks + 2):
-                at = pl.multiple_of(jnp.minimum(first + c, 2 * chunks - 1) * LANES, LANES)
-                turned.append(
-                    jnp.take_along_axis(source[rows, pl.ds(at, LANES)], index, axis=1)
-                )
-            near = place < LANES
-            mid = place < 2 * LANES
-            for c in range(chunks):
-                value = jnp.where(
-                    near, turned[c], jnp.where(mid, turned[c + 1], turned[c + 2])
-                )
-                emit(rows, c, value)
+    last = chunks * 2 - 2
+    for g in range(seq // HALF):
+        for c in range(chunks):
+            block = rel_ref[g * HALF : (g + 1) * HALF, c * LANES : (c + 1) * LANES]
+            base[g * chunks + c] = jnp.minimum(jnp.min(block) // HALF, last)
+
+
+def both_alignments(table):
+    return jnp.concatenate([table, table[HALF:], table[:HALF]], axis=0)
+
+
+def longest(rows):
+    wide = rows.astype(f32)
+    return jnp.sqrt(jnp.max(jnp.sum(wide * wide, axis=1, keepdims=True)))
+
+
+def pack_heads(first, second, dest, top):
+    top = jnp.maximum(top, 1e-30)
+    scale = 32000.0 / top
+    upper = (first * scale).astype(jnp.int32)
+    lower = (second * scale).astype(jnp.int32)
+    dest[...] = upper * 65536 + lower
+    return top * (1.0 / 32000.0)
+
+
+def unpack_heads(words, step):
+    lower = lax.shift_right_arithmetic(lax.shift_left(words, 16), 16)
+    return words.astype(f32) * (step * (1.0 / 65536.0)), lower.astype(f32) * step
+
+
+def picked_words(source, rel_ref, base, rows, c):
+    chunks = rel_ref.shape[1] // LANES
+    first = base[(rows.start // HALF) * chunks + c]
+    place = rel_ref[rows, c * LANES : (c + 1) * LANES] - first * HALF
+    index = place & (LANES - 1)
+    at = pl.multiple_of((first % 2) * (chunks * LANES) + (first // 2) * LANES, LANES)
+    near = jnp.take_along_axis(source[rows, pl.ds(at, LANES)], index, axis=1)
+    at = pl.multiple_of(at + LANES, LANES)
+    far = jnp.take_along_axis(source[rows, pl.ds(at, LANES)], index, axis=1)
+    return jnp.where(place < LANES, near, far)
 
 
 def unshift_in_order(source, words_ref, base, dest):
@@ -120,188 +141,177 @@
         base[g] = (seq - 1 - top) // LANES
 
 
-def split_store(dest, rows, upper_at, lower_at, value):
-    upper = value.astype(bf16)
-    dest[rows, upper_at : upper_at + LANES] = upper
-    dest[rows, lower_at : lower_at + LANES] = (value - upper.astype(f32)).astype(bf16)
-
-
-def softmax_rows(scores):
+def softmax_weights(scores):
     factor = math.log2(math.e) / math.sqrt(3.0 * HEAD)
-    weights = jnp.exp2((scores - jnp.max(scores, axis=1, keepdims=True)) * factor)
-    return (weights * (1.0 / jnp.sum(weights, axis=1, keepdims=True))).astype(bf16)
+    top = jnp.max(functools.reduce(jnp.maximum, scores), axis=1, keepdims=True)
+    return [jnp.exp2((score - top) * factor) for score in scores]
+
+
+def head_lanes(a):
+    return (lane_iota() < HEAD) if a == 0 else (lane_iota() >= HEAD)
 
 
 def picked_kernel(
-    rel_ref, pick_ref, qc_ref, k_ref, v_ref, pk_ref, pq_ref,
-    ctx_ref, prob_ref, keyrow_ref, word_ref, wordc_ref,
-    left, right, crel, base,
+    pos_ref, rel_ref, qc_ref, k_ref, v_ref, pk_ref, pq_ref,
+    ctx_ref, prob_ref, key_ref, word_ref, wordc_ref,
+    packed, cpick, relc, keyc, base,
 ):
     seq = k_ref.shape[0]
     picks = qc_ref.shape[0]
     chunks = seq // LANES
-    at = [LANES + n * seq for n in range(4)]
 
     @pl.when(pl.program_id(0) == 0)
     def _():
         row = lax.broadcasted_iota(jnp.int32, (seq, seq), 0)
         col = lax.broadcasted_iota(jnp.int32, (seq, seq), 1)
-        side = pk_ref.shape[0] // 4
+        side = pk_ref.shape[0] // 2
         step = jnp.sum(jnp.where(col == row - 1, rel_ref[...] - side, 0), axis=1, keepdims=True)
         steps = jnp.broadcast_to(step.astype(f32), (seq, LANES)).astype(bf16)
-        words = dot_nn((col <= row).astype(f32).astype(bf16), steps).astype(jnp.int32)
-        word_ref[...] = words
-        group_bases(words, base)
+        word_ref[...] = dot_nn((col <= row).astype(f32).astype(bf16), steps).astype(jnp.int32)
+        id_bases(rel_ref, base)
+        for n in range(picks):
+            place = jnp.maximum(pos_ref[n], 0)
+            relc[n : n + 1, :] = rel_ref[pl.ds(place, 1), :]
+            wordc_ref[n : n + 1, :] = word_ref[pl.ds(place, 1), :]
+
+    zero = jnp.zeros((), bf16)
+    table = both_alignments(pq_ref[...])
+    keys = [dot_nt(jnp.where(head_lanes(a), k_ref[...], zero), table) for a in range(2)]
+    unit = pack_heads(keys[0], keys[1], packed, longest(k_ref[...]) * longest(pq_ref[...]))
+    for a in range(2):
+        cpick[a] = dot_nt(jnp.where(head_lanes(a), qc_ref[...], zero), pk_ref[...])
+    for g in range(chunks):
         for c in range(chunks):
-            member = member_chunk(words, c)
-            right[:, at[0] + c * LANES : at[0] + (c + 1) * LANES] = member
-            right[:, at[1] + c * LANES : at[1] + (c + 1) * LANES] = member
-        memberc = dot_nn(pick_ref[...], right[:, at[0] : at[1]])
-        left[:, at[2] : at[3]] = memberc.astype(bf16)
-        left[:, at[3] : at[3] + seq] = memberc.astype(bf16)
-        index = lax.broadcasted_iota(jnp.int32, (picks, seq), 1).astype(f32)
-        total = jnp.sum(memberc * index, axis=1, keepdims=True)
-        wordc_ref[...] = jnp.broadcast_to(total, (picks, LANES)).astype(jnp.int32)
-
-    lane = lane_iota()
-    zero = jnp.zeros((), bf16)
+            parts = []
+            for start in range(g * LANES, (g + 1) * LANES, ROWS):
+                parts.append(picked_words(packed, rel_ref, base, slice(start, start + ROWS), c))
+            block = jnp.concatenate(parts, axis=0).T
+            for a, value in enumerate(unpack_heads(block, unit)):
+                key_ref[a, c * LANES : (c + 1) * LANES, g * LANES : (g + 1) * LANES] = value
+
+    for n in range(picks):
+        place = jnp.maximum(pos_ref[n], 0)
+        for a in range(2):
+            keyc[a, n : n + 1, :] = key_ref[a, pl.ds(place, 1), :]
     for a in range(2):
-        mine = (lane < HEAD) if a == 0 else (lane >= HEAD)
-        q_a = jnp.where(mine, qc_ref[...], zero)
-        k_a = jnp.where(mine, k_ref[...], zero)
-        left[:, :LANES] = q_a
-        right[:, :LANES] = k_a
-        crel[...] = dot_nt(k_a, pq_ref[...])
-        far = dot_nt(q_a, pk_ref[...])
-
-        def emit(rows, c, value):
-            split_store(right, rows, at[2] + c * LANES, at[3] + c * LANES, value)
-
-        shift_in_order(crel, word_ref, base, emit)
-        keyrow_ref[a] = right[:, at[2] :]
-        place = lane + (seq - 1) - wordc_ref[...]
-        index = place & (LANES - 1)
-        turned = [
-            jnp.take_along_axis(far[:, c * LANES : (c + 1) * LANES], index, axis=1)
-            for c in range(2 * chunks)
-        ]
+        mine = head_lanes(a)
+        direct = dot_nt(jnp.where(mine, qc_ref[...], zero), k_ref[...])
+        scores = []
         for c in range(chunks):
-            value = turned[c]
-            for n in range(1, chunks + 1):
-                if c + n < 2 * chunks:
-                    value = jnp.where(place >= n * LANES, turned[c + n], value)
-            split_store(left, slice(None), at[0] + c * LANES, at[1] + c * LANES, value)
-        probs = softmax_rows(dot_nt(left[...], right[...]))
+            ids = relc[:, c * LANES : (c + 1) * LANES]
+            index = ids & (LANES - 1)
+            value = jnp.take_along_axis(cpick[a, :, :LANES], index, axis=1)
+            for n in range(1, pk_ref.shape[0] // LANES):
+                other = cpick[a, :, n * LANES : (n + 1) * LANES]
+                value = jnp.where(
+                    ids >= n * LANES, jnp.take_along_axis(other, index, axis=1), value
+                )
+            cols = slice(c * LANES, (c + 1) * LANES)
+            scores.append(direct[:, cols] + value + keyc[a, :, cols])
+        weights = softmax_weights(scores)
+        inverse = 1.0 / jnp.sum(sum(weights[1:], weights[0]), axis=1, keepdims=True)
+        probs = jnp.concatenate([(weight * inverse).astype(bf16) for weight in weights], axis=1)
         prob_ref[a] = probs
         mixed = dot_nn(probs, v_ref[...]).astype(bf16)
-        if a == 0:
-            ctx_ref[...] = mixed
-        else:
-            ctx_ref[...] = jnp.where(mine, mixed, ctx_ref[...])
-
-
-def attend_picked(rel_ids, pick, q_pick, k, v, pos_query, pos_key):
+        ctx_ref[...] = mixed if a == 0 else jnp.where(mine, mixed, ctx_ref[...])
+
+
+def attend_picked(positions, rel_ids, q_pick, k, v, pos_query, pos_key):
     seq, width = k.shape
     picks = q_pick.shape[0]
+    table = pos_key.shape[0]
     pairs = width // LANES
-    wide = LANES + 4 * seq
     whole = lambda rows, cols: pl.BlockSpec((rows, cols), lambda h: (0, 0))
     col = lambda rows: pl.BlockSpec((rows, LANES), lambda h: (0, h))
+    heads = lambda rows: pl.BlockSpec((2, rows, seq), lambda h: (h, 0, 0))
     return pl.pallas_call(
         picked_kernel,
         grid=(pairs,),
         in_specs=[
-            whole(seq, seq), whole(picks, seq),
-            col(picks), col(seq), col(seq), col(2 * seq), col(2 * seq),
+            pl.BlockSpec(memory_space=pltpu.SMEM), whole(seq, seq),
+            col(picks), col(seq), col(seq), col(table), col(table),
         ],
         out_specs=[
-            col(picks),
-            pl.BlockSpec((2, picks, seq), lambda h: (h, 0, 0)),
-            pl.BlockSpec((2, seq, 2 * seq), lambda h: (h, 0, 0)),
-            whole(seq, LANES), whole(picks, LANES),
+            col(picks), heads(picks), heads(seq), whole(seq, LANES), whole(picks, LANES),
         ],
         out_shape=[
             jax.ShapeDtypeStruct((picks, width), bf16),
             jax.ShapeDtypeStruct((2 * pairs, picks, seq), bf16),
-            jax.ShapeDtypeStruct((2 * pairs, seq, 2 * seq), bf16),
+            jax.ShapeDtypeStruct((2 * pairs, seq, seq), f32),
             jax.ShapeDtypeStruct((seq, LANES), jnp.int32),
             jax.ShapeDtypeStruct((picks, LANES), jnp.int32),
         ],
         scratch_shapes=[
-            pltpu.VMEM((picks, wide), bf16),
-            pltpu.VMEM((seq, wide), bf16),
-            pltpu.VMEM((seq, 2 * seq), f32),
-            pltpu.SMEM((seq // LANES,), jnp.int32),
+            pltpu.VMEM((seq, 2 * table), jnp.int32),
+            pltpu.VMEM((2, picks, table), f32),
+            pltpu.VMEM((picks, seq), jnp.int32),
+            pltpu.VMEM((2, picks, seq), f32),
+            pltpu.SMEM((seq // HALF * (seq // LANES),), jnp.int32),
         ],
         compiler_params=pltpu.CompilerParams(vmem_limit_bytes=48 * 2**20),
         name="attend_picked",
-    )(rel_ids, pick, q_pick, k, v, pos_key, pos_query)
-
-
-def full_kernel(
-    word_ref, q_ref, k_ref, v_ref, pk_ref, keyrow_ref, ctx_ref, left, right, crel, base
-):
+    )(positions, rel_ids, q_pick, k, v, pos_key, pos_query)
+
+
+def full_kernel(rel_ref, q_ref, k_ref, v_ref, pk_ref, key_ref, ctx_ref, packed, direct, low, base):
     seq = q_ref.shape[0]
     chunks = seq // LANES
-    at = [LANES + n * seq for n in range(4)]
 
     @pl.when(pl.program_id(0) == 0)
     def _():
-        words = word_ref[...]
-        group_bases(words, base)
+        id_bases(rel_ref, base)
+
+    zero = jnp.zeros((), bf16)
+    table = both_alignments(pk_ref[...])
+    far = []
+    for a in range(2):
+        q_a = jnp.where(head_lanes(a), q_ref[...], zero)
+        far.append(dot_nt(q_a, table))
+        direct[a] = dot_nt(q_a, k_ref[...])
+    unit = pack_heads(far[0], far[1], packed, longest(q_ref[...]) * longest(pk_ref[...]))
+    for start in range(0, seq, HALF):
+        rows = slice(start, start + HALF)
+        scores = [[], []]
         for c in range(chunks):
-            member = member_chunk(words, c)
-            for ref, n in ((right, 0), (right, 1), (left, 2), (left, 3)):
-                ref[:, at[n] + c * LANES : at[n] + (c + 1) * LANES] = member
-
-    lane = lane_iota()
-    zero = jnp.zeros((), bf16)
-    for a in range(2):
-        mine = (lane < HEAD) if a == 0 else (lane >= HEAD)
-        q_a = jnp.where(mine, q_ref[...], zero)
-        left[:, :LANES] = q_a
-        right[:, :LANES] = k_ref[...]
-        right[:, at[2] :] = keyrow_ref[a]
-        crel[...] = dot_nt(q_a, pk_ref[...])
-
-        def emit(rows, c, value):
-            split_store(left, rows, at[0] + c * LANES, at[1] + c * LANES, value)
-
-        shift_in_order(crel, word_ref, base, emit)
-        for g in range(chunks):
-            rows = slice(g * LANES, (g + 1) * LANES)
-            probs = softmax_rows(dot_nt(left[rows, :], right[...]))
-            mixed = dot_nn(probs, v_ref[...]).astype(bf16)
-            if a == 0:
-                ctx_ref[rows, :] = mixed
-            else:
-                ctx_ref[rows, :] = jnp.where(mine, mixed, ctx_ref[rows, :])
-
-
-def attend_full(words, q, k, v, pos_key, keyrows):
+            cols = slice(c * LANES, (c + 1) * LANES)
+            values = unpack_heads(picked_words(packed, rel_ref, base, rows, c), unit)
+            for a in range(2):
+                scores[a].append(values[a] + direct[a, rows, cols] + key_ref[a, rows, cols])
+        for a in range(2):
+            for c, weight in enumerate(softmax_weights(scores[a])):
+                low[a, rows, c * LANES : (c + 1) * LANES] = weight.astype(bf16)
+    mixed = [
+        dot_nn(low[a], jnp.where(head_lanes(a), v_ref[...], jnp.ones((), bf16))) for a in range(2)
+    ]
+    upper = head_lanes(0)
+    totals = pltpu.roll(jnp.where(upper, mixed[1], mixed[0]), HEAD, 1)
+    ctx_ref[...] = (jnp.where(upper, mixed[0], mixed[1]) * (1.0 / totals)).astype(bf16)
+
+
+def attend_full(rel_ids, q, k, v, pos_key, key_scores):
     seq, width = k.shape
+    table = pos_key.shape[0]
     pairs = width // LANES
-    wide = LANES + 4 * seq
     col = lambda rows: pl.BlockSpec((rows, LANES), lambda h: (0, h))
     return pl.pallas_call(
         full_kernel,
         grid=(pairs,),
         in_specs=[
-            pl.BlockSpec((seq, LANES), lambda h: (0, 0)),
-            col(seq), col(seq), col(seq), col(2 * seq),
-            pl.BlockSpec((2, seq, 2 * seq), lambda h: (h, 0, 0)),
+            pl.BlockSpec((seq, seq), lambda h: (0, 0)),
+            col(seq), col(seq), col(seq), col(table),
+            pl.BlockSpec((2, seq, seq), lambda h: (h, 0, 0)),
         ],
         out_specs=col(seq),
         out_shape=jax.ShapeDtypeStruct((seq, width), bf16),
         scratch_shapes=[
-            pltpu.VMEM((seq, wide), bf16),
-            pltpu.VMEM((seq, wide), bf16),
-            pltpu.VMEM((seq, 2 * seq), f32),
-            pltpu.SMEM((seq // LANES,), jnp.int32),
+            pltpu.VMEM((seq, 2 * table), jnp.int32),
+            pltpu.VMEM((2, seq, seq), f32),
+            pltpu.VMEM((2, seq, seq), bf16),
+            pltpu.SMEM((seq // HALF * (seq // LANES),), jnp.int32),
         ],
         compiler_params=pltpu.CompilerParams(vmem_limit_bytes=48 * 2**20),
         name="attend_full",
-    )(words, q, k, v, pos_key, keyrows)
+    )(rel_ids, q, k, v, pos_key, key_scores)
 
 
 def back_kernel(
@@ -458,8 +468,10 @@
         distance_rows(seq_len, table_rows)[:, None] == np.arange(table_rows)[None, :]
     ).astype(np.float32)
     expand = jnp.asarray(to_rows, bf16)
-    pos_query = low(dot_nn(expand, low(dot_nn(rel_table, w_query) + b_query)))
-    pos_key = low(dot_nn(expand, low(dot_nn(rel_table, w_key) + b_key)))
+    pos_query = low(dot_nn(rel_table, w_query) + b_query)
+    pos_key = low(dot_nn(rel_table, w_key) + b_key)
+    far_query = low(dot_nn(expand, pos_query))
+    far_key = low(dot_nn(expand, pos_key))
 
     place = mask_pos + lax.broadcasted_iota(jnp.int32, mask_pos.shape, 0) * seq_len
     place = jnp.where(mask_pos >= 0, place, -1).reshape(-1)
@@ -473,12 +485,9 @@
     firsts = []
     for s in range(seq_count):
         rows = lambda value: seq_rows(value, s, seq_len)
-        own_pick = seq_rows(pick, s, slots)
-        if seq_count > 1:
-            own_pick = own_pick[:, s * seq_len : (s + 1) * seq_len]
         firsts.append(
             attend_picked(
-                rel_ids[s], own_pick, seq_rows(q_pick, s, slots), rows(k), rows(v), pos_query, pos_key
+                mask_pos[s], rel_ids[s], seq_rows(q_pick, s, slots), rows(k), rows(v), pos_query, pos_key
             )
         )
     join = lambda parts: parts[0] if seq_count == 1 else jnp.concatenate(parts, axis=0)
@@ -534,7 +543,7 @@
         _, probs, _, words, words_pick = firsts[s]
         backs.append(
             attend_back(
-                words, words_pick, picks(q_pick), rows(k), rows(v), picks(dctx), probs, pos_query, pos_key
+                words, words_pick, picks(q_pick), rows(k), rows(v), picks(dctx), probs, far_query, far_key
             )
         )
     dq = join([back[0] for back in backs])
@@ -576,7 +585,7 @@
     ctx = join(
         [
             attend_full(
-                firsts[s][3],
+                rel_ids[s],
                 seq_rows(q, s, seq_len),
                 seq_rows(k, s, seq_len),
                 seq_rows(v, s, seq_len),

time: 340 us -> 314 us (0.924)
  Pallas kernels: 123 us -> 87.5 us
  waiting for transfers between devices: 64.4 us -> 79.2 us
  matrix products: 61.6 us -> 54.9 us
    pallas_call x2, Pallas kernels: 96.4 us -> 52.2 us  [the longest x1 27.9 us: attend_picked(): pl.pallas_call(picked_kernel, grid=(pairs,), in_specs=[pl.BlockSpec(memor...]
    ppermute x15, waiting for transfers between devices: 64.4 us -> 79.2 us  [swap(): return lax.ppermute(values, axis, [(n, n ^ bit) for n in range(size)])]
    pallas_call x1, Pallas kernels: 27 us -> 35.3 us  [attend_back(): pl.pallas_call(back_kernel, grid=(pairs,), in_specs=[whole(seq, LANES), w...]
    dot_general x13 -> x15, matrix products: 33.4 us -> 26.5 us  [dot_nn(): lax.dot_general(first_op, second_op, (((1,), (0,)), ((), ())), preferred_...]
    unnamed x212 -> x210, local copies, waits for them, and re-layouts: 17.1 us -> 17.3 us
  transfers between devices with their start and end apart: 15 -> 15, of which waited for: 7 -> 8; matrix products, arithmetic and copies ran while one was open for 27% -> 32% of each run, Pallas kernels for 27% -> 11%
where the time goes in v2:
time: 314 us; the launch traced here: 309 us
  Pallas kernels  87.5 us (28%)
  waiting for transfers between devices  79.2 us (25%)
  matrix products  54.9 us (17%)
  local copies, waits for them, and re-layouts  37.8 us (12%)
  other arithmetic  24.3 us (8%)
  starting transfers between devices  23.4 us (7%)
    ppermute x15, waiting for transfers between devices, swap(): return lax.ppermute(values, axis, [(n, n ^ bit) for n in range(size)])  79.2 us
    pallas_call x1, Pallas kernels, attend_back(): pl.pallas_call(back_kernel, grid=(pairs,), in_specs=[whole(seq, LANES), w...  35.3 us
    pallas_call x1, Pallas kernels, attend_picked(): pl.pallas_call(picked_kernel, grid=(pairs,), in_specs=[pl.BlockSpec(memor...  27.9 us
    dot_general x15, matrix products, dot_nn(): lax.dot_general(first_op, second_op, (((1,), (0,)), ((), ())), preferred_...  26.5 us
    pallas_call x1, Pallas kernels, attend_full(): pl.pallas_call(full_kernel, grid=(pairs,), in_specs=[pl.BlockSpec((seq, s...  24.3 us
    ppermute x15, starting transfers between devices, swap(): return lax.ppermute(values, axis, [(n, n ^ bit) for n in range(size)])  23.4 us
    dot_general x12, matrix products, dot_tn(): lax.dot_general(first_op, second_op, (((0,), (0,)), ((), ())), preferred_...  18.4 us
    unnamed x210, local copies, waits for them, and re-layouts  17.3 us
  transfers between devices with their start and end apart: 15, of which 8 were waited for; matrix products, arithmetic and copies ran while one was open for 32% of the time, Pallas kernels for 11%

profile of v2, /device:TPU:0, one launch (start us, length us, event | category | flops | bytes accessed | tf_op | source)
XLA Modules:
  0.0 309.2 jit_solution(13162927591932962783)
XLA Ops:
  0.7 2.4 add_convert_fusion.6.k_ref
  8.0 27.9 %attend_picked.1 = (bf16[80,768]{1,0:T(8,128)(2,1)S(1)}, bf16[12,80,512]{2,1,0:T(8,128)(2,1)S(1)}, f32[12,512,512]{2,1,0:T(8,128)}, s32[512,128]{1,0:T(8,128)S(1)}, s32[80,128]{1,0:T(8,128)S(1)}) custom-call(s32[80]{0:T(128)S(1)} %bitcast.201, s32[512,512]{1,0:T(8,128)S(1)} %bitcast.199, bf16[80,768]{1,0:T(8,128)(2,1)S(1)} %convolution_convert_fusion.11.qc_ref, ...), custom_call_target="tpu_custom_call" | custom-call | tf_op jit(solution)/shard_map/attend_picked/pallas_call | solution.py:227
  36.9 24.3 %attend_full.1 = bf16[512,768]{1,0:T(8,128)(2,1)S(1)} custom-call(s32[512,512]{1,0:T(8,128)S(1)} %bitcast.200, bf16[512,768]{1,0:T(8,128)(2,1)S(1)} %add_convert_fusion.7.q_ref, bf16[512,768]{1,0:T(8,128)(2,1)S(1)} %add_convert_fusion.6.k_ref, bf16[512,768]{1,0:T(8,128)(2,1)S(1)} %add_convert_fusion.5.v_ref, bf16[512,768]{1,0:T(8,128)(2,1)S(1)} %add_convert_fusion.4.pk_ref, ...), custom_call_target="tpu_custom_call" | custom-call | tf_op jit(solution)/shard_map/attend_full/pallas_call | solution.py:296
  62.8 1.2 fusion.10
  64.0 3.0 collective-permute-start
  68.2 2.1 fusion.6.pk_ref
  70.4 17.0 %collective-permute-done.2 = bf16[80,768]{1,0:T(8,128)(2,1)S(1)} collective-permute-done((bf16[80,768]{1,0:T(8,128)(2,1)S(1)}, bf16[80,768]{1,0:T(8,128)(2,1)S(1)}, u32[]{:S(2)}, u32[]{:S(2)}) %collective-permute-start.2) | collective-permute-done | bytes 122912 | tf_op jit(solution)/shard_map/ppermute | solution.py:434
  87.4 1.6 multiply_convert_fusion.2
  89.8 1.8 collective-permute-start.3
  91.5 3.1 %collective-permute-done.3 = bf16[80,768]{1,0:T(8,128)(2,1)S(1)} collective-permute-done((bf16[80,768]{1,0:T(8,128)(2,1)S(1)}, bf16[80,768]{1,0:T(8,128)(2,1)S(1)}, u32[]{:S(2)}, u32[]{:S(2)}) %collective-permute-start.3) | collective-permute-done | bytes 122912 | tf_op jit(solution)/shard_map/ppermute | solution.py:434
  95.9 1.4 fusion.64
  97.3 1.8 collective-permute-start.4
  99.1 2.2 fusion.7.pq_ref
  101.3 1.4 stack_reshape.34
  102.7 1.4 stack_reshape.35
  104.1 1.4 stack_reshape.36
  105.4 3.6 %fusion.72 = (bf16[1536]{0:T(1024)(128)(2,1)}, bf16[160,1536]{1,0:T(8,128)(2,1)S(1)}) fusion(f32[160,1536]{1,0:T(8,128)} %get-tuple-element.76, bf16[1536,768]{1,0:T(8,128)(2,1)} %param.39, bf16[80,768]{1,0:T(8,128)(2,1)} %collective-permute-done.4, bf16[80,768]{1,0:T(8,128)(2,1)} %get-tuple-element.48), kind=kOutput, calls=%fused_computation.199 | convolution fusion | flops 380680704 | bytes 4082688 | tf_op jit(solution)/shard_map/dot_general | solution.py:29
  111.8 1.6 copy_dynamic-update-slice_fusion.1
  114.2 1.9 concatenate.43
  116.1 2.0 convolution_convert_fusion
  118.1 1.6 copy_dynamic-update-slice_fusion
  120.8 3.5 %dynamic-slice_bitcast_fusion.1 = bf16[8,104,1536]{2,1,0:T(8,128)(2,1)} fusion(bf16[8,2,104,1536]{3,2,0,1:T(8,128)(2,1)} %copy_dynamic-update-slice_fusion.2, s32[]{:T(128)S(6)} %select_n.106), kind=kLoop, calls=%fused_computation.17 | loop fusion | bytes 5111812 | tf_op jit(solution)/shard_map/jit(dynamic_index_in_dim)/squeeze | solution.py:444
  124.5 1.4 multiply_reduce_fusion.2
  126.6 1.6 convolution_convert_fusion.4
  128.2 35.3 %attend_back.1 = (bf16[80,768]{1,0:T(8,128)(2,1)S(1)}, bf16[512,768]{1,0:T(8,128)(2,1)S(1)}, bf16[512,768]{1,0:T(8,128)(2,1)S(1)}, bf16[1024,768]{1,0:T(8,128)(2,1)}, bf16[1024,768]{1,0:T(8,128)(2,1)}) custom-call(s32[512,128]{1,0:T(8,128)S(1)} %copy-done.11, s32[80,128]{1,0:T(8,128)S(1)} %get-tuple-element.32.wordc_ref, ...), custom_call_target="tpu_custom_call" | custom-call | tf_op jit(solution)/shard_map/attend_back/pallas_call | solution.py:388
  163.6 2.3 fusion.76
  166.0 1.9 convolution_convert_fusion.5
  167.9 1.3 reduce.3
  169.2 2.8 fusion.70
  173.8 1.1 constant_dynamic-update-slice_fusion.14
  175.7 2.0 fusion.71
  178.2 2.7 add_convert_fusion
  181.0 1.2 constant_dynamic-update-slice_fusion.13
  182.6 2.5 constant_dynamic-update-slice_fusion.12
  185.1 1.2 constant_dynamic-update-slice_fusion.11
  189.3 1.0 constant_dynamic-update-slice_fusion.10
  191.1 3.7 %dynamic-slice_bitcast_fusion = bf16[8,2,120,768]{3,2,1,0:T(8,128)(2,1)} fusion(bf16[8,2,2,120,768]{4,3,2,1,0:T(8,128)(2,1)} %constant_dynamic-update-slice_fusion.9, s32[]{:T(128)S(6)} %select_n.106), kind=kLoop, calls=%fused_computation.12 | loop fusion | bytes 5898244 | tf_op jit(solution)/shard_map/jit(dynamic_index_in_dim)/squeeze | solution.py:444
  197.8 2.4 fusion.1
  200.2 1.2 dynamic-slice_bitcast_fusion.3
  201.4 1.7 collective-permute-start.12
  203.1 2.0 add_add_fusion
  205.1 5.8 %convolution_convert_fusion.6 = bf16[512,768]{1,0:T(8,128)(2,1)} fusion(bf16[1536,768]{1,0:T(8,128)(2,1)} %param.39, bf16[512,768]{1,0:T(8,128)(2,1)} %collective-permute-done, bf16[768,1536]{1,0:T(8,128)(2,1)S(1)} %copy-done, f32[1536]{0:T(1024)S(1)} %copy-done.65), kind=kOutput, calls=%fused_computation.48 | convolution fusion | flops 2421030912 | bytes 6297600 | tf_op jit(solution)/shard_map/dot_general | solution.py:23
  210.9 1.7 collective-permute-start.1
  212.7 3.5 %fusion = bf16[8,2,120,768]{3,2,1,0:T(8,128)(2,1)S(1)} fusion(bf16[8,2,120,768]{3,2,1,0:T(8,128)(2,1)} %collective-permute-done.6, bf16[8,2,2,120,768]{4,3,2,1,0:T(8,128)(2,1)} %constant_dynamic-update-slice_fusion.9, s32[]{:T(128)S(6)} %select_n.105), kind=kLoop, calls=%fused_computation.1 | loop fusion | flops 5898240 | bytes 8847364 | tf_op jit(solution)/shard_map/convert_element_type | solution.py:446
  216.2 1.2 dynamic-slice_bitcast_fusion.2
  217.4 1.6 collective-permute-start.7
  219.0 13.7 %collective-permute-done.12 = bf16[4,104,1536]{2,1,0:T(8,128)(2,1)} collective-permute-done((bf16[4,104,1536]{2,1,0:T(8,128)(2,1)}, bf16[4,104,1536]{2,1,0:T(8,128)(2,1)}, u32[]{:S(2)}, u32[]{:S(2)}) %collective-permute-start.12) | collective-permute-done | bytes 1277984 | tf_op jit(solution)/shard_map/ppermute | solution.py:434
  232.6 1.6 fusion.3
  234.3 1.1 copy-done.23
  235.4 1.9 collective-permute-start.13
  237.3 6.9 %fusion.68 = (f32[512]{0:T(512)S(1)}, f32[512,768]{1,0:T(8,128)}) fusion(f32[768]{0:T(1024)S(1)} %copy-done.84, bf16[512,768]{1,0:T(8,128)(2,1)} %collective-permute-done.1, bf16[1536,768]{1,0:T(8,128)(2,1)} %param.39, bf16[768,1536]{1,0:T(8,128)(2,1)S(1)} %copy-done, f32[1536]{0:T(1024)S(1)} %copy-done.65, f32[768]{0:T(1024)S(1)} %copy-done.56, ...), kind=kOutput, calls=%fused_computation.195 | convolution fusion | flops 2426928640 | bytes 8672256 | tf_op jit(solution)/shard_map/dot_general | solution.py:23
  244.2 1.9 multiply_reduce_fusion
  246.1 4.3 %collective-permute-done.13 = bf16[2,104,1536]{2,1,0:T(8,128)(2,1)} collective-permute-done((bf16[2,104,1536]{2,1,0:T(8,128)(2,1)S(1)}, bf16[2,104,1536]{2,1,0:T(8,128)(2,1)}, u32[]{:S(2)}, u32[]{:S(2)}) %collective-permute-start.13) | collective-permute-done | bytes 639008 | tf_op jit(solution)/shard_map/ppermute | solution.py:434
  250.4 1.4 fusion.9
  251.9 2.8 collective-permute-start.14
  254.7 8.7 %collective-permute-done.7 = bf16[4,2,120,768]{3,2,1,0:T(8,128)(2,1)} collective-permute-done((bf16[4,2,120,768]{3,2,1,0:T(8,128)(2,1)}, bf16[4,2,120,768]{3,2,1,0:T(8,128)(2,1)}, u32[]{:S(2)}, u32[]{:S(2)}) %collective-permute-start.7) | collective-permute-done | bytes 1474592 | tf_op jit(solution)/shard_map/ppermute | solution.py:434
  263.4 1.8 fusion.2
  265.3 1.9 collective-permute-start.8
  267.2 1.2 add_convert_fusion.2
  268.5 14.7 %collective-permute-done.8 = bf16[2,2,120,768]{3,2,1,0:T(8,128)(2,1)S(1)} collective-permute-done((bf16[2,2,120,768]{3,2,1,0:T(8,128)(2,1)S(1)}, bf16[2,2,120,768]{3,2,1,0:T(8,128)(2,1)S(1)}, u32[]{:S(2)}, u32[]{:S(2)}) %collective-permute-start.8) | collective-permute-done | bytes 737312 | tf_op jit(solution)/shard_map/ppermute | solution.py:434
  283.4 2.8 collective-permute-start.9
  287.1 14.2 %collective-permute-done.9 = bf16[1,2,120,768]{3,2,1,0:T(8,128)(2,1)S(1)} collective-permute-done((bf16[1,2,120,768]{3,2,1,0:T(8,128)(2,1)S(1)}, bf16[1,2,120,768]{3,2,1,0:T(8,128)(2,1)S(1)}, u32[]{:S(2)}, u32[]{:S(2)}) %collective-permute-start.9) | collective-permute-done | bytes 368672 | tf_op jit(solution)/shard_map/ppermute | solution.py:434
  301.4 1.6 collective-permute-start.10
  303.5 3.5 %collective-permute-done.10 = bf16[1,120,768]{2,1,0:T(8,128)(2,1)S(1)} collective-permute-done((bf16[1,120,768]{2,1,0:T(8,128)(2,1)S(1)}, bf16[1,120,768]{2,1,0:T(8,128)(2,1)S(1)}, u32[]{:S(2)}, u32[]{:S(2)}) %collective-permute-start.10) | collective-permute-done | bytes 184352 | tf_op jit(solution)/shard_map/ppermute | solution.py:434
  (288 shorter events, 30.1 us)
Async XLA Ops:
  0.7 86.7 %copy-start = (bf16[768,1536]{1,0:T(8,128)(2,1)S(1)}, bf16[768,1536]{1,0:T(8,128)(2,1)}, u32[]{:S(2)}) copy-start(bf16[768,1536]{1,0:T(8,128)(2,1)} %param.37) | copy-start | bytes 7077892
  6.8 60.3 %copy-start.72 = (s32[80]{0:T(128)}, s32[80]{0:T(128)S(1)}, u32[]{:S(2)}) copy-start(s32[80]{0:T(128)S(1)} %fusion.50) | copy-start | bytes 964
  7.6 29.3 %copy-start.1 = (bf16[512,768]{1,0:T(8,128)(2,1)}, bf16[512,768]{1,0:T(8,128)(2,1)S(1)}, u32[]{:S(2)}) copy-start(bf16[512,768]{1,0:T(8,128)(2,1)S(1)} %add_convert_fusion.5.v_ref) | copy-start | bytes 2359300
  36.8 24.3 %copy-start.10 = (s32[512,128]{1,0:T(8,128)}, s32[512,128]{1,0:T(8,128)S(1)}, u32[]{:S(2)}) copy-start(s32[512,128]{1,0:T(8,128)S(1)} %get-tuple-element.31.word_ref) | copy-start | bytes 786436
  36.8 24.3 %copy-start.24 = (bf16[768,768]{1,0:T(8,128)(2,1)S(1)}, bf16[768,768]{1,0:T(8,128)(2,1)}, u32[]{:S(2)}) copy-start(bf16[768,768]{1,0:T(8,128)(2,1)} %param.29) | copy-start | bytes 3538948
  36.8 24.3 %copy-start.82 = (f32[768]{0:T(1024)S(1)}, f32[768]{0:T(1024)}, u32[]{:S(2)}) copy-start(f32[768]{0:T(1024)} %param.33) | copy-start | bytes 9220
  62.8 4.5 %copy-start.68 = (f32[512]{0:T(512)}, f32[512]{0:T(512)S(1)}, u32[]{:S(2)}) copy-start(f32[512]{0:T(512)S(1)} %add_rsqrt_fusion.1) | copy-start | bytes 6148
  64.0 4.2 %copy-start.93 = (bf16[1024,512]{1,0:T(8,128)(2,1)S(1)}, bf16[1024,512]{1,0:T(8,128)(2,1)}, u32[]{:S(2)}) copy-start(bf16[1024,512]{1,0:T(8,128)(2,1)} %constant.203.clone) | copy-start | bytes 3145732
  64.0 141.1 %collective-permute-start = (bf16[512,768]{1,0:T(8,128)(2,1)}, bf16[512,768]{1,0:T(8,128)(2,1)}, u32[]{:S(2)}, u32[]{:S(2)}) collective-permute-start(bf16[512,768]{1,0:T(8,128)(2,1)} %fusion.10), channel_id=1, source_target_pairs={{0,1},{1,0},{2,3},{3,2},{4,5},{5,4},{6,7},{7,6},{8,9},{9,8},{10,11... | collective-permute-start | bytes 2359304 | tf_op jit(solution)/shard_map/ppermute | solution.py:434
  67.3 3.0 copy-start.35
  67.8 26.9 %copy-start.17 = (f32[80,768]{1,0:T(8,128)}, f32[80,768]{1,0:T(8,128)S(1)}, u32[]{:S(2)}) copy-start(f32[80,768]{1,0:T(8,128)S(1)} %get-tuple-element.74) | copy-start | bytes 737284
  67.8 26.8 %copy-start.62 = (f32[80]{0:T(128)}, f32[80]{0:T(128)S(1)}, u32[]{:S(2)}) copy-start(f32[80]{0:T(128)S(1)} %broadcast_multiply_fusion.7) | copy-start | bytes 964
  68.0 26.6 %copy-start.70 = (f32[80]{0:T(128)}, f32[80]{0:T(128)S(1)}, u32[]{:S(2)}) copy-start(f32[80]{0:T(128)S(1)} %add_rsqrt_fusion.3) | copy-start | bytes 964
  68.1 19.3 %copy-start.64 = (f32[1536]{0:T(1024)S(1)}, f32[1536]{0:T(1024)}, u32[]{:S(2)}) copy-start(f32[1536]{0:T(1024)} %param.38) | copy-start | bytes 18436
  68.2 19.2 %collective-permute-start.2 = (bf16[80,768]{1,0:T(8,128)(2,1)S(1)}, bf16[80,768]{1,0:T(8,128)(2,1)S(1)}, u32[]{:S(2)}, u32[]{:S(2)}) collective-permute-start(bf16[80,768]{1,0:T(8,128)(2,1)S(1)} %fusion.33), channel_id=1, source_target_pairs={{0,1},{1,0},{2,3},{3,2},{4,5},{5,4},{6,7},{7,6},{8,9},{9,8},{10,11... | collective-permute-start | bytes 368648 | tf_op jit(solution)/shard_map/ppermute | solution.py:434
  70.4 18.6 %copy-start.34 = (bf16[1536,768]{1,0:T(8,128)(2,1)S(1)}, bf16[1536,768]{1,0:T(8,128)(2,1)}, u32[]{:S(2)}) copy-start(bf16[1536,768]{1,0:T(8,128)(2,1)} %param.39) | copy-start | bytes 7077892
  89.0 5.7 %copy-start.83 = (f32[768]{0:T(1024)S(1)}, f32[768]{0:T(1024)}, u32[]{:S(2)}) copy-start(f32[768]{0:T(1024)} %param.40) | copy-start | bytes 9220
  89.0 6.1 %copy-start.44 = (bf16[1,80,768]{2,1,0:T(8,128)(2,1)S(1)}, bf16[1,80,768]{2,1,0:T(8,128)(2,1)}, u32[]{:S(2)}) copy-start(bf16[1,80,768]{2,1,0:T(8,128)(2,1)} %param.25) | copy-start | bytes 368644
  89.0 6.1 %copy-start.53 = (f32[768]{0:T(1024)S(1)}, f32[768]{0:T(1024)}, u32[]{:S(2)}) copy-start(f32[768]{0:T(1024)} %param.41) | copy-start | bytes 9220
  89.8 4.9 %collective-permute-start.3 = (bf16[80,768]{1,0:T(8,128)(2,1)S(1)}, bf16[80,768]{1,0:T(8,128)(2,1)S(1)}, u32[]{:S(2)}, u32[]{:S(2)}) collective-permute-start(bf16[80,768]{1,0:T(8,128)(2,1)S(1)} %slice.141), channel_id=1, source_target_pairs={{0,1},{1,0},{2,3},{3,2},{4,5},{5,4},{6,7},{7,6},{8,9},{9,8},{10,11... | collective-permute-start | bytes 368648 | tf_op jit(solution)/shard_map/ppermute | solution.py:434
  91.5 9.8 %copy-start.74 = (pred[80]{0:T(512)(128)(4,1)}, pred[80]{0:T(512)(128)(4,1)S(1)}, u32[]{:S(2)}) copy-start(pred[80]{0:T(512)(128)(4,1)S(1)} %broadcast_compare_fusion) | copy-start | bytes 244
  97.3 8.1 %collective-permute-start.4 = (bf16[80,768]{1,0:T(8,128)(2,1)}, bf16[80,768]{1,0:T(8,128)(2,1)}, u32[]{:S(2)}, u32[]{:S(2)}) collective-permute-start(bf16[80,768]{1,0:T(8,128)(2,1)} %get-tuple-element.48), channel_id=1, source_target_pairs={{0,1},{1,0},{2,3},{3,2},{4,5},{5,4},{6,7},{7,6},{8,9},{9,8},{10,11... | collective-permute-start | bytes 368648 | tf_op jit(solution)/shard_map/ppermute | solution.py:434
  110.7 13.7 %collective-permute-start.5 = (bf16[80,768]{1,0:T(8,128)(2,1)}, bf16[80,768]{1,0:T(8,128)(2,1)}, u32[]{:S(2)}, u32[]{:S(2)}) collective-permute-start(bf16[80,768]{1,0:T(8,128)(2,1)} %slice.143), channel_id=1, source_target_pairs={{0,1},{1,0},{2,3},{3,2},{4,5},{5,4},{6,7},{7,6},{8,9},{9,8},{10,11... | collective-permute-start | bytes 368648 | tf_op jit(solution)/shard_map/ppermute | solution.py:434
  120.7 3.7 %copy-start.18 = (f32[80,768]{1,0:T(8,128)S(1)}, f32[80,768]{1,0:T(8,128)}, u32[]{:S(2)}) copy-start(f32[80,768]{1,0:T(8,128)} %copy-done.17) | copy-start | bytes 737284
  120.7 3.7 %copy-start.22 = (f32[80,768]{1,0:T(8,128)S(1)}, f32[80,768]{1,0:T(8,128)}, u32[]{:S(2)}) copy-start(f32[80,768]{1,0:T(8,128)} %copy-done.21) | copy-start | bytes 737284
  120.7 3.7 %copy-start.45 = (bf16[1,80,768]{2,1,0:T(8,128)(2,1)S(1)}, bf16[1,80,768]{2,1,0:T(8,128)(2,1)}, u32[]{:S(2)}) copy-start(bf16[1,80,768]{2,1,0:T(8,128)(2,1)} %param.25) | copy-start | bytes 368644
  120.7 3.7 %copy-start.47 = (bf16[160,768]{1,0:T(8,128)(2,1)S(1)}, bf16[160,768]{1,0:T(8,128)(2,1)}, u32[]{:S(2)}) copy-start(bf16[160,768]{1,0:T(8,128)(2,1)} %copy-done.46) | copy-start | bytes 737284
  120.7 3.7 %copy-start.52 = (f32[768]{0:T(1024)S(1)}, f32[768]{0:T(1024)}, u32[]{:S(2)}) copy-start(f32[768]{0:T(1024)} %param.35) | copy-start | bytes 9220
  120.7 3.7 %copy-start.54 = (f32[768]{0:T(1024)S(1)}, f32[768]{0:T(1024)}, u32[]{:S(2)}) copy-start(f32[768]{0:T(1024)} %param.41) | copy-start | bytes 9220
  120.7 3.7 %copy-start.63 = (f32[80]{0:T(128)S(1)}, f32[80]{0:T(128)}, u32[]{:S(2)}) copy-start(f32[80]{0:T(128)} %copy-done.62) | copy-start | bytes 964
  120.7 3.7 %copy-start.67 = (f32[80]{0:T(128)S(1)}, f32[80]{0:T(128)}, u32[]{:S(2)}) copy-start(f32[80]{0:T(128)} %copy-done.66) | copy-start | bytes 964
  120.7 3.7 %copy-start.71 = (f32[80]{0:T(128)S(1)}, f32[80]{0:T(128)}, u32[]{:S(2)}) copy-start(f32[80]{0:T(128)} %copy-done.70) | copy-start | bytes 964
  120.8 3.7 %copy-start.75 = (pred[80]{0:T(512)(128)(4,1)S(1)}, pred[80]{0:T(512)(128)(4,1)}, u32[]{:S(2)}) copy-start(pred[80]{0:T(512)(128)(4,1)} %copy-done.74) | copy-start | bytes 244
  120.8 3.7 %copy-start.77 = (f32[80]{0:T(128)S(1)}, f32[80]{0:T(128)}, u32[]{:S(2)}) copy-start(f32[80]{0:T(128)} %copy-done.76) | copy-start | bytes 964
  120.8 3.7 %copy-start.79 = (f32[80]{0:T(128)S(1)}, f32[80]{0:T(128)}, u32[]{:S(2)}) copy-start(f32[80]{0:T(128)} %copy-done.78) | copy-start | bytes 964
  120.8 3.7 %copy-start.81 = (f32[80]{0:T(128)S(1)}, f32[80]{0:T(128)}, u32[]{:S(2)}) copy-start(f32[80]{0:T(128)} %copy-done.80) | copy-start | bytes 964
  124.3 73.4 %collective-permute-start.11 = (bf16[8,104,1536]{2,1,0:T(8,128)(2,1)}, bf16[8,104,1536]{2,1,0:T(8,128)(2,1)}, u32[]{:S(2)}, u32[]{:S(2)}) collective-permute-start(bf16[8,104,1536]{2,1,0:T(8,128)(2,1)} %dynamic-slice_bitcast_fusion.1), channel_id=1, source_target_pairs={{0,2},{2,0},{4,6},{6,4},{8,10},{10,8},{12,14},{14,12},{16,18},{18,... | collective-permute-start | bytes 7667720 | tf_op jit(solution)/shard_map/ppermute | solution.py:434
  128.2 35.3 %copy-start.33 = (bf16[512,768]{1,0:T(8,128)(2,1)S(1)}, bf16[512,768]{1,0:T(8,128)(2,1)}, u32[]{:S(2)}) copy-start(bf16[512,768]{1,0:T(8,128)(2,1)} %param.22) | copy-start | bytes 2359300
  169.2 2.8 copy-start.31
  188.5 9.2 %slice-start = ((s8[5111808]{0:T(1024)(128)(4,1)}), s8[4194304]{0:T(1024)(128)(4,1)S(1)}, s32[]{:S(2)}) async-start(s8[5111808]{0:T(1024)(128)(4,1)} %bitcast.204), calls=%async_computation | async-start | bytes 8388608
  191.1 4.1 %copy-start.29 = (f32[80,768]{1,0:T(8,128)S(1)}, f32[80,768]{1,0:T(8,128)}, u32[]{:S(2)}) copy-start(f32[80,768]{1,0:T(8,128)} %copy-done.28) | copy-start | bytes 737284
  191.1 6.6 %slice-start.1 = ((s8[5111808]{0:T(1024)(128)(4,1)}), s8[917504]{0:T(1024)(128)(4,1)S(1)}, s32[]{:S(2)}) async-start(s8[5111808]{0:T(1024)(128)(4,1)} %bitcast.204), calls=%async_computation.1 | async-start | bytes 1835008
  194.8 17.8 %collective-permute-start.6 = (bf16[8,2,120,768]{3,2,1,0:T(8,128)(2,1)}, bf16[8,2,120,768]{3,2,1,0:T(8,128)(2,1)}, u32[]{:S(2)}, u32[]{:S(2)}) collective-permute-start(bf16[8,2,120,768]{3,2,1,0:T(8,128)(2,1)} %dynamic-slice_bitcast_fusion), channel_id=1, source_target_pairs={{0,2},{2,0},{4,6},{6,4},{8,10},{10,8},{12,14},{14,12},{16,18},{18,... | collective-permute-start | bytes 8847368 | tf_op jit(solution)/shard_map/ppermute | solution.py:434
  200.2 4.9 %copy-start.15 = (bf16[8,104,1536]{2,1,0:T(8,128)(2,1)}, bf16[8,104,1536]{2,1,0:T(8,128)(2,1)S(1)}, u32[]{:S(2)}) copy-start(bf16[8,104,1536]{2,1,0:T(8,128)(2,1)S(1)} %fusion.1) | copy-start | bytes 7667716
  200.2 2.9 copy-start.7
  200.2 2.9 copy-start.43
  201.4 3.7 %copy-start.65 = (f32[1536]{0:T(1024)S(1)}, f32[1536]{0:T(1024)}, u32[]{:S(2)}) copy-start(f32[1536]{0:T(1024)} %param.38) | copy-start | bytes 18436
  201.4 31.2 %collective-permute-start.12 = (bf16[4,104,1536]{2,1,0:T(8,128)(2,1)}, bf16[4,104,1536]{2,1,0:T(8,128)(2,1)}, u32[]{:S(2)}, u32[]{:S(2)}) collective-permute-start(bf16[4,104,1536]{2,1,0:T(8,128)(2,1)} %dynamic-slice_bitcast_fusion.3), channel_id=1, source_target_pairs={{0,4},{2,6},{4,0},{6,2},{8,12},{10,14},{12,8},{14,10},{16,20},{18,... | collective-permute-start | bytes 3833864 | tf_op jit(solution)/shard_map/ppermute | solution.py:434
  210.9 26.3 %collective-permute-start.1 = (bf16[512,768]{1,0:T(8,128)(2,1)}, bf16[512,768]{1,0:T(8,128)(2,1)}, u32[]{:S(2)}, u32[]{:S(2)}) collective-permute-start(bf16[512,768]{1,0:T(8,128)(2,1)} %convolution_convert_fusion.6), channel_id=1, source_target_pairs={{0,1},{1,0},{2,3},{3,2},{4,5},{5,4},{6,7},{7,6},{8,9},{9,8},{10,11... | collective-permute-start | bytes 2359304 | tf_op jit(solution)/shard_map/ppermute | solution.py:434
  216.1 18.1 %copy-start.13 = (bf16[8,2,120,768]{3,2,1,0:T(8,128)(2,1)}, bf16[8,2,120,768]{3,2,1,0:T(8,128)(2,1)S(1)}, u32[]{:S(2)}) copy-start(bf16[8,2,120,768]{3,2,1,0:T(8,128)(2,1)S(1)} %fusion) | copy-start | bytes 8847364
  216.2 16.5 %copy-start.16 = (bf16[8,104,1536]{2,1,0:T(8,128)(2,1)S(1)}, bf16[8,104,1536]{2,1,0:T(8,128)(2,1)}, u32[]{:S(2)}) copy-start(bf16[8,104,1536]{2,1,0:T(8,128)(2,1)} %copy-done.15) | copy-start | bytes 7667716
  217.4 19.9 %copy-start.56 = (f32[768]{0:T(1024)S(1)}, f32[768]{0:T(1024)}, u32[]{:S(2)}) copy-start(f32[768]{0:T(1024)} %param.36) | copy-start | bytes 9220
  217.4 19.9 %copy-start.61 = (f32[512]{0:T(512)S(1)}, f32[512]{0:T(512)}, u32[]{:S(2)}) copy-start(f32[512]{0:T(512)} %copy-done.60) | copy-start | bytes 6148
  217.4 19.9 %copy-start.69 = (f32[512]{0:T(512)S(1)}, f32[512]{0:T(512)}, u32[]{:S(2)}) copy-start(f32[512]{0:T(512)} %copy-done.68) | copy-start | bytes 6148
  217.4 19.9 %copy-start.84 = (f32[768]{0:T(1024)S(1)}, f32[768]{0:T(1024)}, u32[]{:S(2)}) copy-start(f32[768]{0:T(1024)} %param.40) | copy-start | bytes 9220
  217.4 46.0 %collective-permute-start.7 = (bf16[4,2,120,768]{3,2,1,0:T(8,128)(2,1)}, bf16[4,2,120,768]{3,2,1,0:T(8,128)(2,1)}, u32[]{:S(2)}, u32[]{:S(2)}) collective-permute-start(bf16[4,2,120,768]{3,2,1,0:T(8,128)(2,1)} %dynamic-slice_bitcast_fusion.2), channel_id=1, source_target_pairs={{0,4},{2,6},{4,0},{6,2},{8,12},{10,14},{12,8},{14,10},{16,20},{18,... | collective-permute-start | bytes 4423688 | tf_op jit(solution)/shard_map/ppermute | solution.py:434
  235.4 15.0 %collective-permute-start.13 = (bf16[2,104,1536]{2,1,0:T(8,128)(2,1)S(1)}, bf16[2,104,1536]{2,1,0:T(8,128)(2,1)}, u32[]{:S(2)}, u32[]{:S(2)}) collective-permute-start(bf16[2,104,1536]{2,1,0:T(8,128)(2,1)S(1)} %dynamic-slice_bitcast_fusion.5), channel_id=1, source_target_pairs={{0,8},{2,10},{4,12},{6,14},{8,0},{10,2},{12,4},{14,6},{16,24},{18,... | collective-permute-start | bytes 1916936 | tf_op jit(solution)/shard_map/ppermute | solution.py:434
  244.2 19.2 %copy-start.14 = (bf16[8,2,120,768]{3,2,1,0:T(8,128)(2,1)S(1)}, bf16[8,2,120,768]{3,2,1,0:T(8,128)(2,1)}, u32[]{:S(2)}) copy-start(bf16[8,2,120,768]{3,2,1,0:T(8,128)(2,1)} %copy-done.13) | copy-start | bytes 8847364
  251.9 15.4 %copy-start.85 = (f32[768]{0:T(1024)S(1)}, f32[768]{0:T(1024)}, u32[]{:S(2)}) copy-start(f32[768]{0:T(1024)} %param.42) | copy-start | bytes 9220
  251.9 16.5 %collective-permute-start.14 = (bf16[1,104,1536]{2,1,0:T(8,128)(2,1)S(1)}, bf16[1,104,1536]{2,1,0:T(8,128)(2,1)S(1)}, u32[]{:S(2)}, u32[]{:S(2)}) collective-permute-start(bf16[1,104,1536]{2,1,0:T(8,128)(2,1)S(1)} %constant_dynamic-slice_fusion), channel_id=1, source_target_pairs={{0,16},{2,18},{4,20},{6,22},{8,24},{10,26},{12,28},{14,30},{16,0},... | collective-permute-start | bytes 958472 | tf_op jit(solution)/shard_map/ppermute | solution.py:434
  263.4 3.8 %copy-start.20 = (f32[512,768]{1,0:T(8,128)S(1)}, f32[512,768]{1,0:T(8,128)}, u32[]{:S(2)}) copy-start(f32[512,768]{1,0:T(8,128)} %get-tuple-element.72) | copy-start | bytes 4718596
  265.3 17.8 %collective-permute-start.8 = (bf16[2,2,120,768]{3,2,1,0:T(8,128)(2,1)S(1)}, bf16[2,2,120,768]{3,2,1,0:T(8,128)(2,1)S(1)}, u32[]{:S(2)}, u32[]{:S(2)}) collective-permute-start(bf16[2,2,120,768]{3,2,1,0:T(8,128)(2,1)S(1)} %dynamic-slice_bitcast_fusion.4), channel_id=1, source_target_pairs={{0,8},{2,10},{4,12},{6,14},{8,0},{10,2},{12,4},{14,6},{16,24},{18,... | collective-permute-start | bytes 2211848 | tf_op jit(solution)/shard_map/ppermute | solution.py:434
  283.4 17.8 %collective-permute-start.9 = (bf16[1,2,120,768]{3,2,1,0:T(8,128)(2,1)S(1)}, bf16[1,2,120,768]{3,2,1,0:T(8,128)(2,1)S(1)}, u32[]{:S(2)}, u32[]{:S(2)}) collective-permute-start(bf16[1,2,120,768]{3,2,1,0:T(8,128)(2,1)S(1)} %constant_dynamic-slice_fusion.1), channel_id=1, source_target_pairs={{0,16},{2,18},{4,20},{6,22},{8,24},{10,26},{12,28},{14,30},{16,0},... | collective-permute-start | bytes 1105928 | tf_op jit(solution)/shard_map/ppermute | solution.py:434
  301.4 5.6 %collective-permute-start.10 = (bf16[1,120,768]{2,1,0:T(8,128)(2,1)S(1)}, bf16[1,120,768]{2,1,0:T(8,128)(2,1)S(1)}, u32[]{:S(2)}, u32[]{:S(2)}) collective-permute-start(bf16[1,120,768]{2,1,0:T(8,128)(2,1)S(1)} %dynamic-slice_bitcast_fusion.6), channel_id=1, source_target_pairs={{0,1},{1,0},{2,3},{3,2},{4,5},{5,4},{6,7},{7,6},{8,9},{9,8},{10,11... | collective-permute-start | bytes 552968 | tf_op jit(solution)/shard_map/ppermute | solution.py:434
  (48 other events, 76.6 us)

commit v3 on v2

--- a/solution.py
+++ b/solution.py
@@ -288,21 +288,20 @@
     ctx_ref[...] = (jnp.where(upper, mixed[0], mixed[1]) * (1.0 / totals)).astype(bf16)
 
 
-def attend_full(rel_ids, q, k, v, pos_key, key_scores):
-    seq, width = k.shape
+def attend_full(rel_ids, q, k, v, pos_key, key_scores, first, pairs):
+    seq = k.shape[0]
     table = pos_key.shape[0]
-    pairs = width // LANES
-    col = lambda rows: pl.BlockSpec((rows, LANES), lambda h: (0, h))
+    col = lambda rows: pl.BlockSpec((rows, LANES), lambda h: (0, h + first))
     return pl.pallas_call(
         full_kernel,
         grid=(pairs,),
         in_specs=[
             pl.BlockSpec((seq, seq), lambda h: (0, 0)),
             col(seq), col(seq), col(seq), col(table),
-            pl.BlockSpec((2, seq, seq), lambda h: (h, 0, 0)),
-        ],
-        out_specs=col(seq),
-        out_shape=jax.ShapeDtypeStruct((seq, width), bf16),
+            pl.BlockSpec((2, seq, seq), lambda h: (h + first, 0, 0)),
+        ],
+        out_specs=pl.BlockSpec((seq, LANES), lambda h: (0, h)),
+        out_shape=jax.ShapeDtypeStruct((seq, pairs * LANES), bf16),
         scratch_shapes=[
             pltpu.VMEM((seq, 2 * table), jnp.int32),
             pltpu.VMEM((2, seq, seq), f32),
@@ -316,7 +315,7 @@
 
 def back_kernel(
     word_ref, wordc_ref, qc_ref, k_ref, v_ref, dctx_ref, prob_ref, pk_ref, pq_ref,
-    dq_ref, dk_ref, dv_ref, dpk_ref, dpq_ref,
+    dq_ref, dk_ref, dv_ref, dpos_ref,
     side, sidec, moved, movedc, grel, base,
 ):
     seq = k_ref.shape[0]
@@ -372,7 +371,7 @@
         dk = out[:, seq:] + dot_nn(moved[:, : 2 * seq], keep(pq_ref[...]))
         dpq = dot_tn(moved[:, : 2 * seq], k_a)
         for ref, value in (
-            (dq_ref, dq), (dk_ref, dk), (dv_ref, dv), (dpk_ref, dpk), (dpq_ref, dpq),
+            (dq_ref, dq), (dk_ref, dk), (dv_ref, dv), (dpos_ref.at[0], dpk), (dpos_ref.at[1], dpq),
         ):
             low = value.astype(bf16)
             ref[...] = low if a == 0 else jnp.where(mine, low, ref[...])
@@ -394,8 +393,14 @@
             pl.BlockSpec((2, picks, seq), lambda h: (h, 0, 0)),
             col(2 * seq), col(2 * seq),
         ],
-        out_specs=[col(picks), col(seq), col(seq), col(2 * seq), col(2 * seq)],
-        out_shape=[shape(picks), shape(seq), shape(seq), shape(2 * seq), shape(2 * seq)],
+        out_specs=[
+            col(picks), col(seq), col(seq),
+            pl.BlockSpec((2, 2 * seq, LANES), lambda h: (0, 0, h)),
+        ],
+        out_shape=[
+            shape(picks), shape(seq), shape(seq),
+            jax.ShapeDtypeStruct((2, 2 * seq, width), bf16),
+        ],
         scratch_shapes=[
             pltpu.VMEM((seq, seq + LANES), bf16),
             pltpu.VMEM((picks, seq + LANES), bf16),
@@ -409,6 +414,76 @@
     )(words, words_pick, q_pick, k, v, dctx, probs, pos_key, pos_query)
 
 
+def grads_kernel(
+    half, x_ref, rel_ref, xpick_ref, cpick_ref, dpos_ref,
+    dq_ref, dk_ref, dv_ref, dattn_ref, dposk_ref, dposq_ref, wq_ref, wk_ref,
+    out_ref, sum_ref,
+):
+    width = x_ref.shape[1]
+    group = 2 * LANES
+    seq = x_ref.shape[0]
+
+    def left(ref):
+        starts = range(half * LANES, width, group)
+        return jnp.concatenate([ref[:, at : at + LANES] for at in starts], axis=1)
+
+    def put(at, value):
+        for n in range(value.shape[0] // LANES):
+            out_ref[at + n] = value[n * LANES : (n + 1) * LANES].astype(bf16)
+
+    count = width // group
+    rel_left = left(rel_ref)
+    x_left = left(x_ref)
+    put(0, dot_tn(left(xpick_ref), dq_ref[...]) + dot_tn(rel_left, dposq_ref[0]))
+    put(count, dot_tn(x_left, dk_ref[...]) + dot_tn(rel_left, dposk_ref[0]))
+    put(2 * count, dot_tn(x_left, dv_ref[...]))
+    put(3 * count, dot_tn(left(cpick_ref), dattn_ref[...]))
+    for n in range(dpos_ref.shape[1] // group):
+        rows = slice(n * group + half * LANES, n * group + (half + 1) * LANES)
+        put(
+            4 * count + n,
+            dot_nt(dpos_ref[0, rows, :], wk_ref[...]) + dot_nt(dpos_ref[1, rows, :], wq_ref[...]),
+        )
+    total = lambda ref: jnp.sum(ref[...].astype(f32), axis=-2).reshape(1, group)
+    sum_ref[...] = jnp.concatenate(
+        [
+            total(dq_ref) + total(dposq_ref),
+            total(dk_ref) + total(dposk_ref),
+            total(dv_ref),
+            jnp.zeros((5, group), f32),
+        ],
+        axis=0,
+    )
+
+
+def weight_grads(half, x, rel, x_pick, c_pick, dpos, dq, dk, dv, dattn, w_query, w_key):
+    seq, width = x.shape
+    group = 2 * LANES
+    planes = 4 * (width // group) + dpos.shape[1] // group
+    whole = lambda value: pl.BlockSpec(value.shape, lambda n: (0,) * value.ndim)
+    col = lambda value: pl.BlockSpec((value.shape[0], group), lambda n: (0, n))
+    row = lambda value: pl.BlockSpec((group, value.shape[1]), lambda n: (n, 0))
+    plane = lambda t: pl.BlockSpec((1, dpos.shape[1], group), lambda n: (t, 0, n))
+    return pl.pallas_call(
+        functools.partial(grads_kernel, half),
+        grid=(width // group,),
+        in_specs=[
+            whole(x), whole(rel), whole(x_pick), whole(c_pick), whole(dpos),
+            col(dq), col(dk), col(dv), col(dattn), plane(0), plane(1), row(w_query), row(w_key),
+        ],
+        out_specs=[
+            pl.BlockSpec((planes, LANES, group), lambda n: (0, 0, n)),
+            pl.BlockSpec((8, group), lambda n: (0, n)),
+        ],
+        out_shape=[
+            jax.ShapeDtypeStruct((planes, LANES, width), bf16),
+            jax.ShapeDtypeStruct((8, width), f32),
+        ],
+        compiler_params=pltpu.CompilerParams(vmem_limit_bytes=48 * 2**20),
+        name="weight_grads",
+    )(x, rel, x_pick, c_pick, dpos, dq, dk, dv, dattn, dpos, dpos, w_query, w_key)
+
+
 def norm_stats(values):
     centered = values - jnp.mean(values, axis=1, keepdims=True)
     inv_std = lax.rsqrt(jnp.mean(centered * centered, axis=1, keepdims=True) + norm_eps)
@@ -434,18 +509,50 @@
     return lax.ppermute(values, axis, [(n, n ^ bit) for n in range(size)])
 
 
-def halve_over(values, axis):
-    size = lax.axis_size(axis)
-    me = lax.axis_index(axis)
-    bit = 1
-    while bit < size:
-        mine = (me // bit) % 2
-        view = values.reshape((values.shape[0] // 2, 2) + values.shape[1:])
-        send = lax.dynamic_index_in_dim(view, 1 - mine, 1, keepdims=False)
-        keep = lax.dynamic_index_in_dim(view, mine, 1, keepdims=False)
-        values = (keep.astype(f32) + swap(send, axis, bit).astype(f32)).astype(bf16)
-        bit *= 2
-    return values[0]
+def after(values, *others):
+    return lax.optimization_barrier((values, others))[0]
+
+
+class Halving:
+    def __init__(self, axes, core, near, size):
+        rest = [1 << n for n in range(size.bit_length() - 1) if (1 << n) != core]
+        near = [bit for bit in near if bit in rest]
+        rest = [bit for bit in rest if bit not in near]
+        turned = near[-1:] + near[:-1]
+        self.axes, self.core, self.size = axes, core, size
+        self.orders = [[core] + near + rest, [core] + turned + rest]
+        self.steps = len(self.orders[0])
+        self.me = lax.axis_index(axes)
+        self.upper = (self.me // core) % 2
+
+    def core_of(self, place):
+        return (place // self.core) % 2
+
+    def send(self, values, step):
+        pairs = [(n, n ^ self.orders[self.core_of(n)][step]) for n in range(self.size)]
+        return lax.ppermute(values, self.axes, pairs)
+
+    def bit(self, step):
+        first, second = (order[step] for order in self.orders)
+        return jnp.where(self.upper == 0, first, second)
+
+    def block_of(self, places):
+        relative = []
+        for upper in range(2):
+            masks = []
+            for place in range(self.size):
+                bits = [(place >> (self.steps - 1 - step)) & 1 for step in range(self.steps)]
+                order = self.orders[upper ^ bits[0]]
+                mask = 0
+                for step, bit in enumerate(bits):
+                    mask ^= bit * order[step]
+                masks.append(mask)
+            relative.append(np.array(masks, np.int32)[places])
+        return self.me ^ jnp.where(self.upper == 0, relative[0], relative[1])
+
+
+def reorder(source, length):
+    return (lax.broadcasted_iota(jnp.int32, (length, source.shape[0]), 0) == source[None, :]).astype(bf16)
 
 
 def local(
@@ -457,41 +564,80 @@
     table_rows = rel_table.shape[0]
     hidden_cols = w_in.shape[1]
     slots = mask_pos.shape[1]
+    pairs = width // LANES
     n_tok = lax.axis_size("tok")
     n_ffn = lax.axis_size("ffn")
+    n_all = n_tok * n_ffn
     low = lambda value: value.astype(bf16)
 
-    q = low(dot_nn(tokens, w_query) + b_query)
-    k = low(dot_nn(tokens, w_key) + b_key)
-    v = low(dot_nn(tokens, w_value) + b_value)
-    to_rows = (
-        distance_rows(seq_len, table_rows)[:, None] == np.arange(table_rows)[None, :]
-    ).astype(np.float32)
-    expand = jnp.asarray(to_rows, bf16)
-    pos_query = low(dot_nn(rel_table, w_query) + b_query)
-    pos_key = low(dot_nn(rel_table, w_key) + b_key)
-    far_query = low(dot_nn(expand, pos_query))
-    far_key = low(dot_nn(expand, pos_key))
+    core = lax.axis_index("tok") % 2
+    half_cols = hidden_cols // 2
+    own_half = (
+        lax.dynamic_slice_in_dim(w_in, core * half_cols, half_cols, 1),
+        lax.dynamic_slice_in_dim(w_down, core * half_cols, half_cols, 0),
+        lax.dynamic_slice_in_dim(b_in, core * half_cols, half_cols, 0),
+    )
+    far_half = [swap(value, "ffn", 1) for value in own_half]
+    near_half = [swap(value, "tok", 1) for value in far_half]
+    shards = [(w_in, w_down, b_in), far_half, near_half]
 
     place = mask_pos + lax.broadcasted_iota(jnp.int32, mask_pos.shape, 0) * seq_len
     place = jnp.where(mask_pos >= 0, place, -1).reshape(-1)
     pick = low(place[:, None] == lax.broadcasted_iota(jnp.int32, (place.shape[0], rows_here), 1))
     x_pick = dot_nn(pick, tokens)
-    q_pick = low(dot_nn(pick, q))
+    x_pick_low = low(x_pick)
+    q_pick = low(dot_nn(x_pick_low, w_query) + b_query)
+    k = low(dot_nn(tokens, w_key) + b_key)
+    v = low(dot_nn(tokens, w_value) + b_value)
+    pos_query = low(dot_nn(rel_table, w_query) + b_query)
+    pos_key = low(dot_nn(rel_table, w_key) + b_key)
 
     def seq_rows(values, s, count):
         return values if seq_count == 1 else values[s * count : (s + 1) * count]
 
-    firsts = []
-    for s in range(seq_count):
-        rows = lambda value: seq_rows(value, s, seq_len)
-        firsts.append(
-            attend_picked(
-                mask_pos[s], rel_ids[s], seq_rows(q_pick, s, slots), rows(k), rows(v), pos_query, pos_key
-            )
+    firsts = [
+        attend_picked(
+            mask_pos[s],
+            rel_ids[s],
+            seq_rows(q_pick, s, slots),
+            seq_rows(k, s, seq_len),
+            seq_rows(v, s, seq_len),
+            pos_query,
+            pos_key,
         )
+        for s in range(seq_count)
+    ]
     join = lambda parts: parts[0] if seq_count == 1 else jnp.concatenate(parts, axis=0)
     ctx_pick = join([first[0] for first in firsts])
+
+    over_tok = Halving("tok", 1, [2, 4], n_tok)
+    over_all = Halving(("tok", "ffn"), n_ffn, [2 * n_ffn, 1, 4 * n_ffn], n_all)
+    part = width // n_tok
+    spots = np.arange(width)
+    tok_order = reorder(over_tok.block_of(spots // part) * part + spots % part, width)
+    own, own_rel = width // n_all, table_rows // n_all
+    unit = math.gcd(own, own_rel)
+    group = n_all * unit
+
+    def all_source(count, size):
+        spots = np.arange(count)
+        return (
+            over_all.block_of(spots % group // unit) * size
+            + spots // group * unit
+            + spots % unit
+        )
+
+    all_order = reorder(all_source(width, own), width)
+    rel_source = all_source(table_rows, own_rel)
+    rel_order = reorder(rel_source, table_rows)
+    to_rows = lax.optimization_barrier(jnp.asarray(distance_rows(seq_len, table_rows)))
+    expand = (to_rows[:, None] == lax.broadcasted_iota(jnp.int32, (1, table_rows), 1)).astype(bf16)
+    expand_order = (to_rows[:, None] == rel_source[None, :]).astype(bf16)
+    far_query = low(dot_nn(expand, pos_query))
+    far_key = low(dot_nn(expand, pos_key))
+    x_turned = low(dot_nn(tokens, all_order))
+    x_pick_turned = low(dot_nn(x_pick_low, all_order))
+    rel_turned = low(dot_nn(low(dot_tn(rel_order, rel_table)), all_order))
 
     h1_normed, h1_inv = norm_stats(x_pick + (dot_nn(ctx_pick, w_out) + b_out))
     h1_pick = h1_normed * ln1_gain + ln1_bias
@@ -513,106 +659,138 @@
     slope = cdf + pre * (jnp.exp(-0.5 * pre * pre) * (1.0 / math.sqrt(2.0 * math.pi)))
     dpre = low(dot_nt(dffn_both, w_down) * slope)
     dh1 = dz2 + both(dot_nt(dpre, w_in))
-    gw_down_t = low(dot_tn(dffn_both, hidden))
-    gw_in = low(dot_tn(h1_both, dpre))
-    gb_in = low(jnp.sum(dpre.astype(f32), axis=0))
+    gb_in = jnp.sum(dpre.astype(f32), axis=0)
     dz1, g_ln1_gain, g_ln1_bias = norm_backward(dh1, h1_normed, h1_inv, ln1_gain)
     dattn = low(dz1)
     g_b_out = jnp.sum(dattn.astype(f32), axis=0)
-    g_w_out = dot_tn(ctx_pick, dattn)
     dctx = low(dot_nt(dattn, w_out))
 
-    part = width // n_tok
-    ffn_blocks = jnp.concatenate(
-        [
-            gw_in.reshape(n_tok, part, hidden_cols),
-            gw_down_t.reshape(n_tok, part, hidden_cols),
-            jnp.pad(
-                gb_in.reshape(n_tok, 1, hidden_cols // n_tok),
-                ((0, 0), (0, 7), (0, hidden_cols - hidden_cols // n_tok)),
-            ),
-        ],
-        axis=1,
-    )
-    s_ffn = halve_over(ffn_blocks, "tok")
+    lefts = (low(dot_nn(h1_both, tok_order)), low(dot_nn(dffn_both, tok_order)))
+    rights = (dpre, hidden)
+    middle = width // 2
+    sends = [low(dot_tn(a[:, middle:], b)) for a, b in zip(lefts, rights)]
+    dctx, sends = lax.optimization_barrier((dctx, sends))
+    got = [over_tok.send(value, 0) for value in sends]
+    ffn_sums = [
+        low(dot_tn(a[:, :middle], b) + value.astype(f32)) for a, b, value in zip(lefts, rights, got)
+    ]
+
+    def halve(values, sums, step, axis):
+        size = values[0].shape[axis] // 2
+        cut = lambda value, at: lax.slice_in_dim(value, at, at + size, axis=axis)
+        got = [sums.send(cut(value, size), step) for value in values]
+        return [
+            low(cut(value, 0).astype(f32) + other.astype(f32)) for value, other in zip(values, got)
+        ]
 
     backs = []
     for s in range(seq_count):
-        rows = lambda value: seq_rows(value, s, seq_len)
         picks = lambda value: seq_rows(value, s, slots)
         _, probs, _, words, words_pick = firsts[s]
         backs.append(
             attend_back(
-                words, words_pick, picks(q_pick), rows(k), rows(v), picks(dctx), probs, far_query, far_key
+                words,
+                words_pick,
+                picks(q_pick),
+                seq_rows(k, s, seq_len),
+                seq_rows(v, s, seq_len),
+                picks(dctx),
+                probs,
+                far_query,
+                far_key,
             )
         )
     dq = join([back[0] for back in backs])
     dk = join([back[1] for back in backs])
     dv = join([back[2] for back in backs])
-    dpos_key = dot_tn(expand, sum(back[3].astype(f32) for back in backs).astype(bf16))
-    dpos_query = dot_tn(expand, sum(back[4].astype(f32) for back in backs).astype(bf16))
+    dfar = backs[0][3] if seq_count == 1 else low(sum(back[3].astype(f32) for back in backs))
+    for step in range(1, over_tok.steps):
+        ffn_sums = halve(ffn_sums, over_tok, step, 0)
+
+    dpos = low(jnp.einsum("mr,tmc->trc", expand_order, dfar, preferred_element_type=f32))
+    c_pick_turned = low(dot_nn(ctx_pick, all_order))
+    grads = lambda half: weight_grads(
+        half, x_turned, rel_turned, x_pick_turned, c_pick_turned, dpos, dq, dk, dv, dattn, w_query, w_key
+    )
+    send, sums = grads(1)
+    got = over_all.send(send, 0)
+    dk_later = after(dk, send)
+    keep, _ = weight_grads(
+        0, x_turned, rel_turned, x_pick_turned, c_pick_turned, dpos, dq, dk_later, dv, dattn, w_query, w_key
+    )
+    all_sums = low(keep.astype(f32) + got.astype(f32))
+    vectors = jnp.concatenate(
+        [
+            sums[:3],
+            jnp.stack([g_b_out, g_ln1_gain, g_ln1_bias, g_b_down, g_ln2_gain, g_ln2_bias]),
+            gb_in.reshape(hidden_cols // width, width),
+        ],
+        axis=0,
+    )
+    shared = lax.broadcasted_iota(jnp.int32, (vectors.shape[0], 1), 0) < 9
+
+    def double(values, step):
+        other = over_all.send(values, step)
+        return values + jnp.where(shared | (over_all.bit(step) != 1), other, 0.0)
+
+    vectors = double(vectors, 0)
+
+    q = low(dot_nn(after(tokens, dk), w_query) + b_query)
+    cuts = [0, pairs // 2, pairs]
+    ctx = []
+    for step in range(1, over_all.steps):
+        (next_sums,) = halve([all_sums], over_all, step, 1)
+        next_vectors = double(vectors, step)
+        if step < len(cuts):
+            at, stop = cuts[step - 1], cuts[step]
+            q = after(q, all_sums)
+            ctx.append(
+                join(
+                    [
+                        attend_full(
+                            rel_ids[s],
+                            seq_rows(q, s, seq_len),
+                            seq_rows(k, s, seq_len),
+                            seq_rows(v, s, seq_len),
+                            pos_key,
+                            firsts[s][2],
+                            at,
+                            stop - at,
+                        )
+                        for s in range(seq_count)
+                    ]
+                )
+            )
+        all_sums, vectors = next_sums, next_vectors
+    attn = sum(
+        dot_nn(value, w_out[at * LANES : stop * LANES])
+        for value, at, stop in zip(ctx, cuts[:-1], cuts[1:])
+    )
+    normed, _ = norm_stats(tokens.astype(f32) + (attn + b_out))
+    h1 = normed * ln1_gain + ln1_bias
+    h1_low = low(h1)
+    branch_all = b_down
+    for in_part, down_part, bias_part in shards:
+        pre_act = dot_nn(h1_low, in_part) + bias_part
+        branch_all = branch_all + dot_nn(low(pre_act * normal_cdf(pre_act)), down_part)
+    final, _ = norm_stats(h1 + branch_all)
+    output = low(final * ln2_gain + ln2_bias)
+
     sparse = dz1 + dot_nt(dq, w_query)
     sparse_up = low(sparse)
     sparse_lo = low(sparse - sparse_up.astype(f32))
     grad_tokens = (
         dot_tn(pick, sparse_up) + dot_tn(pick, sparse_lo) + dot_nt(dk, w_key) + dot_nt(dv, w_value)
     )
-    g_w_query = dot_tn(low(x_pick), dq) + dot_tn(rel_table, low(dpos_query))
-    g_w_key = dot_tn(tokens, dk) + dot_tn(rel_table, low(dpos_key))
-    g_w_value = dot_tn(tokens, dv)
-    g_rel = dot_nt(low(dpos_query), w_query) + dot_nt(low(dpos_key), w_key)
-    total = lambda value: jnp.sum(value.astype(f32), axis=0)
-    vectors = [
-        total(dq) + total(dpos_query),
-        total(dk) + total(dpos_key),
-        total(dv),
-        g_b_out, g_ln1_gain, g_ln1_bias, g_b_down, g_ln2_gain, g_ln2_bias,
-    ]
-    n_all = n_tok * n_ffn
-    own = width // n_all
-    vec_blocks = jnp.stack([value.reshape(n_all, own) for value in vectors], axis=1)
-    vec_blocks = vec_blocks.reshape(n_all, 1, len(vectors) * own)
-    vec_blocks = jnp.pad(vec_blocks, ((0, 0), (0, 7), (0, width - len(vectors) * own)))
-    all_blocks = jnp.concatenate(
-        [low(value).reshape(n_all, own, width) for value in (g_w_query, g_w_key, g_w_value, g_w_out)]
-        + [low(g_rel).reshape(n_all, table_rows // n_all, width), low(vec_blocks)],
-        axis=1,
-    )
-    tok_first = all_blocks.reshape((n_tok, n_ffn) + all_blocks.shape[1:])
-    s_tok = halve_over(tok_first, "tok")
-    s_all = halve_over(s_tok, "ffn")
-
-    ctx = join(
-        [
-            attend_full(
-                rel_ids[s],
-                seq_rows(q, s, seq_len),
-                seq_rows(k, s, seq_len),
-                seq_rows(v, s, seq_len),
-                pos_key,
-                firsts[s][2],
-            )
-            for s in range(seq_count)
-        ]
-    )
-    normed, _ = norm_stats(tokens.astype(f32) + (dot_nn(ctx, w_out) + b_out))
-    middle = normed * ln1_gain + ln1_bias
-    mine = low(middle)
-    theirs = swap(mine, "ffn", 1)
-
-    def ffn_part(value):
-        pre_act = dot_nn(value, w_in) + b_in
-        return low(dot_nn(low(pre_act * normal_cdf(pre_act)), w_down))
-
-    back = swap(ffn_part(theirs), "ffn", 1)
-    branch_all = ffn_part(mine).astype(f32) + back.astype(f32) + b_down
-    final, _ = norm_stats(middle + branch_all)
-    output = low(final * ln2_gain + ln2_bias)
 
     wide = lambda value: value.astype(f32)
-    s_vec = wide(s_all[4 * own + table_rows // n_all, : len(vectors) * own]).reshape(len(vectors), own)
-    s_w = [wide(s_all[n * own : (n + 1) * own]) for n in range(4)]
-    s_rel = wide(s_all[4 * own : 4 * own + table_rows // n_all])
+    all_sums = all_sums.reshape(all_sums.shape[0] * unit, width)
+    s_w = [wide(all_sums[n * own : (n + 1) * own]) for n in range(4)]
+    s_rel = wide(all_sums[4 * own :])
+    s_vec = lax.dynamic_slice_in_dim(vectors[:9], over_all.me * own, own, 1)
+    s_bin = lax.dynamic_slice_in_dim(
+        vectors[9:].reshape(1, hidden_cols), over_tok.me * (hidden_cols // n_tok), hidden_cols // n_tok, 1
+    )
     return (
         output,
         grad_tokens,
@@ -627,9 +805,9 @@
         s_rel,
         s_vec[4],
         s_vec[5],
-        wide(s_ffn[:part]),
-        wide(s_ffn[2 * part : 2 * part + 1, : hidden_cols // n_tok]),
-        jnp.transpose(wide(s_ffn[part : 2 * part])),
+        wide(ffn_sums[0]),
+        s_bin,
+        jnp.transpose(wide(ffn_sums[1])),
         s_vec[6],
         s_vec[7],
         s_vec[8],

time: 314 us -> 328 us (1.045)
  starting transfers between devices: 23.4 us -> 39.7 us
  matrix products: 54.9 us -> 69.5 us
  local copies, waits for them, and re-layouts: 37.8 us -> 23.5 us
  waiting for transfers between devices: 79.2 us -> 70.8 us
  Pallas kernels: 87.5 us -> 94.3 us
    ppermute x15 -> x10, waiting for transfers between devices: 79.2 us -> 28.5 us  [swap(): return lax.ppermute(values, axis, [(n, n ^ bit) for n in range(size)])]
    ppermute x0 -> x18, waiting for transfers between devices: none -> 42.3 us  [send(): return lax.ppermute(values, self.axes, pairs)]
    ppermute x0 -> x18, starting transfers between devices: none -> 29.3 us  [send(): return lax.ppermute(values, self.axes, pairs)]
    dot_general x15 -> x23, matrix products: 26.5 us -> 47.2 us  [dot_nn(): lax.dot_general(first_op, second_op, (((1,), (0,)), ((), ())), preferred_...]
    pallas_call x0 -> x2, Pallas kernels: none -> 13.1 us  [weight_grads(): pl.pallas_call(functools.partial(grads_kernel, half), grid=(width // grou...]
    ppermute x15 -> x10, starting transfers between devices: 23.4 us -> 10.4 us  [swap(): return lax.ppermute(values, axis, [(n, n ^ bit) for n in range(size)])]
    convert_element_type x9 -> x0, other arithmetic: 11.2 us -> none  [halve_over(): values = (keep.astype(f32) + swap(send, axis, bit).astype(f32)).astype(bf16)]
    dot_general x12 -> x6, matrix products: 18.4 us -> 7.55 us  [dot_tn(): lax.dot_general(first_op, second_op, (((0,), (0,)), ((), ())), preferred_...]
  transfers between devices with their start and end apart: 15 -> 28, of which waited for: 8 -> 14; matrix products, arithmetic and copies ran while one was open for 32% -> 29% of each run, Pallas kernels for 11% -> 20%
where the time goes in v3:
time: 328 us; the launch traced here: 322 us
  Pallas kernels  94.3 us (29%)
  waiting for transfers between devices  70.8 us (22%)
  matrix products  69.5 us (21%)
  starting transfers between devices  39.7 us (12%)
  local copies, waits for them, and re-layouts  23.5 us (7%)
  other arithmetic  21.6 us (7%)
    dot_general x23, matrix products, dot_nn(): lax.dot_general(first_op, second_op, (((1,), (0,)), ((), ())), preferred_...  47.2 us
    ppermute x18, waiting for transfers between devices, send(): return lax.ppermute(values, self.axes, pairs)  42.3 us
    ppermute x18, starting transfers between devices, send(): return lax.ppermute(values, self.axes, pairs)  29.3 us
    ppermute x10, waiting for transfers between devices, swap(): return lax.ppermute(values, axis, [(n, n ^ bit) for n in range(size)])  28.5 us
    pallas_call x1, Pallas kernels, attend_picked(): pl.pallas_call(picked_kernel, grid=(pairs,), in_specs=[pl.BlockSpec(memor...  28.3 us
    pallas_call x1, Pallas kernels, attend_back(): pl.pallas_call(back_kernel, grid=(pairs,), in_specs=[whole(seq, LANES), w...  26.9 us
    pallas_call x2, Pallas kernels, attend_full(): pl.pallas_call(full_kernel, grid=(pairs,), in_specs=[pl.BlockSpec((seq, s...  26 us
    pallas_call x2, Pallas kernels, weight_grads(): pl.pallas_call(functools.partial(grads_kernel, half), grid=(width // grou...  13.1 us
  transfers between devices with their start and end apart: 28, of which 14 were waited for; matrix products, arithmetic and copies ran while one was open for 29% of the time, Pallas kernels for 20%

profile of v3, /device:TPU:0, one launch (start us, length us, event | category | flops | bytes accessed | tf_op | source)
XLA Modules:
  0.0 321.8 jit_solution(10662758547244115542)
XLA Ops:
  2.0 1.4 fusion.68
  3.5 2.4 add_convert_fusion.9.k_ref
  10.7 28.3 %attend_picked.1 = (bf16[80,768]{1,0:T(8,128)(2,1)S(1)}, bf16[12,80,512]{2,1,0:T(8,128)(2,1)S(1)}, f32[12,512,512]{2,1,0:T(8,128)}, s32[512,128]{1,0:T(8,128)S(1)}, s32[80,128]{1,0:T(8,128)S(1)}) custom-call(s32[80]{0:T(128)S(1)} %bitcast.128, s32[512,512]{1,0:T(8,128)S(1)} %bitcast.125, bf16[80,768]{1,0:T(8,128)(2,1)S(1)} %fusion.33.qc_ref, ...), custom_call_target="tpu_custom_call" | custom-call | tf_op jit(solution)/shard_map/attend_picked/pallas_call | solution.py:227
  43.3 3.0 collective-permute-start
  50.5 3.4 %fusion.15.pk_ref = bf16[1024,768]{1,0:T(8,128)(2,1)} fusion(bf16[512,768]{1,0:T(8,128)(2,1)} %copy-done.10, s32[1024]{0:T(1024)S(1)} %copy-done.110), kind=kOutput, calls=%fused_computation.26 | convolution fusion | flops 806617088 | bytes 2363392 | tf_op jit(solution)/shard_map/dot_general | solution.py:23
  54.0 2.3 fusion.16.pq_ref
  57.0 2.1 fusion.35.cpick_ref
  59.1 2.9 fusion.22.x_ref
  62.0 1.2 fusion.34.xpick_ref
  63.8 3.5 %fusion.21.rel_ref = bf16[512,768]{1,0:T(8,128)(2,1)} fusion(bf16[512,768]{1,0:T(8,128)(2,1)} %param.45, s32[768]{0:T(1024)} %copy-done.98, s32[512]{0:T(512)} %multiply_add_fusion.4), kind=kOutput, calls=%fused_computation.45 | convolution fusion | flops 1008271360 | bytes 1577984 | tf_op jit(solution)/shard_map/dot_general | solution.py:23
  67.3 1.3 multiply_add_fusion.3
  69.7 2.7 multiply_convert_fusion.3
  76.3 26.7 %collective-permute-done.1 = bf16[80,768]{1,0:T(8,128)(2,1)} collective-permute-done((bf16[80,768]{1,0:T(8,128)(2,1)}, bf16[80,768]{1,0:T(8,128)(2,1)}, u32[]{:S(2)}, u32[]{:S(2)}) %collective-permute-start.1) | collective-permute-done | bytes 122912 | tf_op jit(solution)/shard_map/ppermute | solution.py:509
  103.1 1.3 fusion.109
  104.7 1.2 fusion.64
  107.0 1.8 collective-permute-start.2
  108.8 1.6 fusion.24
  112.8 1.5 convolution_convert_fusion
  114.4 1.6 convert_reduce_fusion
  117.6 1.5 collective-permute-start.3
  119.1 1.5 convolution_convert_fusion.1
  121.3 1.4 collective-permute-done.3
  122.8 1.7 multiply_reduce_fusion.2
  124.5 1.8 convert_reduce_fusion.2
  126.3 1.8 convolution_convert_fusion.5.dctx_ref
  128.2 26.9 %attend_back.1 = (bf16[80,768]{1,0:T(8,128)(2,1)S(1)}, bf16[512,768]{1,0:T(8,128)(2,1)S(1)}, bf16[512,768]{1,0:T(8,128)(2,1)S(1)}, bf16[2,1024,768]{2,1,0:T(8,128)(2,1)}) custom-call(s32[512,128]{1,0:T(8,128)S(1)} %copy-done.38, s32[80,128]{1,0:T(8,128)S(1)} %copy-done.41, bf16[80,768]{1,0:T(8,128)(2,1)S(1)} %copy-done.26, bf16[512,768]{1,0:T(8,128)(2,1)S(1)} %copy-done.3, ...), custom_call_target="tpu_custom_call" | custom-call | tf_op jit(solution)/shard_map/attend_back/pallas_call | solution.py:387
  155.1 5.6 %fusion.17.dpos_ref.dposk_ref.dposq_ref = bf16[2,512,768]{2,1,0:T(8,128)(2,1)} fusion(bf16[2,1024,768]{2,1,0:T(8,128)(2,1)} %get-tuple-element.45, s32[512]{0:T(512)S(1)} %copy-done.100, s32[1024]{0:T(1024)S(1)} %copy-done.112), kind=kOutput, calls=%fused_computation.42 | convolution fusion | flops 1611923456 | bytes 4724736 | tf_op jit(solution)/shard_map/mr,tmc->trc/dot_general | solution.py:710
  160.8 6.4 %weight_grads.2 = (bf16[14,128,768]{2,1,0:T(8,128)(2,1)}, f32[8,768]{1,0:T(8,128)S(1)}) custom-call(bf16[512,768]{1,0:T(8,128)(2,1)S(1)} %copy-done.17, bf16[512,768]{1,0:T(8,128)(2,1)S(1)} %copy-done.19, bf16[80,768]{1,0:T(8,128)(2,1)S(1)} %copy-done.35, bf16[80,768]{1,0:T(8,128)(2,1)S(1)} %copy-done.33, ...), custom_call_target="tpu_custom_call" | custom-call | tf_op jit(solution)/shard_map/weight_grads/pallas_call | solution.py:467
  169.5 2.7 concatenate.11
  172.2 2.4 fusion.119
  175.1 1.5 collective-permute-start.16
  177.2 2.1 collective-permute-done.16
  179.4 1.6 collective-permute-start.17
  181.4 2.1 collective-permute-done.17
  183.6 1.6 collective-permute-start.18
  185.8 1.9 collective-permute-done.18
  187.8 2.7 collective-permute-start.19
  190.5 2.0 add_add_fusion
  194.9 6.7 %weight_grads.3 = (bf16[14,128,768]{2,1,0:T(8,128)(2,1)}, f32[8,768]{1,0:T(8,128)}) custom-call(bf16[512,768]{1,0:T(8,128)(2,1)S(1)} %copy-done.18, bf16[512,768]{1,0:T(8,128)(2,1)S(1)} %copy-done.20, bf16[80,768]{1,0:T(8,128)(2,1)S(1)} %copy-done.36, bf16[80,768]{1,0:T(8,128)(2,1)S(1)} %copy-done.34, ...), custom_call_target="tpu_custom_call" | custom-call | tf_op jit(solution)/shard_map/weight_grads/pallas_call | solution.py:467
  201.7 1.8 add_convert_fusion.2
  203.5 1.5 collective-permute-start.25
  205.7 1.6 collective-permute-start.7
  207.3 1.8 add_convert_fusion.3
  211.1 2.4 collective-permute-done.25
  213.7 6.1 %collective-permute-done.21 = bf16[192,1536]{1,0:T(8,128)(2,1)S(1)} collective-permute-done((bf16[192,1536]{1,0:T(8,128)(2,1)S(1)}, bf16[192,1536]{1,0:T(8,128)(2,1)S(1)}, u32[]{:S(2)}, u32[]{:S(2)}) %collective-permute-start.21) | collective-permute-done | bytes 589856 | tf_op jit(solution)/shard_map/ppermute | solution.py:533
  219.8 1.6 collective-permute-start.26
  221.6 5.0 %collective-permute-done.26 = bf16[96,1536]{1,0:T(8,128)(2,1)S(1)} collective-permute-done((bf16[96,1536]{1,0:T(8,128)(2,1)S(1)}, bf16[96,1536]{1,0:T(8,128)(2,1)S(1)}, u32[]{:S(2)}, u32[]{:S(2)}) %collective-permute-start.26) | collective-permute-done | bytes 294944 | tf_op jit(solution)/shard_map/ppermute | solution.py:533
  226.5 1.6 collective-permute-start.22
  228.2 3.1 collective-permute-start.27
  232.2 6.2 %collective-permute-done.22 = bf16[96,1536]{1,0:T(8,128)(2,1)S(1)} collective-permute-done((bf16[96,1536]{1,0:T(8,128)(2,1)S(1)}, bf16[96,1536]{1,0:T(8,128)(2,1)S(1)}, u32[]{:S(2)}, u32[]{:S(2)}) %collective-permute-start.22) | collective-permute-done | bytes 294944 | tf_op jit(solution)/shard_map/ppermute | solution.py:533
  238.5 5.9 %collective-permute-start.23 = (bf16[48,1536]{1,0:T(8,128)(2,1)S(1)}, bf16[48,1536]{1,0:T(8,128)(2,1)S(1)}, u32[]{:S(2)}, u32[]{:S(2)}) collective-permute-start(bf16[48,1536]{1,0:T(8,128)(2,1)S(1)} %slice.219), channel_id=1, source_target_pairs={{0,16},{2,18},{4,20},{6,22},{8,24},{10,26},{12,28},{14,30},{16,0},... | collective-permute-start | bytes 442376 | tf_op jit(solution)/shard_map/ppermute | solution.py:533
  245.1 3.6 %collective-permute-done.23 = bf16[48,1536]{1,0:T(8,128)(2,1)S(1)} collective-permute-done((bf16[48,1536]{1,0:T(8,128)(2,1)S(1)}, bf16[48,1536]{1,0:T(8,128)(2,1)S(1)}, u32[]{:S(2)}, u32[]{:S(2)}) %collective-permute-start.23) | collective-permute-done | bytes 147488 | tf_op jit(solution)/shard_map/ppermute | solution.py:533
  249.4 12.9 %attend_full.2 = bf16[512,384]{1,0:T(8,128)(2,1)S(1)} custom-call(s32[512,512]{1,0:T(8,128)S(1)} %bitcast.126, bf16[512,768]{1,0:T(8,128)(2,1)S(1)} %add_convert_fusion.5.q_ref, bf16[512,768]{1,0:T(8,128)(2,1)S(1)} %copy-done.4, bf16[512,768]{1,0:T(8,128)(2,1)S(1)} %copy-done.7, bf16[512,768]{1,0:T(8,128)(2,1)S(1)} %copy-done.11, ...), custom_call_target="tpu_custom_call" | custom-call | tf_op jit(solution)/shard_map/attend_full/pallas_call | solution.py:295
  264.6 1.5 collective-permute-start.12
  266.2 13.1 %attend_full.3 = bf16[512,384]{1,0:T(8,128)(2,1)S(1)} custom-call(s32[512,512]{1,0:T(8,128)S(1)} %bitcast.127, bf16[512,768]{1,0:T(8,128)(2,1)S(1)} %add_convert_fusion.5.q_ref, bf16[512,768]{1,0:T(8,128)(2,1)S(1)} %copy-done.4, bf16[512,768]{1,0:T(8,128)(2,1)S(1)} %copy-done.7, bf16[512,768]{1,0:T(8,128)(2,1)S(1)} %copy-done.11, ...), custom_call_target="tpu_custom_call" | custom-call | tf_op jit(solution)/shard_map/attend_full/pallas_call | solution.py:295
  281.4 6.1 %fusion.49 = f32[512,768]{1,0:T(8,128)} fusion(bf16[1536,768]{1,0:T(8,128)(2,1)} %param.50, bf16[768,1536]{1,0:T(8,128)(2,1)S(1)} %copy-done, f32[1536]{0:T(1024)S(1)} %copy-done.78, f32[512,768]{1,0:T(8,128)} %copy-done.50, f32[768]{0:T(1024)S(1)} %copy-done.80, f32[768]{0:T(1024)S(1)} %copy-done.75, f32[512]{0:T(512)S(1)} %add_rsqrt_fusion.1, ...), kind=kOutput, calls=%fused_computation.87 | convolution fusion | flops 2422603776 | bytes 7880704 | tf_op jit(solution)/shard_map/dot_general | solution.py:23
  287.6 4.9 %fusion.44 = f32[512,768]{1,0:T(8,128)} fusion(bf16[768,768]{1,0:T(8,128)(2,1)} %collective-permute-done.8, bf16[768,768]{1,0:T(8,128)(2,1)} %collective-permute-done.6, f32[768]{0:T(1024)S(1)} %collective-permute-done.7, f32[512,768]{1,0:T(8,128)} %copy-done.50, f32[768]{0:T(1024)S(1)} %copy-done.80, f32[768]{0:T(1024)S(1)} %copy-done.75, ...), kind=kOutput, calls=%fused_computation.82 | convolution fusion | flops 1212284928 | bytes 5518336 | tf_op jit(solution)/shard_map/dot_general | solution.py:23
  292.5 6.3 %fusion.112 = (f32[512]{0:T(512)S(1)}, f32[512,768]{1,0:T(8,128)}) fusion(bf16[768,768]{1,0:T(8,128)(2,1)} %collective-permute-done.11, bf16[768,768]{1,0:T(8,128)(2,1)} %collective-permute-done.9, f32[768]{0:T(1024)S(1)} %collective-permute-done.10, f32[512,768]{1,0:T(8,128)} %fusion.44, f32[512,768]{1,0:T(8,128)} %fusion.49, f32[768]{0:T(1024)S(1)} %copy-done.93, ...), kind=kOutput, calls=%fused_computation.211 | convolution fusion | flops 1215823360 | bytes 8669184 | tf_op jit(solution)/shard_map/dot_general | solution.py:23
  298.8 1.4 add_convert_fusion.10
  300.3 3.0 collective-permute-start.13
  303.6 4.9 %collective-permute-done.13 = bf16[14,16,768]{2,1,0:T(8,128)(2,1)S(1)} collective-permute-done((bf16[14,16,768]{2,1,0:T(8,128)(2,1)S(1)}, bf16[14,16,768]{2,1,0:T(8,128)(2,1)S(1)}, u32[]{:S(2)}, u32[]{:S(2)}) %collective-permute-start.13) | collective-permute-done | bytes 344096 | tf_op jit(solution)/shard_map/ppermute | solution.py:533
  308.6 2.6 collective-permute-start.14
  311.2 1.2 add_convert_fusion.4
  312.4 7.6 %collective-permute-done.14 = bf16[14,8,768]{2,1,0:T(8,128)(2,1)S(1)} collective-permute-done((bf16[14,8,768]{2,1,0:T(8,128)(2,1)S(1)}, bf16[14,8,768]{2,1,0:T(8,128)(2,1)S(1)}, u32[]{:S(2)}, u32[]{:S(2)}) %collective-permute-start.14) | collective-permute-done | bytes 172064 | tf_op jit(solution)/shard_map/ppermute | solution.py:533
  (336 shorter events, 45.7 us)
Async XLA Ops:
  0.7 45.6 %copy-start = (bf16[768,1536]{1,0:T(8,128)(2,1)S(1)}, bf16[768,1536]{1,0:T(8,128)(2,1)}, u32[]{:S(2)}) copy-start(bf16[768,1536]{1,0:T(8,128)(2,1)} %param.48) | copy-start | bytes 7077892
  3.4 37.3 %copy-start.61 = (f32[80,768]{1,0:T(8,128)}, f32[80,768]{1,0:T(8,128)S(1)}, u32[]{:S(2)}) copy-start(f32[80,768]{1,0:T(8,128)S(1)} %fusion.68) | copy-start | bytes 737284
  10.2 28.8 %copy-start.5 = (bf16[512,768]{1,0:T(8,128)(2,1)}, bf16[512,768]{1,0:T(8,128)(2,1)S(1)}, u32[]{:S(2)}) copy-start(bf16[512,768]{1,0:T(8,128)(2,1)S(1)} %add_convert_fusion.8.v_ref) | copy-start | bytes 2359300
  10.7 30.7 %copy-start.43 = (bf16[768,768]{1,0:T(8,128)(2,1)S(1)}, bf16[768,768]{1,0:T(8,128)(2,1)}, u32[]{:S(2)}) copy-start(bf16[768,768]{1,0:T(8,128)(2,1)} %param.40) | copy-start | bytes 3538948
  10.7 30.7 %copy-start.81 = (f32[768]{0:T(1024)S(1)}, f32[768]{0:T(1024)}, u32[]{:S(2)}) copy-start(f32[768]{0:T(1024)} %param.44) | copy-start | bytes 9220
  43.3 26.4 %collective-permute-start = (bf16[80,768]{1,0:T(8,128)(2,1)}, bf16[80,768]{1,0:T(8,128)(2,1)}, u32[]{:S(2)}, u32[]{:S(2)}) collective-permute-start(bf16[80,768]{1,0:T(8,128)(2,1)} %fusion.65), channel_id=1, source_target_pairs={{0,1},{1,0},{2,3},{3,2},{4,5},{5,4},{6,7},{7,6},{8,9},{9,8},{10,11... | collective-permute-start | bytes 368648 | tf_op jit(solution)/shard_map/ppermute | solution.py:509
  47.3 163.2 %collective-permute-start.6 = (bf16[768,768]{1,0:T(8,128)(2,1)}, bf16[768,768]{1,0:T(8,128)(2,1)}, u32[]{:S(2)}, u32[]{:S(2)}) collective-permute-start(bf16[768,768]{1,0:T(8,128)(2,1)} %constant_dynamic-slice_fusion.3), channel_id=1, source_target_pairs={{0,1},{1,0},{2,3},{3,2},{4,5},{5,4},{6,7},{7,6},{8,9},{9,8},{10,11... | collective-permute-start | bytes 3538952 | tf_op jit(solution)/shard_map/ppermute | solution.py:509
  49.5 161.1 %collective-permute-start.8 = (bf16[768,768]{1,0:T(8,128)(2,1)}, bf16[768,768]{1,0:T(8,128)(2,1)}, u32[]{:S(2)}, u32[]{:S(2)}) collective-permute-start(bf16[768,768]{1,0:T(8,128)(2,1)} %constant_dynamic-slice_fusion.2), channel_id=1, source_target_pairs={{0,1},{1,0},{2,3},{3,2},{4,5},{5,4},{6,7},{7,6},{8,9},{9,8},{10,11... | collective-permute-start | bytes 3538952 | tf_op jit(solution)/shard_map/ppermute | solution.py:509
  63.8 5.9 %copy-start.77 = (f32[1536]{0:T(1024)S(1)}, f32[1536]{0:T(1024)}, u32[]{:S(2)}) copy-start(f32[1536]{0:T(1024)} %param.49) | copy-start | bytes 18436
  72.4 32.3 %copy-start.76 = (f32[768]{0:T(1024)S(1)}, f32[768]{0:T(1024)}, u32[]{:S(2)}) copy-start(f32[768]{0:T(1024)} %param.52) | copy-start | bytes 9220
  73.6 29.5 %collective-permute-start.1 = (bf16[80,768]{1,0:T(8,128)(2,1)}, bf16[80,768]{1,0:T(8,128)(2,1)}, u32[]{:S(2)}, u32[]{:S(2)}) collective-permute-start(bf16[80,768]{1,0:T(8,128)(2,1)} %slice.194), channel_id=1, source_target_pairs={{0,1},{1,0},{2,3},{3,2},{4,5},{5,4},{6,7},{7,6},{8,9},{9,8},{10,11... | collective-permute-start | bytes 368648 | tf_op jit(solution)/shard_map/ppermute | solution.py:509
  75.8 33.0 %copy-start.97 = (s32[768]{0:T(1024)S(1)}, s32[768]{0:T(1024)}, u32[]{:S(2)}) copy-start(s32[768]{0:T(1024)} %multiply_add_fusion.3) | copy-start | bytes 9220
  107.0 5.8 %copy-start.47 = (bf16[160,1536]{1,0:T(8,128)(2,1)S(1)}, bf16[160,1536]{1,0:T(8,128)(2,1)}, u32[]{:S(2)}) copy-start(bf16[160,1536]{1,0:T(8,128)(2,1)} %copy-done.46) | copy-start | bytes 1474564
  107.0 5.2 %collective-permute-start.2 = (bf16[80,768]{1,0:T(8,128)(2,1)S(1)}, bf16[80,768]{1,0:T(8,128)(2,1)S(1)}, u32[]{:S(2)}, u32[]{:S(2)}) collective-permute-start(bf16[80,768]{1,0:T(8,128)(2,1)S(1)} %get-tuple-element.66), channel_id=1, source_target_pairs={{0,1},{1,0},{2,3},{3,2},{4,5},{5,4},{6,7},{7,6},{8,9},{9,8},{10,11... | collective-permute-start | bytes 368648 | tf_op jit(solution)/shard_map/ppermute | solution.py:509
  110.4 8.7 %copy-start.70 = (bf16[160,768]{1,0:T(8,128)(2,1)}, bf16[160,768]{1,0:T(8,128)(2,1)S(1)}, u32[]{:S(2)}) copy-start(bf16[160,768]{1,0:T(8,128)(2,1)S(1)} %fusion.24) | copy-start | bytes 737284
  117.6 5.2 %collective-permute-start.3 = (bf16[80,768]{1,0:T(8,128)(2,1)}, bf16[80,768]{1,0:T(8,128)(2,1)}, u32[]{:S(2)}, u32[]{:S(2)}) collective-permute-start(bf16[80,768]{1,0:T(8,128)(2,1)} %slice.196), channel_id=1, source_target_pairs={{0,1},{1,0},{2,3},{3,2},{4,5},{5,4},{6,7},{7,6},{8,9},{9,8},{10,11... | collective-permute-start | bytes 368648 | tf_op jit(solution)/shard_map/ppermute | solution.py:509
  121.3 6.8 %copy-start.3 = (bf16[512,768]{1,0:T(8,128)(2,1)S(1)}, bf16[512,768]{1,0:T(8,128)(2,1)}, u32[]{:S(2)}) copy-start(bf16[512,768]{1,0:T(8,128)(2,1)} %copy-done.2) | copy-start | bytes 2359300
  121.3 6.8 %copy-start.6 = (bf16[512,768]{1,0:T(8,128)(2,1)S(1)}, bf16[512,768]{1,0:T(8,128)(2,1)}, u32[]{:S(2)}) copy-start(bf16[512,768]{1,0:T(8,128)(2,1)} %copy-done.5) | copy-start | bytes 2359300
  121.3 6.8 %copy-start.26 = (bf16[80,768]{1,0:T(8,128)(2,1)S(1)}, bf16[80,768]{1,0:T(8,128)(2,1)}, u32[]{:S(2)}) copy-start(bf16[80,768]{1,0:T(8,128)(2,1)} %copy-done.25) | copy-start | bytes 368644
  121.3 6.8 %copy-start.30 = (bf16[12,80,512]{2,1,0:T(8,128)(2,1)S(1)}, bf16[12,80,512]{2,1,0:T(8,128)(2,1)}, u32[]{:S(2)}) copy-start(bf16[12,80,512]{2,1,0:T(8,128)(2,1)} %copy-done.29) | copy-start | bytes 2949124
  121.3 6.8 %copy-start.38 = (s32[512,128]{1,0:T(8,128)S(1)}, s32[512,128]{1,0:T(8,128)}, u32[]{:S(2)}) copy-start(s32[512,128]{1,0:T(8,128)} %copy-done.37) | copy-start | bytes 786436
  121.3 6.8 %copy-start.41 = (s32[80,128]{1,0:T(8,128)S(1)}, s32[80,128]{1,0:T(8,128)}, u32[]{:S(2)}) copy-start(s32[80,128]{1,0:T(8,128)} %copy-done.40) | copy-start | bytes 122884
  126.3 34.4 %copy-start.23 = (bf16[80,768]{1,0:T(8,128)(2,1)}, bf16[80,768]{1,0:T(8,128)(2,1)S(1)}, u32[]{:S(2)}) copy-start(bf16[80,768]{1,0:T(8,128)(2,1)S(1)} %get-tuple-element.68.dattn_ref) | copy-start | bytes 368644
  128.1 26.9 %copy-start.100 = (s32[512]{0:T(512)S(1)}, s32[512]{0:T(512)}, u32[]{:S(2)}) copy-start(s32[512]{0:T(512)} %multiply_add_fusion.4) | copy-start | bytes 6148
  128.2 26.9 %copy-start.112 = (s32[1024]{0:T(1024)S(1)}, s32[1024]{0:T(1024)}, u32[]{:S(2)}) copy-start(s32[1024]{0:T(1024)} %constant.146.clone) | copy-start | bytes 12292
  172.2 2.9 collective-permute-start.15
  174.6 6.4 %copy-start.90 = (s32[80]{0:T(128)S(1)}, s32[80]{0:T(128)}, u32[]{:S(2)}) copy-start(s32[80]{0:T(128)} %copy-done.89) | copy-start | bytes 964
  174.6 27.0 %collective-permute-start.24 = (bf16[384,1536]{1,0:T(8,128)(2,1)}, bf16[384,1536]{1,0:T(8,128)(2,1)}, u32[]{:S(2)}, u32[]{:S(2)}) collective-permute-start(bf16[384,1536]{1,0:T(8,128)(2,1)} %convolution_convert_fusion), channel_id=1, source_target_pairs={{0,2},{2,0},{4,6},{6,4},{8,10},{10,8},{12,14},{14,12},{16,18},{18,... | collective-permute-start | bytes 3538952 | tf_op jit(solution)/shard_map/ppermute | solution.py:533
  175.1 4.2 %collective-permute-start.16 = (f32[11,768]{1,0:T(8,128)S(1)}, f32[11,768]{1,0:T(8,128)S(1)}, u32[]{:S(2)}, u32[]{:S(2)}) collective-permute-start(f32[11,768]{1,0:T(8,128)S(1)} %add.391), channel_id=1, source_target_pairs={{0,4},{1,5},{2,10},{3,11},{4,0},{5,1},{6,14},{7,15},{8,12},{9,13},... | collective-permute-start | bytes 101384 | tf_op jit(solution)/shard_map/ppermute | solution.py:533
  176.7 6.9 %copy-start.105 = (pred[11]{0:T(512)(128)(4,1)S(1)}, pred[11]{0:T(512)(128)(4,1)}, u32[]{:S(2)}) copy-start(pred[11]{0:T(512)(128)(4,1)} %broadcast_or_fusion.1) | copy-start | bytes 37
  179.4 6.3 %copy-start.63 = (bf16[384,1536]{1,0:T(8,128)(2,1)S(1)}, bf16[384,1536]{1,0:T(8,128)(2,1)}, u32[]{:S(2)}) copy-start(bf16[384,1536]{1,0:T(8,128)(2,1)} %convolution_convert_fusion.1) | copy-start | bytes 3538948
  179.4 8.4 %copy-start.106 = (pred[11]{0:T(512)(128)(4,1)S(1)}, pred[11]{0:T(512)(128)(4,1)}, u32[]{:S(2)}) copy-start(pred[11]{0:T(512)(128)(4,1)} %broadcast_or_fusion) | copy-start | bytes 37
  179.4 11.1 %copy-start.13 = (bf16[512,768]{1,0:T(8,128)(2,1)S(1)}, bf16[512,768]{1,0:T(8,128)(2,1)}, u32[]{:S(2)}) copy-start(bf16[512,768]{1,0:T(8,128)(2,1)} %copy-done.12) | copy-start | bytes 2359300
  179.4 11.1 %copy-start.65 = (bf16[768,768]{1,0:T(8,128)(2,1)S(1)}, bf16[768,768]{1,0:T(8,128)(2,1)}, u32[]{:S(2)}) copy-start(bf16[768,768]{1,0:T(8,128)(2,1)} %param.39) | copy-start | bytes 3538948
  179.4 4.2 %collective-permute-start.17 = (f32[11,768]{1,0:T(8,128)S(1)}, f32[11,768]{1,0:T(8,128)S(1)}, u32[]{:S(2)}, u32[]{:S(2)}) collective-permute-start(f32[11,768]{1,0:T(8,128)S(1)} %select_add_fusion.2), channel_id=1, source_target_pairs={{0,1},{1,0},{2,6},{3,7},{4,5},{5,4},{6,2},{7,3},{8,9},{9,8},{10,14... | collective-permute-start | bytes 101384 | tf_op jit(solution)/shard_map/ppermute | solution.py:533
  183.6 4.1 %collective-permute-start.18 = (f32[11,768]{1,0:T(8,128)S(1)}, f32[11,768]{1,0:T(8,128)S(1)}, u32[]{:S(2)}, u32[]{:S(2)}) collective-permute-start(f32[11,768]{1,0:T(8,128)S(1)} %select_add_fusion.1), channel_id=1, source_target_pairs={{0,8},{1,9},{2,3},{3,2},{4,12},{5,13},{6,7},{7,6},{8,0},{9,1},{10,... | collective-permute-start | bytes 101384 | tf_op jit(solution)/shard_map/ppermute | solution.py:533
  185.7 20.0 %collective-permute-start.20 = (bf16[384,1536]{1,0:T(8,128)(2,1)S(1)}, bf16[384,1536]{1,0:T(8,128)(2,1)}, u32[]{:S(2)}, u32[]{:S(2)}) collective-permute-start(bf16[384,1536]{1,0:T(8,128)(2,1)S(1)} %copy-done.63), channel_id=1, source_target_pairs={{0,2},{2,0},{4,6},{6,4},{8,10},{10,8},{12,14},{14,12},{16,18},{18,... | collective-permute-start | bytes 3538952 | tf_op jit(solution)/shard_map/ppermute | solution.py:533
  187.8 5.1 %collective-permute-start.19 = (f32[11,768]{1,0:T(8,128)S(1)}, f32[11,768]{1,0:T(8,128)S(1)}, u32[]{:S(2)}, u32[]{:S(2)}) collective-permute-start(f32[11,768]{1,0:T(8,128)S(1)} %select_add_fusion), channel_id=1, source_target_pairs={{0,16},{1,17},{2,18},{3,19},{4,20},{5,21},{6,22},{7,23},{8,24},{9,... | collective-permute-start | bytes 101384 | tf_op jit(solution)/shard_map/ppermute | solution.py:533
  192.9 35.3 %collective-permute-start.4 = (bf16[14,128,768]{2,1,0:T(8,128)(2,1)}, bf16[14,128,768]{2,1,0:T(8,128)(2,1)S(1)}, u32[]{:S(2)}, u32[]{:S(2)}) collective-permute-start(bf16[14,128,768]{2,1,0:T(8,128)(2,1)} %get-tuple-element.48), channel_id=1, source_target_pairs={{0,2},{1,3},{2,0},{3,1},{4,6},{5,7},{6,4},{7,5},{8,10},{9,11},{10,... | collective-permute-start | bytes 8257544 | tf_op jit(solution)/shard_map/ppermute | solution.py:533
  194.9 6.7 %copy-start.48 = (bf16[160,1536]{1,0:T(8,128)(2,1)S(1)}, bf16[160,1536]{1,0:T(8,128)(2,1)}, u32[]{:S(2)}) copy-start(bf16[160,1536]{1,0:T(8,128)(2,1)} %copy-done.46) | copy-start | bytes 1474564
  194.9 6.7 %copy-start.73 = (bf16[160,768]{1,0:T(8,128)(2,1)S(1)}, bf16[160,768]{1,0:T(8,128)(2,1)}, u32[]{:S(2)}) copy-start(bf16[160,768]{1,0:T(8,128)(2,1)} %copy-done.72) | copy-start | bytes 737284
  201.6 5.7 %copy-start.57 = (bf16[160,1536]{1,0:T(8,128)(2,1)S(1)}, bf16[160,1536]{1,0:T(8,128)(2,1)}, u32[]{:S(2)}) copy-start(bf16[160,1536]{1,0:T(8,128)(2,1)} %copy-done.56) | copy-start | bytes 1474564
  203.5 9.9 %collective-permute-start.25 = (bf16[192,1536]{1,0:T(8,128)(2,1)S(1)}, bf16[192,1536]{1,0:T(8,128)(2,1)S(1)}, u32[]{:S(2)}, u32[]{:S(2)}) collective-permute-start(bf16[192,1536]{1,0:T(8,128)(2,1)S(1)} %slice.223), channel_id=1, source_target_pairs={{0,4},{2,10},{4,0},{6,14},{8,12},{10,2},{12,8},{14,6},{16,20},{18,... | collective-permute-start | bytes 1769480 | tf_op jit(solution)/shard_map/ppermute | solution.py:533
  205.7 3.7 %collective-permute-start.7 = (f32[768]{0:T(1024)S(1)}, f32[768]{0:T(1024)S(1)}, u32[]{:S(2)}, u32[]{:S(2)}) collective-permute-start(f32[768]{0:T(1024)S(1)} %copy-done.99), channel_id=1, source_target_pairs={{0,1},{1,0},{2,3},{3,2},{4,5},{5,4},{6,7},{7,6},{8,9},{9,8},{10,11... | collective-permute-start | bytes 9224 | tf_op jit(solution)/shard_map/ppermute | solution.py:509
  209.4 10.4 %collective-permute-start.21 = (bf16[192,1536]{1,0:T(8,128)(2,1)S(1)}, bf16[192,1536]{1,0:T(8,128)(2,1)S(1)}, u32[]{:S(2)}, u32[]{:S(2)}) collective-permute-start(bf16[192,1536]{1,0:T(8,128)(2,1)S(1)} %slice.215), channel_id=1, source_target_pairs={{0,4},{2,10},{4,0},{6,14},{8,12},{10,2},{12,8},{14,6},{16,20},{18,... | collective-permute-start | bytes 1769480 | tf_op jit(solution)/shard_map/ppermute | solution.py:533
  210.6 81.9 %collective-permute-start.10 = (f32[768]{0:T(1024)S(1)}, f32[768]{0:T(1024)S(1)}, u32[]{:S(2)}, u32[]{:S(2)}) collective-permute-start(f32[768]{0:T(1024)S(1)} %collective-permute-done.7), channel_id=1, source_target_pairs={{0,2},{2,0},{4,6},{6,4},{8,10},{10,8},{12,14},{14,12},{16,18},{18,... | collective-permute-start | bytes 9224 | tf_op jit(solution)/shard_map/ppermute | solution.py:509
  210.6 81.9 %collective-permute-start.11 = (bf16[768,768]{1,0:T(8,128)(2,1)}, bf16[768,768]{1,0:T(8,128)(2,1)}, u32[]{:S(2)}, u32[]{:S(2)}) collective-permute-start(bf16[768,768]{1,0:T(8,128)(2,1)} %collective-permute-done.8), channel_id=1, source_target_pairs={{0,2},{2,0},{4,6},{6,4},{8,10},{10,8},{12,14},{14,12},{16,18},{18,... | collective-permute-start | bytes 3538952 | tf_op jit(solution)/shard_map/ppermute | solution.py:509
  213.5 79.0 %collective-permute-start.9 = (bf16[768,768]{1,0:T(8,128)(2,1)}, bf16[768,768]{1,0:T(8,128)(2,1)}, u32[]{:S(2)}, u32[]{:S(2)}) collective-permute-start(bf16[768,768]{1,0:T(8,128)(2,1)} %collective-permute-done.6), channel_id=1, source_target_pairs={{0,2},{2,0},{4,6},{6,4},{8,10},{10,8},{12,14},{14,12},{16,18},{18,... | collective-permute-start | bytes 3538952 | tf_op jit(solution)/shard_map/ppermute | solution.py:509
  213.7 17.6 %copy-start.60 = (bf16[14,128,768]{2,1,0:T(8,128)(2,1)S(1)}, bf16[14,128,768]{2,1,0:T(8,128)(2,1)}, u32[]{:S(2)}) copy-start(bf16[14,128,768]{2,1,0:T(8,128)(2,1)} %get-tuple-element.50) | copy-start | bytes 8257540
  219.8 6.7 %collective-permute-start.26 = (bf16[96,1536]{1,0:T(8,128)(2,1)S(1)}, bf16[96,1536]{1,0:T(8,128)(2,1)S(1)}, u32[]{:S(2)}, u32[]{:S(2)}) collective-permute-start(bf16[96,1536]{1,0:T(8,128)(2,1)S(1)} %slice.225), channel_id=1, source_target_pairs={{0,8},{2,6},{4,12},{6,2},{8,0},{10,14},{12,4},{14,10},{16,24},{18,... | collective-permute-start | bytes 884744 | tf_op jit(solution)/shard_map/ppermute | solution.py:533
  226.5 11.8 %collective-permute-start.22 = (bf16[96,1536]{1,0:T(8,128)(2,1)S(1)}, bf16[96,1536]{1,0:T(8,128)(2,1)S(1)}, u32[]{:S(2)}, u32[]{:S(2)}) collective-permute-start(bf16[96,1536]{1,0:T(8,128)(2,1)S(1)} %slice.217), channel_id=1, source_target_pairs={{0,8},{2,6},{4,12},{6,2},{8,0},{10,14},{12,4},{14,10},{16,24},{18,... | collective-permute-start | bytes 884744 | tf_op jit(solution)/shard_map/ppermute | solution.py:533
  228.2 10.2 %collective-permute-start.27 = (bf16[48,1536]{1,0:T(8,128)(2,1)S(1)}, bf16[48,1536]{1,0:T(8,128)(2,1)S(1)}, u32[]{:S(2)}, u32[]{:S(2)}) collective-permute-start(bf16[48,1536]{1,0:T(8,128)(2,1)S(1)} %slice.227), channel_id=1, source_target_pairs={{0,16},{2,18},{4,20},{6,22},{8,24},{10,26},{12,28},{14,30},{16,0},... | collective-permute-start | bytes 442376 | tf_op jit(solution)/shard_map/ppermute | solution.py:533
  232.0 17.3 %copy-start.9 = (s32[1,512,512]{2,1,0:T(8,128)S(1)}, s32[1,512,512]{2,1,0:T(8,128)}, u32[]{:S(2)}) copy-start(s32[1,512,512]{2,1,0:T(8,128)} %param.34) | copy-start | bytes 3145732
  232.2 17.2 %copy-start.4 = (bf16[512,768]{1,0:T(8,128)(2,1)S(1)}, bf16[512,768]{1,0:T(8,128)(2,1)}, u32[]{:S(2)}) copy-start(bf16[512,768]{1,0:T(8,128)(2,1)} %copy-done.2) | copy-start | bytes 2359300
  232.2 17.2 %copy-start.7 = (bf16[512,768]{1,0:T(8,128)(2,1)S(1)}, bf16[512,768]{1,0:T(8,128)(2,1)}, u32[]{:S(2)}) copy-start(bf16[512,768]{1,0:T(8,128)(2,1)} %copy-done.5) | copy-start | bytes 2359300
  232.2 17.2 %copy-start.11 = (bf16[512,768]{1,0:T(8,128)(2,1)S(1)}, bf16[512,768]{1,0:T(8,128)(2,1)}, u32[]{:S(2)}) copy-start(bf16[512,768]{1,0:T(8,128)(2,1)} %copy-done.10) | copy-start | bytes 2359300
  238.4 24.6 %collective-permute-start.5 = (bf16[14,64,768]{2,1,0:T(8,128)(2,1)S(1)}, bf16[14,64,768]{2,1,0:T(8,128)(2,1)S(1)}, u32[]{:S(2)}, u32[]{:S(2)}) collective-permute-start(bf16[14,64,768]{2,1,0:T(8,128)(2,1)S(1)} %slice.200), channel_id=1, source_target_pairs={{0,4},{1,5},{2,10},{3,11},{4,0},{5,1},{6,14},{7,15},{8,12},{9,13},... | collective-permute-start | bytes 4128776 | tf_op jit(solution)/shard_map/ppermute | solution.py:533
  238.5 10.2 %collective-permute-start.23 = (bf16[48,1536]{1,0:T(8,128)(2,1)S(1)}, bf16[48,1536]{1,0:T(8,128)(2,1)S(1)}, u32[]{:S(2)}, u32[]{:S(2)}) collective-permute-start(bf16[48,1536]{1,0:T(8,128)(2,1)S(1)} %slice.219), channel_id=1, source_target_pairs={{0,16},{2,18},{4,20},{6,22},{8,24},{10,26},{12,28},{14,30},{16,0},... | collective-permute-start | bytes 442376 | tf_op jit(solution)/shard_map/ppermute | solution.py:533
  249.4 12.9 %copy-start.44 = (bf16[768,768]{1,0:T(8,128)(2,1)S(1)}, bf16[768,768]{1,0:T(8,128)(2,1)}, u32[]{:S(2)}) copy-start(bf16[768,768]{1,0:T(8,128)(2,1)} %param.40) | copy-start | bytes 3538948
  264.6 14.6 %copy-start.82 = (f32[768]{0:T(1024)S(1)}, f32[768]{0:T(1024)}, u32[]{:S(2)}) copy-start(f32[768]{0:T(1024)} %param.44) | copy-start | bytes 9220
  264.6 34.2 %collective-permute-start.12 = (bf16[14,32,768]{2,1,0:T(8,128)(2,1)}, bf16[14,32,768]{2,1,0:T(8,128)(2,1)S(1)}, u32[]{:S(2)}, u32[]{:S(2)}) collective-permute-start(bf16[14,32,768]{2,1,0:T(8,128)(2,1)} %slice.202), channel_id=1, source_target_pairs={{0,1},{1,0},{2,6},{3,7},{4,5},{5,4},{6,2},{7,3},{8,9},{9,8},{10,14... | collective-permute-start | bytes 2064392 | tf_op jit(solution)/shard_map/ppermute | solution.py:533
  300.3 10.9 %copy-start.94 = (f32[768]{0:T(1024)S(1)}, f32[768]{0:T(1024)}, u32[]{:S(2)}) copy-start(f32[768]{0:T(1024)} %param.53) | copy-start | bytes 9220
  300.3 8.3 %collective-permute-start.13 = (bf16[14,16,768]{2,1,0:T(8,128)(2,1)S(1)}, bf16[14,16,768]{2,1,0:T(8,128)(2,1)S(1)}, u32[]{:S(2)}, u32[]{:S(2)}) collective-permute-start(bf16[14,16,768]{2,1,0:T(8,128)(2,1)S(1)} %slice.204), channel_id=1, source_target_pairs={{0,8},{1,9},{2,3},{3,2},{4,12},{5,13},{6,7},{7,6},{8,0},{9,1},{10,... | collective-permute-start | bytes 1032200 | tf_op jit(solution)/shard_map/ppermute | solution.py:533
  308.6 11.4 %collective-permute-start.14 = (bf16[14,8,768]{2,1,0:T(8,128)(2,1)S(1)}, bf16[14,8,768]{2,1,0:T(8,128)(2,1)S(1)}, u32[]{:S(2)}, u32[]{:S(2)}) collective-permute-start(bf16[14,8,768]{2,1,0:T(8,128)(2,1)S(1)} %slice.206), channel_id=1, source_target_pairs={{0,16},{1,17},{2,18},{3,19},{4,20},{5,21},{6,22},{7,23},{8,24},{9,... | collective-permute-start | bytes 516104 | tf_op jit(solution)/shard_map/ppermute | solution.py:533
  (77 other events, 215.6 us)
